TPU v7x, 32 devices: a whole 2x2x4 slice. The times are simulated.
32 devices in a mesh: shard: 8 (over z, x), head: 2 (over core), tensor: 2 (over y).
Axes of the slice: x: 2, y: 2, z: 4, core: 2. Of those that a mesh axis runs over, the one named last changes fastest.
Arguments:
- tokens: bfloat16 [64, 320, 1024], P('shard'), may hold values from -6 to 6
- kept_counts: int32 [64], P('shard'), may hold values from 200 to 256
- cotangent: bfloat16 [64, 320, 1024], P(('shard', 'head')), may hold values from -6 to 6
- w_qkv: bfloat16 [3, 1024, 1024], P(None, 'shard', 'head'), may hold values from -0.1875 to 0.1875
- w_out: bfloat16 [1024, 1024], P('head', 'shard'), may hold values from -1.5 to 1.5
- w_up: bfloat16 [1024, 4096], P('shard', 'tensor'), may hold values from -0.1875 to 0.1875
- w_down: bfloat16 [4096, 1024], P('tensor', 'shard'), may hold values from -0.09375 to 0.09375
- ln1_gain: float32 [1024], replicated, may hold values from 0.5 to 1.5
- ln1_bias: float32 [1024], replicated, may hold values from -1.5 to 1.5
- ln2_gain: float32 [1024], replicated, may hold values from 0.5 to 1.5
- ln2_bias: float32 [1024], replicated, may hold values from -1.5 to 1.5
- out_bias: float32 [1024], replicated, may hold values from -1.5 to 1.5
- up_bias: float32 [4096], replicated, may hold values from -2.5 to 2.5
- down_bias: float32 [1024], replicated, may hold values from -1.5 to 1.5
- attn_owner: int32 [2, 512, 1], P('head'), may hold values from 0 to 15; in each aligned block of 512 rows (0 to 511, 512 to 1023, ..., all dimensions but the last counted through in order) at most 33 rows name the same one
- mlp_owner: int32 [2, 1024, 1], P('tensor'), may hold values from 0 to 15; in each aligned block of 1024 rows (0 to 1023, 1024 to 2047, ..., all dimensions but the last counted through in order) at most 65 rows name the same one
- attn_left: float32 [2, 528, 64, 64], P('head', ('shard', 'tensor')), may hold values from -0.75 to 0.75
- attn_right: float32 [2, 528, 64, 64], P('head', ('shard', 'tensor')), may hold values from -0.75 to 0.75
- attn_first: float32 [2, 528, 64, 64], P('head', ('shard', 'tensor')), may hold values from -16 to 16
- attn_second: float32 [2, 528, 64, 64], P('head', ('shard', 'tensor')), may hold values from 40.96 to 614.4
- attn_master: float32 [2, 528, 64, 64], P('head', ('shard', 'tensor')), may hold values from -0.1875 to 0.1875
- mlp_left: float32 [2, 1040, 64, 64], P('tensor', ('shard', 'head')), may hold values from -0.75 to 0.75
- mlp_right: float32 [2, 1040, 64, 64], P('tensor', ('shard', 'head')), may hold values from -0.75 to 0.75
- mlp_first: float32 [2, 1040, 64, 64], P('tensor', ('shard', 'head')), may hold values from -16 to 16
- mlp_second: float32 [2, 1040, 64, 64], P('tensor', ('shard', 'head')), may hold values from 40.96 to 614.4
- mlp_master: float32 [2, 1040, 64, 64], P('tensor', ('shard', 'head')), may hold values from -0.1875 to 0.1875
Outputs:
- out: bfloat16 [64, 320, 1024], P(('shard', 'head', 'tensor'))
- tokens_grad: float32 [64, 320, 1024], P(('shard', 'head', 'tensor'))
- ln1_gain_grad: float32 [1024], replicated
- ln1_bias_grad: float32 [1024], replicated
- ln2_gain_grad: float32 [1024], replicated
- ln2_bias_grad: float32 [1024], replicated
- out_bias_grad: float32 [1024], replicated
- down_bias_grad: float32 [1024], replicated
- up_bias_grad: float32 [4096], replicated
- attn_grad: float32 [2, 528, 64, 64], P('head', ('shard', 'tensor'))
- attn_first_new: float32 [2, 528, 64, 64], P('head', ('shard', 'tensor'))
- attn_second_new: float32 [2, 528, 64, 64], P('head', ('shard', 'tensor'))
- attn_master_new: float32 [2, 528, 64, 64], P('head', ('shard', 'tensor'))
- mlp_grad: float32 [2, 1040, 64, 64], P('tensor', ('shard', 'head'))
- mlp_first_new: float32 [2, 1040, 64, 64], P('tensor', ('shard', 'head'))
- mlp_second_new: float32 [2, 1040, 64, 64], P('tensor', ('shard', 'head'))
- mlp_master_new: float32 [2, 1040, 64, 64], P('tensor', ('shard', 'head'))
- w_qkv_new: bfloat16 [3, 1024, 1024], P(None, 'shard', 'head')
- w_out_new: bfloat16 [1024, 1024], P('head', 'shard')
- w_up_new: bfloat16 [1024, 4096], P('shard', 'tensor')
- w_down_new: bfloat16 [4096, 1024], P('tensor', 'shard')
Inputs may be any that keep to these rules, and one draw needn't show every extreme that they name: `attn_owner`: the owner of each block, an index along shard and tensor; no owner holds more than 33 blocks of one head group, and some owner holds exactly 33. `mlp_owner`: the owner of each block, an index along shard and head; no owner holds more than 65 blocks of one hidden-unit group, and some owner holds exactly 65.
All inputs are finite; a program needn't handle non-finite values.
Results may differ from a plain program's by a relative error of at most 0.015.
Values may be sent and summed in bfloat16 or wider, within the bound.
No kernel may reach another device: no remote copies, remote signals or barrier semaphores. Data moves between devices by JAX's collectives and lax.ppermute only.
A program may use at most 256 MiB of HBM per device.

v0:
```python
from functools import partial

import jax
import jax.numpy as jnp
from jax import lax
from jax.sharding import PartitionSpec as P

HD = 64
FF = 4096
BUF = 64


precise = lax.Precision.HIGHEST


def norm_parts(value):
    center = value - jnp.mean(value, axis=-1, keepdims=True)
    inv_root = lax.rsqrt(jnp.mean(center * center, axis=-1, keepdims=True) + 1e-06)
    return (center * inv_root, inv_root)


def norm_back(grad_out, normed, inv_root, gain_vec):
    grad_normed = grad_out * gain_vec
    first_mean = jnp.mean(grad_normed, axis=-1, keepdims=True)
    second_mean = jnp.mean(grad_normed * normed, axis=-1, keepdims=True)
    grad_in = inv_root * (grad_normed - first_mean - normed * second_mean)
    return (grad_in, jnp.sum(grad_out * normed, axis=(0, 1)), jnp.sum(grad_out, axis=(0, 1)))


def split_blocks(matrix, block_size):
    leading = matrix.shape[:-2]
    row_count, col_count = (matrix.shape[-2], matrix.shape[-1])
    shaped = matrix.reshape(
        leading + (row_count // block_size, block_size, col_count // block_size, block_size)
    )
    depth = len(leading)
    axes_order = tuple(range(depth)) + (depth, depth + 2, depth + 1, depth + 3)
    return shaped.transpose(axes_order).reshape(-1, block_size, block_size)


def join_blocks(blocks_in, leading, row_count, col_count, block_size):
    shaped = blocks_in.reshape(
        leading + (row_count // block_size, col_count // block_size, block_size, block_size)
    )
    depth = len(leading)
    axes_order = tuple(range(depth)) + (depth, depth + 2, depth + 1, depth + 3)
    return shaped.transpose(axes_order).reshape(leading + (row_count, col_count))


def slot_numbers(owner_list, capacity, owners):
    onehot = (owner_list[:, None] == jnp.arange(owners, dtype=jnp.int32)[None, :]).astype(jnp.int32)
    earlier = jnp.cumsum(onehot, axis=0) - onehot
    return owner_list * capacity + jnp.sum(earlier * onehot, axis=1)


def slot_index(slot_ids, total):
    matches = slot_ids[None, :] == jnp.arange(total, dtype=jnp.int32)[:, None]
    filled = jnp.any(matches, axis=1)
    picked = jnp.sum(
        jnp.where(matches, jnp.arange(slot_ids.shape[0], dtype=jnp.int32)[None, :], 0), axis=1
    )
    return (picked, filled.astype(jnp.float32))


def soap_update(gradient, left_basis, right_basis, first_moment, second, master):
    turned = jnp.einsum("sji,sjk->sik", left_basis, gradient, precision=precise)
    turned = jnp.einsum("sik,skl->sil", turned, right_basis, precision=precise)
    first_new = 0.95 * first_moment + 0.05 * turned
    second_new = 0.95 * second + 0.05 * turned * turned
    direction = first_new / (jnp.sqrt(second_new) + 1e-08)
    rotated_back = jnp.einsum("sij,sjk->sik", left_basis, direction, precision=precise)
    rotated_back = jnp.einsum("sik,slk->sil", rotated_back, right_basis, precision=precise)
    return (first_new, second_new, master - 0.05 * rotated_back)


def per_device(
    tokens,
    kept_counts,
    cotangent,
    w_qkv,
    w_out,
    w_up,
    w_down,
    ln1_gain,
    ln1_bias,
    ln2_gain,
    ln2_bias,
    out_bias,
    up_bias,
    down_bias,
    attn_owner,
    mlp_owner,
    attn_left,
    attn_right,
    attn_first,
    attn_second,
    attn_master,
    mlp_left,
    mlp_right,
    mlp_first,
    mlp_second,
    mlp_master,
):
    head_count = lax.axis_size("head")
    tensor_count = lax.axis_size("tensor")
    head_pos = lax.axis_index("head")
    tensor_pos = lax.axis_index("tensor")
    shard_pos = lax.axis_index("shard")
    local_images, slot_count, features = tokens.shape
    per_out = local_images // (head_count * tensor_count)
    block_size = attn_left.shape[-1]
    qkv_full, out_full, up_full, down_full = (
        lax.all_gather(w_qkv, "shard", axis=1, tiled=True),
        lax.all_gather(w_out, "shard", axis=1, tiled=True),
        lax.all_gather(w_up, "shard", axis=0, tiled=True),
        lax.all_gather(w_down, "shard", axis=1, tiled=True),
    )
    group_cols = qkv_full.shape[2]
    hidden_cols = up_full.shape[1]
    head_groups = group_cols // HD
    image_grid = tokens.reshape(head_count, tensor_count, per_out, slot_count, features)
    kept_grid = kept_counts.reshape(head_count, tensor_count, per_out)
    attn_tokens = lax.dynamic_index_in_dim(image_grid, tensor_pos, 1, keepdims=False)
    attn_tokens = attn_tokens.reshape(head_count * per_out, slot_count, features)
    attn_kept = lax.dynamic_index_in_dim(kept_grid, tensor_pos, 1, keepdims=False).reshape(-1)
    own_row = lax.dynamic_index_in_dim(image_grid, head_pos, 0, keepdims=False)
    own_tokens = lax.dynamic_index_in_dim(own_row, tensor_pos, 0, keepdims=False).astype(
        jnp.float32
    )
    own_kept = lax.dynamic_index_in_dim(
        lax.dynamic_index_in_dim(kept_grid, head_pos, 0, keepdims=False),
        tensor_pos,
        0,
        keepdims=False,
    )
    mlp_kept = lax.dynamic_index_in_dim(kept_grid, head_pos, 0, keepdims=False).reshape(-1)
    positions = jnp.arange(slot_count, dtype=jnp.int32)
    key_valid = positions[None, :] < (BUF + attn_kept)[:, None]
    own_valid = (positions[None, :] < (BUF + own_kept)[:, None]).astype(jnp.float32)[:, :, None]
    mlp_valid = (positions[None, :] < (BUF + mlp_kept)[:, None]).astype(jnp.bfloat16)[:, :, None]
    normed_one, inv_one = norm_parts(attn_tokens.astype(jnp.float32))
    low_one = (normed_one * ln1_gain + ln1_bias).astype(jnp.bfloat16)
    projected = jnp.einsum(
        "nsd,cde->cnse", low_one, qkv_full, preferred_element_type=jnp.float32
    ).astype(jnp.bfloat16)
    rows_count = projected.shape[1]
    queries = projected[0].reshape(rows_count, slot_count, head_groups, HD)
    key_rows = projected[1].reshape(rows_count, slot_count, head_groups, HD)
    value_rows = projected[2].reshape(rows_count, slot_count, head_groups, HD)

    def scores_of():
        raw_scores = (
            jnp.einsum("nqhe,nkhe->nhqk", queries, key_rows, preferred_element_type=jnp.float32)
            * 0.125
        )
        return jnp.where(key_valid[:, None, None, :], raw_scores, -1000000000.0)

    scores = scores_of()
    row_max = jnp.max(scores, axis=-1, keepdims=True)
    log_total = row_max + jnp.log(jnp.sum(jnp.exp(scores - row_max), axis=-1, keepdims=True))
    attn_probs = jnp.exp(scores - log_total).astype(jnp.bfloat16)
    heads_out = jnp.einsum(
        "nhqk,nkhe->nqhe", attn_probs, value_rows, preferred_element_type=jnp.float32
    )
    heads_out = heads_out.astype(jnp.bfloat16).reshape(rows_count, slot_count, group_cols)
    partial_branch = jnp.einsum(
        "nse,ed->nsd", heads_out, out_full, preferred_element_type=jnp.float32
    )
    partial_branch = partial_branch.reshape(head_count, per_out, slot_count, features)
    branch = (
        lax.psum_scatter(
            partial_branch.astype(jnp.bfloat16), "head", scatter_dimension=0, tiled=True
        ).astype(jnp.float32)[0]
        + out_bias
    )
    residual = own_tokens + branch
    normed_two, inv_two = norm_parts(residual)
    low_two = (normed_two * ln2_gain + ln2_bias).astype(jnp.bfloat16)
    normed_rows = lax.all_gather(low_two, "tensor", axis=0, tiled=True)
    up_local = lax.dynamic_slice_in_dim(up_bias, tensor_pos * hidden_cols, hidden_cols, 0)
    pre_act = (
        jnp.einsum("nsd,df->nsf", normed_rows, up_full, preferred_element_type=jnp.float32)
        + up_local
    )
    hidden_full, gelu_back = jax.vjp(partial(jax.nn.gelu, approximate=False), pre_act)
    hidden = hidden_full.astype(jnp.bfloat16)
    partial_mlp = jnp.einsum("nsf,fd->nsd", hidden, down_full, preferred_element_type=jnp.float32)
    partial_mlp = partial_mlp.reshape(tensor_count, per_out, slot_count, features)
    mlp_out = (
        lax.psum_scatter(
            partial_mlp.astype(jnp.bfloat16), "tensor", scatter_dimension=0, tiled=True
        ).astype(jnp.float32)[0]
        + down_bias
    )
    out = (own_valid * (residual + mlp_out)).astype(jnp.bfloat16)
    grad_mlp_rows = cotangent * mlp_valid
    grad_hidden = jnp.einsum(
        "nsd,fd->nsf", grad_mlp_rows, down_full, preferred_element_type=jnp.float32
    )
    grad_pre = gelu_back(grad_hidden)[0].astype(jnp.bfloat16)
    down_grad = jnp.einsum("nsf,nsd->fd", hidden, grad_mlp_rows, preferred_element_type=jnp.float32)
    up_grad = jnp.einsum("nsd,nsf->df", normed_rows, grad_pre, preferred_element_type=jnp.float32)
    up_bias_part = jnp.sum(grad_pre.astype(jnp.float32), axis=(0, 1))
    partial_normed = jnp.einsum(
        "nsf,df->nsd", grad_pre, up_full, preferred_element_type=jnp.float32
    )
    partial_normed = partial_normed.reshape(tensor_count, per_out, slot_count, features)
    grad_normed_two = lax.psum_scatter(
        partial_normed.astype(jnp.bfloat16), "tensor", scatter_dimension=0, tiled=True
    ).astype(jnp.float32)[0]
    resid_from, ln2_gain_part, ln2_bias_part = norm_back(
        grad_normed_two, normed_two, inv_two, ln2_gain
    )
    own_cot = (
        lax.dynamic_index_in_dim(
            cotangent.reshape(tensor_count, per_out, slot_count, features),
            tensor_pos,
            0,
            keepdims=False,
        ).astype(jnp.float32)
        * own_valid
    )
    down_bias_part = jnp.sum(own_cot, axis=(0, 1))
    grad_resid = own_cot + resid_from
    grad_branch = grad_resid.astype(jnp.bfloat16)
    out_bias_part = jnp.sum(grad_branch.astype(jnp.float32), axis=(0, 1))
    branch_rows = lax.all_gather(grad_branch, "head", axis=0, tiled=True)
    out_grad = jnp.einsum("nse,nsd->ed", heads_out, branch_rows, preferred_element_type=jnp.float32)
    grad_heads = jnp.einsum(
        "nsd,ed->nse", branch_rows, out_full, preferred_element_type=jnp.float32
    )
    grad_heads = grad_heads.astype(jnp.bfloat16).reshape(rows_count, slot_count, head_groups, HD)
    probs_again = jnp.exp(scores_of() - log_total)
    grad_probs = jnp.einsum(
        "nqhe,nkhe->nhqk", grad_heads, value_rows, preferred_element_type=jnp.float32
    )
    grad_scores = probs_again * (
        grad_probs - jnp.sum(probs_again * grad_probs, axis=-1, keepdims=True)
    )
    grad_scores = grad_scores.astype(jnp.bfloat16)
    grad_query = (
        jnp.einsum("nhqk,nkhe->nqhe", grad_scores, key_rows, preferred_element_type=jnp.float32)
        * 0.125
    ).astype(jnp.bfloat16)
    grad_keys = (
        jnp.einsum("nhqk,nqhe->nkhe", grad_scores, queries, preferred_element_type=jnp.float32)
        * 0.125
    ).astype(jnp.bfloat16)
    grad_values = jnp.einsum(
        "nhqk,nqhe->nkhe",
        probs_again.astype(jnp.bfloat16),
        grad_heads,
        preferred_element_type=jnp.float32,
    ).astype(jnp.bfloat16)
    grad_proj = jnp.stack([grad_query, grad_keys, grad_values]).reshape(
        3, rows_count, slot_count, group_cols
    )
    qkv_grad = jnp.einsum("nsd,cnse->cde", low_one, grad_proj, preferred_element_type=jnp.float32)
    partial_input = jnp.einsum(
        "cnse,cde->nsd", grad_proj, qkv_full, preferred_element_type=jnp.float32
    )
    partial_input = partial_input.reshape(head_count, per_out, slot_count, features)
    grad_normed_one = lax.psum_scatter(
        partial_input.astype(jnp.bfloat16), "head", scatter_dimension=0, tiled=True
    ).astype(jnp.float32)[0]
    own_normed = lax.dynamic_index_in_dim(
        normed_one.reshape(head_count, per_out, slot_count, features), head_pos, 0, keepdims=False
    )
    own_inv = lax.dynamic_index_in_dim(
        inv_one.reshape(head_count, per_out, slot_count, 1), head_pos, 0, keepdims=False
    )
    tokens_from, ln1_gain_part, ln1_bias_part = norm_back(
        grad_normed_one, own_normed, own_inv, ln1_gain
    )
    tokens_grad = grad_resid + tokens_from
    up_whole = lax.dynamic_update_slice_in_dim(
        jnp.zeros((FF,), jnp.float32), up_bias_part, tensor_pos * hidden_cols, 0
    )
    small_sums = lax.psum(
        (
            ln1_gain_part,
            ln1_bias_part,
            ln2_gain_part,
            ln2_bias_part,
            out_bias_part,
            down_bias_part,
            up_whole,
        ),
        ("shard", "head", "tensor"),
    )
    attn_blocks = jnp.concatenate(
        [split_blocks(qkv_grad, block_size), split_blocks(out_grad, block_size)], axis=0
    )
    attn_owners = lax.axis_size(("shard", "tensor"))
    attn_cap = attn_master.shape[1]
    attn_slots = slot_numbers(attn_owner[0, :, 0], attn_cap, attn_owners)
    attn_picked, attn_filled = slot_index(attn_slots, attn_owners * attn_cap)
    attn_parcel = jnp.take(attn_blocks, attn_picked, axis=0) * attn_filled[:, None, None]
    attn_sum = lax.psum_scatter(attn_parcel, ("shard", "tensor"), scatter_dimension=0, tiled=True)
    attn_first_new, attn_second_new, attn_master_new = soap_update(
        attn_sum, attn_left[0], attn_right[0], attn_first[0], attn_second[0], attn_master[0]
    )
    attn_all = lax.all_gather(
        attn_master_new.astype(jnp.bfloat16), ("shard", "tensor"), axis=0, tiled=True
    )
    attn_new = jnp.take(attn_all, attn_slots, axis=0)
    qkv_count = 3 * (features // block_size) * (group_cols // block_size)
    new_qkv = join_blocks(attn_new[:qkv_count], (3,), features, group_cols, block_size)
    new_out = join_blocks(attn_new[qkv_count:], (), group_cols, features, block_size)
    w_qkv_new = lax.dynamic_slice_in_dim(new_qkv, shard_pos * w_qkv.shape[1], w_qkv.shape[1], 1)
    w_out_new = lax.dynamic_slice_in_dim(new_out, shard_pos * w_out.shape[1], w_out.shape[1], 1)
    mlp_blocks = jnp.concatenate(
        [split_blocks(up_grad, block_size), split_blocks(down_grad, block_size)], axis=0
    )
    mlp_owners = lax.axis_size(("shard", "head"))
    mlp_cap = mlp_master.shape[1]
    mlp_slots = slot_numbers(mlp_owner[0, :, 0], mlp_cap, mlp_owners)
    mlp_picked, mlp_filled = slot_index(mlp_slots, mlp_owners * mlp_cap)
    mlp_parcel = jnp.take(mlp_blocks, mlp_picked, axis=0) * mlp_filled[:, None, None]
    mlp_sum = lax.psum_scatter(mlp_parcel, ("shard", "head"), scatter_dimension=0, tiled=True)
    mlp_first_new, mlp_second_new, mlp_master_new = soap_update(
        mlp_sum, mlp_left[0], mlp_right[0], mlp_first[0], mlp_second[0], mlp_master[0]
    )
    mlp_all = lax.all_gather(
        mlp_master_new.astype(jnp.bfloat16), ("shard", "head"), axis=0, tiled=True
    )
    mlp_new = jnp.take(mlp_all, mlp_slots, axis=0)
    up_count = features // block_size * (hidden_cols // block_size)
    new_up = join_blocks(mlp_new[:up_count], (), features, hidden_cols, block_size)
    new_down = join_blocks(mlp_new[up_count:], (), hidden_cols, features, block_size)
    w_up_new = lax.dynamic_slice_in_dim(new_up, shard_pos * w_up.shape[0], w_up.shape[0], 0)
    w_down_new = lax.dynamic_slice_in_dim(new_down, shard_pos * w_down.shape[1], w_down.shape[1], 1)
    return (
        out,
        tokens_grad,
        small_sums[0],
        small_sums[1],
        small_sums[2],
        small_sums[3],
        small_sums[4],
        small_sums[5],
        small_sums[6],
        attn_sum[None],
        attn_first_new[None],
        attn_second_new[None],
        attn_master_new[None],
        mlp_sum[None],
        mlp_first_new[None],
        mlp_second_new[None],
        mlp_master_new[None],
        w_qkv_new,
        w_out_new,
        w_up_new,
        w_down_new,
    )


def solution(mesh):
    placed = (
        P("shard", None, None),
        P("shard"),
        P(("shard", "head"), None, None),
        P(None, "shard", "head"),
        P("head", "shard"),
        P("shard", "tensor"),
        P("tensor", "shard"),
        P(),
        P(),
        P(),
        P(),
        P(),
        P(),
        P(),
        P("head", None, None),
        P("tensor", None, None),
        P("head", ("shard", "tensor"), None, None),
        P("head", ("shard", "tensor"), None, None),
        P("head", ("shard", "tensor"), None, None),
        P("head", ("shard", "tensor"), None, None),
        P("head", ("shard", "tensor"), None, None),
        P("tensor", ("shard", "head"), None, None),
        P("tensor", ("shard", "head"), None, None),
        P("tensor", ("shard", "head"), None, None),
        P("tensor", ("shard", "head"), None, None),
        P("tensor", ("shard", "head"), None, None),
    )
    return jax.shard_map(
        per_device,
        mesh=mesh,
        in_specs=placed,
        out_specs=(
            P(("shard", "head", "tensor"), None, None),
            P(("shard", "head", "tensor"), None, None),
            P(),
            P(),
            P(),
            P(),
            P(),
            P(),
            P(),
            P("head", ("shard", "tensor"), None, None),
            P("head", ("shard", "tensor"), None, None),
            P("head", ("shard", "tensor"), None, None),
            P("head", ("shard", "tensor"), None, None),
            P("tensor", ("shard", "head"), None, None),
            P("tensor", ("shard", "head"), None, None),
            P("tensor", ("shard", "head"), None, None),
            P("tensor", ("shard", "head"), None, None),
            P(None, "shard", "head"),
            P("head", "shard"),
            P("shard", "tensor"),
            P("tensor", "shard"),
        ),
        check_vma=False,
    )
```

profile of v0, /device:TPU:0, one launch (start us, length us, event | category | flops | bytes accessed | tf_op | source)
XLA Modules:
  0.0 1528.7 jit_solution(17770768528289046282)
XLA Ops:
  17.4 55.6 %all-gather.9.cloned.1.call-done = bf16[3,1024,512]{2,1,0:T(8,128)(2,1)} async-done(((bf16[3,128,512]{2,1,0:T(8,128)(2,1)}), bf16[3,1024,512]{2,1,0:T(8,128)(2,1)}) %all-gather.9.cloned.1.call-update) | async-done | bytes 3145744 | tf_op jit(solution)/shard_map/all_gather | solution.py:113
  135.9 67.7 %all-gather.15.cloned.1.call-done = bf16[1024,2048]{1,0:T(8,128)(2,1)} async-done(((bf16[128,2048]{1,0:T(8,128)(2,1)}), bf16[1024,2048]{1,0:T(8,128)(2,1)}) %all-gather.15.cloned.1.call-update) | async-done | bytes 4194320 | tf_op jit(solution)/shard_map/all_gather | solution.py:115
  203.6 39.5 %all-gather.13.cloned.1.call-done = bf16[4,320,1024]{2,1,0:T(8,128)(2,1)} async-done(((bf16[2,320,1024]{2,1,0:T(8,128)(2,1)}), bf16[4,320,1024]{2,1,0:T(8,128)(2,1)}) %all-gather.13.cloned.1.call-update) | async-done | bytes 2621456 | tf_op jit(solution)/shard_map/all_gather | solution.py:179
  243.1 12.1 fusion.57
  259.1 25.2 %multiply_convert_fusion.1 = (bf16[4,320,2048]{2,1,0:T(8,128)(2,1)}, f32[4,320,2048]{2,1,0:T(8,128)}) fusion(f32[4,320,2048]{2,1,0:T(8,128)S(1)} %get-tuple-element.141, f32[2048]{0:T(1024)S(1)} %dynamic_slice.51, u8[320,2048]{1,0:T(8,128)(4,1)S(1)} %get-tuple-element.106, u8[320,2048]{1,0:T(8,128)(4,1)S(1)} %get-tuple-element.105), kind=kLoop, calls=%fused_computation.24 | loop fusion | flops 186122240 | bytes 27533312 | tf_op jit(solution)/shard_map/convert_element_type | solution.py:186
  284.3 35.4 %all-gather.17.cloned.1.call-done = bf16[2048,1024]{1,0:T(8,128)(2,1)} async-done(((bf16[2048,128]{1,0:T(8,128)(2,1)}), bf16[2048,1024]{1,0:T(8,128)(2,1)}) %all-gather.17.cloned.1.call-update) | async-done | bytes 4194320 | tf_op jit(solution)/shard_map/all_gather | solution.py:116
  319.7 17.4 %convert_reduce_fusion = (f32[2048]{0:T(1024)}, bf16[4,320,2048]{2,1,0:T(8,128)(2,1)}) fusion(f32[4,320,2048]{2,1,0:T(8,128)} %get-tuple-element.127, bf16[2048,1024]{1,0:T(8,128)(2,1)} %all-gather.17.cloned.1.call-done, bf16[4,320,1024]{2,1,0:T(8,128)(2,1)} %param.28, bf16[4,320]{1,0:T(4,128)(2,1)S(1)} %fusion.114, f32[4,320,2048]{2,1,0:T(8,128)} %copy-done.9, ...), kind=kOutput, calls=%fused_computation.22 | convolution fusion | flops 5414582272 | bytes 33049088 | tf_op jit(solution)/shard_map/nsd,fd->nsf/dot_general | solution.py:197
  357.1 26.0 %reduce-scatter.11.cloned.1.call-done = bf16[1,2,320,1024]{3,2,1,0:T(8,128)(2,1)} async-done(((bf16[2,2,320,1024]{3,2,1,0:T(8,128)(2,1)}), bf16[1,2,320,1024]{3,2,1,0:T(8,128)(2,1)}) %reduce-scatter.11.cloned.1.call-update) | async-done | bytes 1310736 | tf_op jit(solution)/shard_map/reduce_scatter | solution.py:208
  387.0 36.0 %reduce-scatter.9.cloned.1.call-done = bf16[1,2,320,1024]{3,2,1,0:T(8,128)(2,1)} async-done(((bf16[2,2,320,1024]{3,2,1,0:T(8,128)(2,1)}), bf16[1,2,320,1024]{3,2,1,0:T(8,128)(2,1)}) %reduce-scatter.9.cloned.1.call-update) | async-done | bytes 1310736 | tf_op jit(solution)/shard_map/reduce_scatter | solution.py:190
  455.0 12.3 multiply_reduce_fusion
  518.8 12.8 copy.173
  543.0 35.6 %gather_fusion = f32[528,64,64]{2,1,0:T(8,128)} fusion(f32[512,64,64]{2,1,0:T(8,128)} %pad_maximum_fusion.1, s32[1024]{0:T(1024)S(1)} %pad_clamp_fusion.2), kind=kCustom, calls=%fused_computation | custom fusion | bytes 17303616 | tf_op jit(solution)/shard_map/jit(_take)/gather | solution.py:298
  578.6 12.8 select_multiply_fusion.1
  610.5 13.4 reshape.510
  624.0 16.2 %copy.184 = f32[32,64,16,64]{3,1,2,0:T(8,128)} copy(f32[32,64,16,64]{3,2,1,0:T(8,128)} %reshape.510) | data formatting | bytes 16777216 | tf_op jit(solution)/shard_map/reshape | solution.py:33
  650.6 14.5 reshape.508
  665.0 15.7 %copy.183 = f32[16,64,32,64]{3,1,2,0:T(8,128)S(1)} copy(f32[16,64,32,64]{3,2,1,0:T(8,128)} %reshape.508) | data formatting | bytes 16777216 | tf_op jit(solution)/shard_map/reshape | solution.py:33
  680.7 19.0 %pad_maximum_fusion = f32[1024,64,64]{2,1,0:T(8,128)} fusion(f32[512,64,64]{2,1,0:T(8,128)} %bitcast.407, f32[512,64,64]{2,1,0:T(8,128)S(1)} %bitcast.408), kind=kLoop, calls=%fused_computation.5 | loop fusion | flops 4194304 | bytes 33554432 | tf_op jit(solution)/shard_map/concatenate | solution.py:312
  699.7 46.6 %gather_fusion.1 = f32[1040,64,64]{2,1,0:T(8,128)} fusion(f32[1024,64,64]{2,1,0:T(8,128)} %pad_maximum_fusion, s32[2048]{0:T(1024)S(1)} %pad_clamp_fusion), kind=kCustom, calls=%fused_computation.1 | custom fusion | bytes 34082880 | tf_op jit(solution)/shard_map/jit(_take)/gather | solution.py:319
  746.4 24.2 %select_multiply_fusion = f32[1040,64,64]{2,1,0:T(8,128)} fusion(f32[1040,64,64]{2,1,0:T(8,128)} %gather_fusion.1, f32[1040]{0:T(1024)S(1)} %convert_element_type.211, pred[1040]{0:T(1024)(128)(4,1)S(1)} %compare_and_fusion), kind=kLoop, calls=%fused_computation.4 | loop fusion | flops 8519680 | bytes 34083920 | tf_op jit(solution)/shard_map/mul | solution.py:319
  781.8 77.7 %reduce-scatter.15.cloned.1.call-done = f32[33,64,64]{2,1,0:T(8,128)} async-done(((f32[528,64,64]{2,1,0:T(8,128)}), f32[33,64,64]{2,1,0:T(8,128)}) %reduce-scatter.15.cloned.1.call-update) | async-done | bytes 540688 | tf_op jit(solution)/shard_map/reduce_scatter | solution.py:299
  887.9 311.3 %reduce-scatter.17.cloned.1.call-done = f32[65,64,64]{2,1,0:T(8,128)} async-done(((f32[1040,64,64]{2,1,0:T(8,128)}), f32[65,64,64]{2,1,0:T(8,128)}) %reduce-scatter.17.cloned.1.call-update) | async-done | bytes 1064976 | tf_op jit(solution)/shard_map/reduce_scatter | solution.py:320
  1228.6 41.5 %all-reduce = (f32[1024]{0:T(1024)}, f32[1024]{0:T(1024)}, f32[1024]{0:T(1024)}, f32[1024]{0:T(1024)}, f32[1024]{0:T(1024)}, /*index=5*/f32[1024]{0:T(1024)}, f32[4096]{0:T(1024)}) all-reduce(f32[1024]{0:T(1024)S(1)} %get-tuple-element.109, ...), channel_id=1, replica_groups=mesh['shard'=8,'head'=2,'tensor'=2] {'shard','head','tensor'}, use_global_device_ids=true, to_apply=%region_16.17 | all-reduce | flops 10240 | bytes 81920 | tf_op jit(solution)/shard_map/psum | solution.py:279
  1294.1 36.4 %all-gather.21.cloned.1.call-done = bf16[528,64,64]{2,1,0:T(8,128)(2,1)} async-done(((bf16[33,64,64]{2,1,0:T(8,128)(2,1)}), bf16[528,64,64]{2,1,0:T(8,128)(2,1)}) %all-gather.21.cloned.1.call-update) | async-done | bytes 4325392 | tf_op jit(solution)/shard_map/all_gather | solution.py:303
  1330.5 23.1 %gather_fusion.2 = bf16[512,64,64]{2,1,0:T(8,128)(2,1)} fusion(bf16[528,64,64]{2,1,0:T(8,128)(2,1)} %all-gather.21.cloned.1.call-done, s32[1024]{0:T(1024)S(1)} %pad_clamp_fusion.1), kind=kCustom, calls=%fused_computation.2 | custom fusion | bytes 8390656 | tf_op jit(solution)/shard_map/jit(_take)/gather | solution.py:306
  1362.7 15.3 %copy.196 = bf16[3,16,64,8,64]{4,3,2,1,0:T(8,128)(2,1)} copy(bf16[3,16,64,8,64]{4,2,3,1,0:T(8,128)(2,1)S(1)} %bitcast.423) | data formatting | bytes 6291456 | tf_op jit(solution)/shard_map/transpose | solution.py:47
  1396.1 24.3 %all-gather.23.cloned.1.call-done = bf16[1040,64,64]{2,1,0:T(8,128)(2,1)} async-done(((bf16[65,64,64]{2,1,0:T(8,128)(2,1)}), bf16[1040,64,64]{2,1,0:T(8,128)(2,1)}) %all-gather.23.cloned.1.call-update) | async-done | bytes 8519696 | tf_op jit(solution)/shard_map/all_gather | solution.py:324
  1420.4 19.4 %gather_fusion.3 = bf16[1024,64,64]{2,1,0:T(8,128)(2,1)} fusion(bf16[1040,64,64]{2,1,0:T(8,128)(2,1)} %all-gather.23.cloned.1.call-done, s32[1024]{0:T(1024)S(1)} %broadcast_clamp_fusion), kind=kCustom, calls=%fused_computation.3 | custom fusion | bytes 16781312 | tf_op jit(solution)/shard_map/jit(_take)/gather | solution.py:327
  1456.7 13.6 copy.198
  1470.3 12.6 reshape.517
  1484.8 23.2 %copy.199 = bf16[32,64,16,64]{3,2,1,0:T(8,128)(2,1)} copy(bf16[32,64,16,64]{3,1,2,0:T(8,128)(2,1)} %bitcast.421) | data formatting | bytes 8388608 | tf_op jit(solution)/shard_map/transpose | solution.py:47
  1508.0 11.8 reshape.519
  (315 shorter events, 365.0 us)
Async XLA Ops:
  7.2 855.5 %copy-start = (f32[1,33,64,64]{3,2,1,0:T(8,128)S(1)}, f32[1,33,64,64]{3,2,1,0:T(8,128)}, u32[]{:S(2)}) copy-start(f32[1,33,64,64]{3,2,1,0:T(8,128)} %param.43) | copy-start | bytes 1622020
  7.2 65.8 %all-gather.9.cloned.1.call-start = ((), (), s32[]{:S(2)}) async-start(), calls=%async_computation.6 | async-start | bytes 3538944 | tf_op jit(solution)/shard_map/all_gather | solution.py:113
  7.9 105.2 %all-gather.11.cloned.1.call-start = ((), (), s32[]{:S(2)}) async-start(), calls=%async_computation.7 | async-start | bytes 1179648 | tf_op jit(solution)/shard_map/all_gather | solution.py:114
  8.7 118.8 %reduce-scatter.7.cloned.1.call-start = ((), (), s32[]{:S(2)}) async-start(), calls=%async_computation.8 | async-start | bytes 3932160 | tf_op jit(solution)/shard_map/reduce_scatter | solution.py:171
  117.9 85.7 %all-gather.15.cloned.1.call-start = ((), (), s32[]{:S(2)}) async-start(), calls=%async_computation.10 | async-start | bytes 4718592 | tf_op jit(solution)/shard_map/all_gather | solution.py:115
  118.5 124.7 %all-gather.13.cloned.1.call-start = ((), (), s32[]{:S(2)}) async-start(), calls=%async_computation.9 | async-start | bytes 3932160 | tf_op jit(solution)/shard_map/all_gather | solution.py:179
  129.8 293.2 %copy-start.35 = (f32[2,320]{1,0:T(2,128)}, f32[2,320]{1,0:T(2,128)S(1)}, u32[]{:S(2)}) copy-start(f32[2,320]{1,0:T(2,128)S(1)} %broadcast_multiply_fusion.5) | copy-start | bytes 7684
  131.9 291.1 %copy-start.37 = (f32[2,320]{1,0:T(2,128)}, f32[2,320]{1,0:T(2,128)S(1)}, u32[]{:S(2)}) copy-start(f32[2,320]{1,0:T(2,128)S(1)} %add_rsqrt_fusion.1) | copy-start | bytes 7684
  135.1 184.6 %all-gather.17.cloned.1.call-start = ((), (), s32[]{:S(2)}) async-start(), calls=%async_computation.11 | async-start | bytes 4718592 | tf_op jit(solution)/shard_map/all_gather | solution.py:116
  135.6 247.4 %reduce-scatter.11.cloned.1.call-start = ((), (), s32[]{:S(2)}) async-start(), calls=%async_computation.13 | async-start | bytes 3932160 | tf_op jit(solution)/shard_map/reduce_scatter | solution.py:208
  347.0 76.0 %reduce-scatter.9.cloned.1.call-start = ((), (), s32[]{:S(2)}) async-start(), calls=%async_computation.12 | async-start | bytes 3932160 | tf_op jit(solution)/shard_map/reduce_scatter | solution.py:190
  356.9 66.1 %copy-start.67 = (f32[1024]{0:T(1024)S(1)}, f32[1024]{0:T(1024)}, u32[]{:S(2)}) copy-start(f32[1024]{0:T(1024)} %param.39) | copy-start | bytes 12292
  357.0 83.1 %all-gather.19.cloned.1.call-start = ((), (), s32[]{:S(2)}) async-start(), calls=%async_computation.14 | async-start | bytes 3932160 | tf_op jit(solution)/shard_map/all_gather | solution.py:227
  357.1 71.5 %copy-start.53 = (f32[2,320]{1,0:T(2,128)}, f32[2,320]{1,0:T(2,128)S(1)}, u32[]{:S(2)}) copy-start(f32[2,320]{1,0:T(2,128)S(1)} %compare_convert_fusion) | copy-start | bytes 7684
  387.0 41.6 %copy-start.57 = (f32[2,320]{1,0:T(2,128)}, f32[2,320]{1,0:T(2,128)S(1)}, u32[]{:S(2)}) copy-start(f32[2,320]{1,0:T(2,128)S(1)} %get-tuple-element.151) | copy-start | bytes 7684
  428.6 430.9 %reduce-scatter.15.cloned.1.call-start = ((), (), s32[]{:S(2)}) async-start(), calls=%async_computation.16 | async-start | bytes 18382848 | tf_op jit(solution)/shard_map/reduce_scatter | solution.py:299
  591.4 607.7 %reduce-scatter.17.cloned.1.call-start = ((), (), s32[]{:S(2)}) async-start(), calls=%async_computation.17 | async-start | bytes 36208640 | tf_op jit(solution)/shard_map/reduce_scatter | solution.py:320
  770.6 452.7 %reduce-scatter.13.cloned.1.call-start = ((), (), s32[]{:S(2)}) async-start(), calls=%async_computation.15 | async-start | bytes 3932160 | tf_op jit(solution)/shard_map/reduce_scatter | solution.py:263
  781.7 77.8 %copy-start.28 = (f32[1,33,64,64]{3,2,1,0:T(8,128)S(1)}, f32[1,33,64,64]{3,2,1,0:T(8,128)}, u32[]{:S(2)}) copy-start(f32[1,33,64,64]{3,2,1,0:T(8,128)} %param.42) | copy-start | bytes 1622020
  781.7 82.2 %copy-start.29 = (f32[1,33,64,64]{3,2,1,0:T(8,128)S(1)}, f32[1,33,64,64]{3,2,1,0:T(8,128)}, u32[]{:S(2)}) copy-start(f32[1,33,64,64]{3,2,1,0:T(8,128)} %param.45) | copy-start | bytes 1622020
  781.7 548.8 %all-gather.21.cloned.1.call-start = ((), (), s32[]{:S(2)}) async-start(), calls=%async_computation.18 | async-start | bytes 9191424 | tf_op jit(solution)/shard_map/all_gather | solution.py:303
  868.8 551.6 %all-gather.23.cloned.1.call-start = ((), (), s32[]{:S(2)}) async-start(), calls=%async_computation.19 | async-start | bytes 18104320 | tf_op jit(solution)/shard_map/all_gather | solution.py:324
  1223.2 46.9 %copy-start.3 = (bf16[1,2,320,1024]{3,2,1,0:T(8,128)(2,1)S(1)}, bf16[1,2,320,1024]{3,2,1,0:T(8,128)(2,1)}, u32[]{:S(2)}) copy-start(bf16[1,2,320,1024]{3,2,1,0:T(8,128)(2,1)} %reduce-scatter.7.cloned.1.call-done) | copy-start | bytes 3932164
  1223.3 46.9 %copy-start.34 = (f32[1024]{0:T(1024)S(1)}, f32[1024]{0:T(1024)}, u32[]{:S(2)}) copy-start(f32[1024]{0:T(1024)} %param.37) | copy-start | bytes 12292
  1223.3 46.9 %copy-start.36 = (f32[2,320]{1,0:T(2,128)S(1)}, f32[2,320]{1,0:T(2,128)}, u32[]{:S(2)}) copy-start(f32[2,320]{1,0:T(2,128)} %copy-done.35) | copy-start | bytes 7684
  1223.3 46.9 %copy-start.38 = (f32[2,320]{1,0:T(2,128)S(1)}, f32[2,320]{1,0:T(2,128)}, u32[]{:S(2)}) copy-start(f32[2,320]{1,0:T(2,128)} %copy-done.37) | copy-start | bytes 7684
  1223.3 46.9 %copy-start.44 = (f32[1024]{0:T(1024)S(1)}, f32[1024]{0:T(1024)}, u32[]{:S(2)}) copy-start(f32[1024]{0:T(1024)} %param.35) | copy-start | bytes 12292
  1223.3 46.9 %copy-start.54 = (f32[2,320]{1,0:T(2,128)S(1)}, f32[2,320]{1,0:T(2,128)}, u32[]{:S(2)}) copy-start(f32[2,320]{1,0:T(2,128)} %copy-done.53) | copy-start | bytes 7684
  1223.3 46.9 %copy-start.56 = (f32[2,320]{1,0:T(2,128)S(1)}, f32[2,320]{1,0:T(2,128)}, u32[]{:S(2)}) copy-start(f32[2,320]{1,0:T(2,128)} %copy-done.55) | copy-start | bytes 7684
  1223.3 46.9 %copy-start.58 = (f32[2,320]{1,0:T(2,128)S(1)}, f32[2,320]{1,0:T(2,128)}, u32[]{:S(2)}) copy-start(f32[2,320]{1,0:T(2,128)} %copy-done.57) | copy-start | bytes 7684
  1294.0 59.5 %copy-start.70 = (pred[512]{0:T(512)(128)(4,1)S(1)}, pred[512]{0:T(512)(128)(4,1)}, u32[]{:S(2)}) copy-start(pred[512]{0:T(512)(128)(4,1)} %get-tuple-element.122) | copy-start | bytes 1540
  1396.1 43.7 %copy-start.65 = (pred[1024]{0:T(1024)(128)(4,1)S(1)}, pred[1024]{0:T(1024)(128)(4,1)}, u32[]{:S(2)}) copy-start(pred[1024]{0:T(1024)(128)(4,1)} %get-tuple-element.120) | copy-start | bytes 3076
  (58 other events, 363.4 us)
Sparse Core Ops, SparseCore 0:
  10.2 62.7 all-gather.8
  75.0 38.0 all-gather.10
  118.0 9.4 reduce-scatter.6
  129.5 74.0 all-gather.14
  205.6 37.5 all-gather.12
  245.0 74.6 all-gather.16
  347.2 35.8 reduce-scatter.10
  385.3 37.6 reduce-scatter.8
  428.7 11.3 all-gather.18
  591.6 267.8 reduce-scatter.14
  863.7 335.4 reduce-scatter.16
  1201.8 9.5 reduce-scatter.12
  1214.2 116.1 all-gather.20
  1331.9 88.4 all-gather.22
where the time goes:
time: 1540 us; the launch traced here: 1530 us
  waiting for transfers between devices  732 us (48%)
  local copies, waits for them, and re-layouts  381 us (25%)
  other arithmetic  182 us (12%)
  matrix products  175 us (11%)
  blocking collectives  41.5 us (3%)
  between operations  15.7 us (1%)
    reduce_scatter x1, waiting for transfers between devices, per_device(): lax.psum_scatter(mlp_parcel, ('shard', 'head'), scatter_dimension=0, tile...  311 us
    reshape x6, local copies, waits for them, and re-layouts, split_blocks(): matrix.reshape(leading + (row_count // block_size, block_size, col_count...  83 us
    reduce_scatter x1, waiting for transfers between devices, per_device(): lax.psum_scatter(attn_parcel, ('shard', 'tensor'), scatter_dimension=0, t...  77.7 us
    all_gather x1, waiting for transfers between devices, per_device(): lax.all_gather(w_up, 'shard', axis=0, tiled=True)  67.7 us
    all_gather x1, waiting for transfers between devices, per_device(): lax.all_gather(w_qkv, 'shard', axis=1, tiled=True)  55.6 us
    transpose x4, local copies, waits for them, and re-layouts, join_blocks(): shaped.transpose(axes_order).reshape(leading + (row_count, col_count))  54.9 us
    gather x1, local copies, waits for them, and re-layouts, per_device(): jnp.take(mlp_blocks, mlp_picked, axis=0) * mlp_filled[:, None, None]  46.6 us
    psum x1, blocking collectives, per_device(): lax.psum((ln1_gain_part, ln1_bias_part, ln2_gain_part, ln2_bias_part, out...  41.5 us
  transfers between devices with their start and end apart: 14, of which 13 were waited for; matrix products, arithmetic and copies ran while one was open for 28% of the time, Pallas kernels for 0%

commit v1 on v0

v1 whole, which is shorter than its diff:
```python
from functools import partial

import jax
import jax.numpy as jnp
from jax import lax
from jax.experimental import pallas as pl
from jax.experimental.pallas import tpu as pltpu
from jax.sharding import PartitionSpec as P

HD = 64
FF = 4096
BUF = 64
BS = 64
LANES = 128
F32 = jnp.float32
BF16 = jnp.bfloat16

precise = lax.Precision.HIGHEST


def swap(value, axis):
    return lax.ppermute(value, axis, [(0, 1), (1, 0)])


def total_over_mesh(value):
    for axis in ("head", "tensor", "shard"):
        size = lax.axis_size(axis)
        bit = 1
        while bit < size:
            partner = lax.ppermute(value, axis, [(i, i ^ bit) for i in range(size)])
            value = value + partner
            bit *= 2
    return value


def dot(left, right, contract):
    return lax.dot_general(left, right, ((contract[:1], contract[1:]), ((), ())), preferred_element_type=F32)


def norm_parts(value):
    center = value - jnp.mean(value, axis=-1, keepdims=True)
    inv_root = lax.rsqrt(jnp.mean(center * center, axis=-1, keepdims=True) + 1e-06)
    return (center * inv_root, inv_root)


def norm_back(grad_out, normed, inv_root, gain_vec):
    grad_normed = grad_out * gain_vec
    first_mean = jnp.mean(grad_normed, axis=-1, keepdims=True)
    second_mean = jnp.mean(grad_normed * normed, axis=-1, keepdims=True)
    grad_in = inv_root * (grad_normed - first_mean - normed * second_mean)
    return (grad_in, jnp.sum(grad_out * normed, axis=0), jnp.sum(grad_out, axis=0))


def masked_scores(rows, head, kept_valid, groups):
    q = rows[:, head * HD : (head + 1) * HD]
    k = rows[:, (groups + head) * HD : (groups + head + 1) * HD]
    scores = dot(q, k, (1, 1)) * 0.125
    return jnp.where(kept_valid, scores, -1000000000.0)


def soft(scores):
    shifted = jnp.exp(scores - jnp.max(scores, axis=-1, keepdims=True))
    return shifted * (1.0 / jnp.sum(shifted, axis=-1, keepdims=True))


def attn_forward_body(kept, rows, out):
    groups = rows.shape[1] // (3 * HD)
    slots = rows.shape[0]
    valid = lax.broadcasted_iota(jnp.int32, (slots, slots), 1) < BUF + kept[pl.program_id(0)]
    for pair in range(groups // 2):
        halves = []
        for head in (2 * pair, 2 * pair + 1):
            probs = soft(masked_scores(rows, head, valid, groups)).astype(BF16)
            v = rows[:, (2 * groups + head) * HD : (2 * groups + head + 1) * HD]
            halves.append(dot(probs, v, (1, 0)).astype(BF16))
        out[:, pair * LANES : (pair + 1) * LANES] = jnp.concatenate(halves, axis=1)


def attn_forward(kept, rows, slots):
    images = kept.shape[0]
    width = rows.shape[1]
    return pl.pallas_call(
        attn_forward_body,
        out_shape=jax.ShapeDtypeStruct((images * slots, width // 3), BF16),
        grid_spec=pltpu.PrefetchScalarGridSpec(
            num_scalar_prefetch=1,
            grid=(images,),
            in_specs=[pl.BlockSpec((slots, width), lambda i, kept: (i, 0))],
            out_specs=pl.BlockSpec((slots, width // 3), lambda i, kept: (i, 0)),
        ),
        name="attn_forward",
    )(kept, rows)


def attn_backward_body(kept, rows, grads, out):
    groups = rows.shape[1] // (3 * HD)
    slots = rows.shape[0]
    valid = lax.broadcasted_iota(jnp.int32, (slots, slots), 1) < BUF + kept[pl.program_id(0)]
    for pair in range(groups // 2):
        parts = ([], [], [])
        for head in (2 * pair, 2 * pair + 1):
            probs = soft(masked_scores(rows, head, valid, groups))
            q = rows[:, head * HD : (head + 1) * HD]
            k = rows[:, (groups + head) * HD : (groups + head + 1) * HD]
            v = rows[:, (2 * groups + head) * HD : (2 * groups + head + 1) * HD]
            g = grads[:, head * HD : (head + 1) * HD]
            grad_probs = dot(g, v, (1, 1))
            inner = jnp.sum(probs * grad_probs, axis=-1, keepdims=True)
            grad_scores = (probs * (grad_probs - inner)).astype(BF16)
            parts[0].append((dot(grad_scores, k, (1, 0)) * 0.125).astype(BF16))
            parts[1].append((dot(grad_scores, q, (0, 0)) * 0.125).astype(BF16))
            parts[2].append(dot(probs.astype(BF16), g, (0, 0)).astype(BF16))
        for which in range(3):
            start = which * groups * HD + pair * LANES
            out[:, start : start + LANES] = jnp.concatenate(parts[which], axis=1)


def attn_backward(kept, rows, grads, slots):
    images = kept.shape[0]
    width = rows.shape[1]
    return pl.pallas_call(
        attn_backward_body,
        out_shape=jax.ShapeDtypeStruct(rows.shape, BF16),
        grid_spec=pltpu.PrefetchScalarGridSpec(
            num_scalar_prefetch=1,
            grid=(images,),
            in_specs=[
                pl.BlockSpec((slots, width), lambda i, kept: (i, 0)),
                pl.BlockSpec((slots, width // 3), lambda i, kept: (i, 0)),
            ],
            out_specs=pl.BlockSpec((slots, width), lambda i, kept: (i, 0)),
        ),
        name="attn_backward",
    )(kept, rows, grads)


ERF_TOP = (
    -2.72614225801306e-10,
    2.77068142495902e-08,
    -2.10102402082508e-06,
    -5.69250639462346e-05,
    -7.34990630326855e-04,
    -2.95459980854025e-03,
    -1.60960333262415e-02,
)
ERF_BOTTOM = (
    -1.45660718464996e-05,
    -2.13374055278905e-04,
    -1.68282697438203e-03,
    -7.37332916720468e-03,
    -1.42647390514189e-02,
)


def erf(value):
    value = jnp.clip(value, -4.0, 4.0)
    square = value * value
    top = jnp.full_like(value, ERF_TOP[0])
    for factor in ERF_TOP[1:]:
        top = top * square + factor
    bottom = jnp.full_like(value, ERF_BOTTOM[0])
    for factor in ERF_BOTTOM[1:]:
        bottom = bottom * square + factor
    return value * top / bottom


def feed_body(rows, cot, up, down_t, bias, *refs):
    hidden, grad_pre, bias_sum = refs[-3:]
    pre = dot(rows[...], up[...], (1, 0)) + bias[...]
    grad_hidden = dot(cot[...], down_t[...], (1, 0))
    cdf = 0.5 + 0.5 * erf(pre * 0.7071067811865476)
    density = 0.3989422804014327 * jnp.exp(-0.5 * pre * pre)
    hidden[...] = (pre * cdf).astype(BF16)
    grad = (grad_hidden * (cdf + pre * density)).astype(BF16)
    grad_pre[...] = grad

    @pl.when(pl.program_id(1) == 0)
    def _():
        bias_sum[...] = jnp.zeros(bias_sum.shape, F32)

    bias_sum[...] += jnp.sum(grad.astype(F32), axis=0, keepdims=True)


def feed(rows, cot, up, down_t, bias, half, held, row_block, col_block):
    count, features = rows.shape
    width = up.shape[1]
    steps = count // row_block
    first = half * steps
    whole = jax.ShapeDtypeStruct((2 * count, width), BF16)
    big = pl.BlockSpec((row_block, col_block), lambda j, i: (first + i, j))
    passed = [pl.BlockSpec(memory_space=pl.ANY) for _ in held]
    return pl.pallas_call(
        feed_body,
        out_shape=(whole, whole, jax.ShapeDtypeStruct((1, width), F32)),
        grid=(width // col_block, steps),
        in_specs=[
            pl.BlockSpec((row_block, features), lambda j, i: (i, 0)),
            pl.BlockSpec((row_block, features), lambda j, i: (first + i, 0)),
            pl.BlockSpec((features, col_block), lambda j, i: (0, j)),
            pl.BlockSpec((features, col_block), lambda j, i: (0, j)),
            pl.BlockSpec((1, col_block), lambda j, i: (0, j)),
            *passed,
        ],
        out_specs=(big, big, pl.BlockSpec((1, col_block), lambda j, i: (0, j))),
        input_output_aliases={5: 0, 6: 1} if held else {},
        name="feed",
    )(rows, cot, up, down_t, bias, *held)


def slot_numbers(owner_list, capacity, owners):
    count = owner_list.shape[0]
    onehot = (owner_list[:, None] == jnp.arange(owners, dtype=jnp.int32)[None, :]).astype(BF16)
    order = jnp.arange(count, dtype=jnp.int32)
    before = (order[:, None] > order[None, :]).astype(BF16)
    earlier = dot(before, onehot, (1, 0))
    return owner_list * capacity + jnp.sum(earlier * onehot.astype(F32), axis=1).astype(jnp.int32)


def low_lanes():
    return lax.broadcasted_iota(jnp.int32, (BS // 2, LANES), 1) < BS


def to_parcel_body(indices_of, slots, *refs):
    *inputs, out = refs
    step = pl.program_id(0)

    @pl.when(step == 0)
    def _():
        out[...] = jnp.zeros(out.shape, out.dtype)

    low = low_lanes()
    for number, source in enumerate(inputs):
        rows, cols = source.shape
        for row in range(rows // BS):
            for pair in range(cols // LANES):
                window = pl.ds(pair * LANES, LANES)
                top = source[pl.ds(row * BS, BS // 2), window]
                bottom = source[pl.ds(row * BS + BS // 2, BS // 2), window]
                left, right = indices_of(number, step, row, pair)
                out[slots[left]] = jnp.where(low, top, pltpu.roll(bottom, BS, 1))
                out[slots[right]] = jnp.where(low, pltpu.roll(top, BS, 1), bottom)


def after(value, *others):
    return lax.optimization_barrier((value, *others))[0]


def to_parcel(slots, total, sources, indices_of):
    return pl.pallas_call(
        partial(to_parcel_body, indices_of),
        out_shape=jax.ShapeDtypeStruct((total, BS // 2, LANES), BF16),
        grid_spec=pltpu.PrefetchScalarGridSpec(
            num_scalar_prefetch=1,
            grid=(PARCEL_STEPS,),
            in_specs=[
                pl.BlockSpec((a.shape[0] // PARCEL_STEPS, a.shape[1]), lambda i, slots: (i, 0))
                for a in sources
            ],
            out_specs=pl.BlockSpec(
                (total, BS // 2, LANES), lambda i, slots: (0, 0, 0), pipeline_mode=pl.Buffered(1)
            ),
        ),
        name="to_parcel",
    )(slots, *sources)


PARCEL_STEPS = 4


def attn_parcel(slots, total, qkv_grad, out_grad):
    rows = qkv_grad.shape[0] // BS
    cols = out_grad.shape[0] // BS

    def indices_of(number, step, row, pair):
        if number == 0:
            matrix, col = divmod(2 * pair, cols)
            first = matrix * rows * cols + (step * (rows // PARCEL_STEPS) + row) * cols + col
        else:
            first = 3 * rows * cols + (step * (cols // PARCEL_STEPS) + row) * rows + 2 * pair
        return (first, first + 1)

    sources = (qkv_grad, out_grad)
    return to_parcel(slots, total, sources, indices_of)


def mlp_parcel(slots, total, up_grad, down_grad):
    rows = up_grad.shape[0] // BS
    cols = up_grad.shape[1] // BS

    def indices_of(number, step, row, pair):
        if number == 0:
            first = (step * (rows // PARCEL_STEPS) + row) * cols + 2 * pair
        else:
            first = rows * cols + (step * (cols // PARCEL_STEPS) + row) * rows + 2 * pair
        return (first, first + 1)

    return to_parcel(slots, total, (up_grad, down_grad), indices_of)


def pair_tile(left, right, low):
    top = jnp.where(low, left, pltpu.roll(right, BS, 1))
    bottom = jnp.where(low, pltpu.roll(left, BS, 1), right)
    return (top, bottom)


def local_blocks(place, rows, cols, own):
    matrix = jnp.arange(3, dtype=jnp.int32)[:, None, None]
    row = jnp.arange(own, dtype=jnp.int32)[None, :, None]
    col = jnp.arange(cols, dtype=jnp.int32)[None, None, :]
    first = ((matrix * rows + place * own + row) * cols + col).reshape(-1)
    row = jnp.arange(cols, dtype=jnp.int32)[:, None]
    col = jnp.arange(own, dtype=jnp.int32)[None, :]
    second = (3 * rows * cols + row * rows + place * own + col).reshape(-1)
    return jnp.concatenate([first, second])


def pick_body(table, held, *outs):
    count = outs[0].shape[0]
    for number, out in enumerate(outs):
        for block in range(count):
            out[block] = held[table[number * count + block]]


def pick(table, held, outs):
    whole = pl.BlockSpec(memory_space=pltpu.VMEM)
    shape = jax.ShapeDtypeStruct((table.shape[0] // outs,) + held.shape[1:], held.dtype)
    return pl.pallas_call(
        pick_body,
        out_shape=(shape,) * outs,
        in_specs=[pl.BlockSpec(memory_space=pltpu.SMEM), whole],
        out_specs=(whole,) * outs,
        name="pick",
    )(table, held)


def attn_finish_body(held, arrived, qkv_out, out_out):
    low = low_lanes()
    own = qkv_out.shape[1] // BS
    cols = qkv_out.shape[2] // BS

    def put(target, row, pair, first):
        top, bottom = pair_tile(held[first] + arrived[first], held[first + 1] + arrived[first + 1], low)
        window = pl.ds(pair * LANES, LANES)
        target[pl.ds(row * BS, BS // 2), window] = top
        target[pl.ds(row * BS + BS // 2, BS // 2), window] = bottom

    for matrix in range(3):
        for row in range(own):
            for pair in range(cols // 2):
                put(qkv_out.at[matrix], row, pair, (matrix * own + row) * cols + 2 * pair)
    for row in range(cols):
        for pair in range(own // 2):
            put(out_out, row, pair, 3 * own * cols + row * own + 2 * pair)


def attn_finish(held, arrived, shapes):
    whole = pl.BlockSpec(memory_space=pltpu.VMEM)
    return pl.pallas_call(
        attn_finish_body,
        out_shape=tuple(jax.ShapeDtypeStruct(shape, BF16) for shape in shapes),
        in_specs=[whole, whole],
        out_specs=tuple(whole for _ in shapes),
        name="attn_finish",
    )(held, arrived)


def mlp_return_body(rows, cols, slots, place, held, up_out, down_out):
    low = low_lanes()
    mine = place[0]
    own = up_out.shape[0] // BS

    def put(target, row, pair, first):
        top, bottom = pair_tile(held[slots[first]], held[slots[first + 1]], low)
        window = pl.ds(pair * LANES, LANES)
        target[pl.ds(row * BS, BS // 2), window] = top
        target[pl.ds(row * BS + BS // 2, BS // 2), window] = bottom

    for row in range(own):
        for pair in range(cols // 2):
            put(up_out, row, pair, (mine * own + row) * cols + 2 * pair)
    for row in range(cols):
        for pair in range(own // 2):
            put(down_out, row, pair, rows * cols + row * rows + mine * own + 2 * pair)


def from_slots(body, slots, place, held, shapes):
    whole = pl.BlockSpec(memory_space=pltpu.VMEM)
    table = pl.BlockSpec(memory_space=pltpu.SMEM)
    return pl.pallas_call(
        body,
        out_shape=tuple(jax.ShapeDtypeStruct(shape, BF16) for shape in shapes),
        in_specs=[table, table, whole],
        out_specs=tuple(whole for _ in shapes),
        name="from_slots",
    )(slots, place, held)


def unpack(dense):
    return jnp.concatenate([dense[:, :, :BS], dense[:, :, BS:]], axis=1)


def pack(blocks):
    return jnp.concatenate([blocks[:, : BS // 2], blocks[:, BS // 2 :]], axis=2)


def join_blocks(blocks_in, leading, row_count, col_count):
    shaped = blocks_in.reshape(leading + (row_count // BS, col_count // BS, BS, BS))
    depth = len(leading)
    axes_order = tuple(range(depth)) + (depth, depth + 2, depth + 1, depth + 3)
    return shaped.transpose(axes_order).reshape(leading + (row_count, col_count))


def soap_update(gradient, left_basis, right_basis, first_moment, second, master):
    turned = jnp.einsum("sji,sjk->sik", left_basis, gradient, precision=precise)
    turned = jnp.einsum("sik,skl->sil", turned, right_basis, precision=precise)
    first_new = 0.95 * first_moment + 0.05 * turned
    second_new = 0.95 * second + 0.05 * turned * turned
    direction = first_new / (jnp.sqrt(second_new) + 1e-08)
    rotated_back = jnp.einsum("sij,sjk->sik", left_basis, direction, precision=precise)
    rotated_back = jnp.einsum("sik,slk->sil", rotated_back, right_basis, precision=precise)
    return (first_new, second_new, master - 0.05 * rotated_back)


def per_device(
    tokens,
    kept_counts,
    cotangent,
    w_qkv,
    w_out,
    w_up,
    w_down,
    ln1_gain,
    ln1_bias,
    ln2_gain,
    ln2_bias,
    out_bias,
    up_bias,
    down_bias,
    attn_owner,
    mlp_owner,
    attn_left,
    attn_right,
    attn_first,
    attn_second,
    attn_master,
    mlp_left,
    mlp_right,
    mlp_first,
    mlp_second,
    mlp_master,
):
    head_pos = lax.axis_index("head")
    tensor_pos = lax.axis_index("tensor")
    shard_pos = lax.axis_index("shard")
    local_images, slot_count, features = tokens.shape
    per_out = local_images // 4
    own_rows = per_out * slot_count

    attn_mine = jnp.concatenate([w_qkv[0], w_qkv[1], w_qkv[2], w_out.T], axis=1)
    attn_full = lax.all_gather(attn_mine, "shard", axis=0, tiled=True)
    group_cols = w_qkv.shape[2]
    qkv_full = attn_full[:, : 3 * group_cols]
    out_full_t = attn_full[:, 3 * group_cols :]
    mlp_mine = lax.all_gather(
        jnp.where(head_pos == 0, w_up, w_down.T), "shard", axis=0, tiled=True
    )
    hidden_cols = mlp_mine.shape[1]

    def images_of(array, start):
        return lax.dynamic_slice_in_dim(array, start * per_out, per_out, 0)

    own_index = head_pos * 2 + tensor_pos
    pair_index = (1 - head_pos) * 2 + tensor_pos
    attn_tokens = jnp.concatenate([images_of(tokens, own_index), images_of(tokens, pair_index)])
    attn_tokens = attn_tokens.reshape(2 * own_rows, features)
    own_kept = images_of(kept_counts, own_index)
    attn_kept = jnp.concatenate([own_kept, images_of(kept_counts, pair_index)])
    mlp_kept = jnp.concatenate([own_kept, images_of(kept_counts, head_pos * 2 + 1 - tensor_pos)])
    mlp_cot = jnp.concatenate([images_of(cotangent, tensor_pos), images_of(cotangent, 1 - tensor_pos)])
    positions = jnp.arange(slot_count, dtype=jnp.int32)
    mlp_valid = positions[None, :] < (BUF + mlp_kept)[:, None]
    mlp_cot = jnp.where(mlp_valid[:, :, None], mlp_cot, jnp.zeros_like(mlp_cot))
    mlp_cot = mlp_cot.reshape(2 * own_rows, features)
    own_valid = mlp_valid[:per_out].reshape(own_rows, 1).astype(F32)
    own_cot = mlp_cot[:own_rows].astype(F32)

    normed_one, inv_one = norm_parts(attn_tokens.astype(F32))
    low_one = (normed_one * ln1_gain + ln1_bias).astype(BF16)
    projected = dot(low_one, qkv_full, (1, 0)).astype(BF16)
    heads_out = attn_forward(attn_kept, projected, slot_count)
    pair_branch = dot(heads_out[own_rows:], out_full_t, (1, 1)).astype(BF16)
    branch_in = swap(pair_branch, "head")
    own_branch = dot(heads_out[:own_rows], out_full_t, (1, 1))
    residual = attn_tokens[:own_rows].astype(F32) + (own_branch + branch_in.astype(F32)) + out_bias
    normed_two, inv_two = norm_parts(residual)
    low_two = (normed_two * ln2_gain + ln2_bias).astype(BF16)

    low_in = swap(low_two, "tensor")
    mlp_mine = after(mlp_mine, low_in)
    mlp_other = swap(mlp_mine, "head")
    up_full = jnp.where(head_pos == 0, mlp_mine, mlp_other)
    down_full_t = jnp.where(head_pos == 0, mlp_other, mlp_mine)
    up_local = lax.dynamic_slice_in_dim(up_bias, tensor_pos * hidden_cols, hidden_cols, 0)[None]
    hidden_half, pre_half, pair_sum = feed(
        low_in, mlp_cot, up_full, down_full_t, up_local, 1, (), slot_count, 512
    )
    pair_normed = dot(pre_half[own_rows:], up_full, (1, 1)).astype(BF16)
    normed_in = swap(pair_normed, "tensor")
    hidden, grad_pre, own_sum = feed(
        low_two, mlp_cot, up_full, down_full_t, up_local, 0,
        (hidden_half, after(pre_half, pair_normed)), slot_count, 512,
    )
    up_bias_part = pair_sum + own_sum
    own_grad_normed = dot(grad_pre[:own_rows], up_full, (1, 1))
    normed_rows = jnp.concatenate([low_two, low_in])
    up_grad = dot(normed_rows, grad_pre, (0, 0)).astype(BF16)
    down_grad = dot(hidden, mlp_cot, (0, 0)).astype(BF16)
    mlp_owners = lax.axis_size(("shard", "head"))
    mlp_cap = mlp_master.shape[1]
    mlp_slots = slot_numbers(mlp_owner[0, :, 0], mlp_cap, mlp_owners)
    mlp_parts = mlp_parcel(mlp_slots, mlp_owners * mlp_cap, up_grad, down_grad)
    mlp_sum = lax.psum_scatter(mlp_parts, ("shard", "head"), scatter_dimension=0, tiled=True)
    pair_mlp = dot(hidden[own_rows:], down_full_t, (1, 1)).astype(BF16)
    mlp_in = swap(pair_mlp, "tensor")
    own_mlp = dot(hidden[:own_rows], down_full_t, (1, 1))
    mlp_out = own_mlp + mlp_in.astype(F32) + down_bias
    out = (own_valid * (residual + mlp_out)).astype(BF16)
    resid_from, ln2_gain_part, ln2_bias_part = norm_back(
        own_grad_normed + normed_in.astype(F32), normed_two, inv_two, ln2_gain
    )
    down_bias_part = jnp.sum(own_cot, axis=0)
    grad_resid = own_cot + resid_from
    grad_branch = grad_resid.astype(BF16)
    out_bias_part = jnp.sum(grad_branch.astype(F32), axis=0)

    branch_rows = jnp.concatenate([grad_branch, after(swap(grad_branch, "head"), mlp_parts)])
    grad_heads = dot(branch_rows, out_full_t, (1, 0)).astype(BF16)
    grad_proj = attn_backward(attn_kept, projected, grad_heads, slot_count)
    out_grad = dot(heads_out, branch_rows, (0, 0)).astype(BF16)
    qkv_grad = dot(low_one, grad_proj, (0, 0)).astype(BF16)
    pair_input = dot(grad_proj[own_rows:], qkv_full, (1, 1)).astype(BF16)
    input_in = swap(pair_input, "head")
    own_input = dot(grad_proj[:own_rows], qkv_full, (1, 1))
    tokens_from, ln1_gain_part, ln1_bias_part = norm_back(
        own_input + input_in.astype(F32), normed_one[:own_rows], inv_one[:own_rows], ln1_gain
    )
    tokens_grad = grad_resid + tokens_from

    up_whole = lax.dynamic_update_slice_in_dim(
        jnp.zeros((FF,), F32), up_bias_part[0], tensor_pos * hidden_cols, 0
    )
    small = jnp.concatenate(
        [
            ln1_gain_part,
            ln1_bias_part,
            ln2_gain_part,
            ln2_bias_part,
            out_bias_part,
            down_bias_part,
            up_whole,
        ]
    ).reshape(-1, LANES)
    small = total_over_mesh(small).reshape(-1)
    small_sums = [small[i * features : (i + 1) * features] for i in range(6)] + [small[6 * features :]]

    place = shard_pos.reshape(1).astype(jnp.int32)
    rows = features // BS

    shards = lax.axis_size("shard")
    tensors = lax.axis_size("tensor")
    attn_owners = shards * tensors
    attn_cap = attn_master.shape[1]
    attn_total = attn_owners * attn_cap
    attn_slots = slot_numbers(attn_owner[0, :, 0], attn_cap, attn_owners)
    direct = shards == 8 and tensors == 2
    if direct:
        owner = attn_owner[0, :, 0]
        inner = attn_slots - owner * attn_cap
        off_tensor = (owner % tensors) ^ tensor_pos
        off_shard = (owner // tensors) ^ shard_pos
        bit, high = off_shard % 2, off_shard // 2
        columns = shards // 2
        sizes = ((attn_cap + 1) // 2, attn_cap // 2)
        start = attn_owners * sizes[0]
        spot = jnp.where(
            inner < sizes[0],
            ((off_tensor * 2 + bit) * columns + high) * sizes[0] + inner,
            start + ((bit * 2 + off_tensor) * columns + high) * sizes[1] + inner - sizes[0],
        )
        parts = attn_parcel(spot, attn_total, qkv_grad, out_grad)

        def across(value, bits):
            return lax.ppermute(value, "shard", [(i, i ^ bits) for i in range(shards)])

        def so_far(which, first, count, arrived):
            size = columns * sizes[which]
            begin = which * start
            total = parts[begin + first * size : begin + first * size + count].astype(F32)
            for array in arrived:
                total = total + array[first * size : first * size + count].astype(F32)
            return total

        spans = [columns * size for size in sizes]
        first_a = swap(parts[2 * spans[0] : 4 * spans[0]], "tensor")
        first_b = across(parts[start + 2 * spans[1] : start + 4 * spans[1]], 1)
        next_a = so_far(0, 1, spans[0], (first_a,)).astype(BF16)
        next_b = so_far(1, 1, spans[1], (first_b,)).astype(BF16)
        mlp_sum = after(mlp_sum, next_a, next_b)
        second_a = across(next_a, 1)
        second_b = swap(next_b, "tensor")
        sums = jnp.concatenate(
            [
                so_far(0, 0, spans[0], (first_a, second_a)).reshape(columns, sizes[0], BS // 2, LANES),
                so_far(1, 0, spans[1], (first_b, second_b)).reshape(columns, sizes[1], BS // 2, LANES),
            ],
            axis=1,
        )
        attn_sum = sums[0]
        for step in range(1, columns):
            attn_sum = attn_sum + across(sums[step].astype(BF16), 2 * step).astype(F32)
    else:
        parts = attn_parcel(attn_slots, attn_total, qkv_grad, out_grad)
        attn_sum = lax.psum_scatter(parts, ("shard", "tensor"), scatter_dimension=0, tiled=True)
    attn_sum = unpack(attn_sum).astype(F32)
    mlp_sum = unpack(mlp_sum).astype(F32)

    mlp_first_new, mlp_second_new, mlp_master_new = soap_update(
        mlp_sum, mlp_left[0], mlp_right[0], mlp_first[0], mlp_second[0], mlp_master[0]
    )
    mlp_dense = pack(mlp_master_new.astype(BF16))
    if direct:
        mlp_dense = after(mlp_dense, second_a, second_b)
    mlp_all = lax.all_gather(mlp_dense, ("shard", "head"), axis=0, tiled=True)
    mlp_outs = lax.optimization_barrier(
        tuple(jnp.transpose(a, (1, 2, 0)) for a in (mlp_sum, mlp_first_new, mlp_second_new, mlp_master_new))
    )
    attn_first_new, attn_second_new, attn_master_new = soap_update(
        attn_sum, attn_left[0], attn_right[0], attn_first[0], attn_second[0], attn_master[0]
    )
    attn_dense = pack(attn_master_new.astype(BF16))

    own = w_qkv.shape[1]
    if direct:
        column = [attn_dense] + [across(attn_dense, 2 * step) for step in range(1, columns)]
        empty = jnp.zeros((1,) + attn_dense.shape[1:], BF16)
        here = (off_tensor == 0) & (bit == 0)
        where = jnp.where(here, high * attn_cap + inner, columns * attn_cap)
        lists = [local_blocks(p, rows, group_cols // BS, own // BS) for p in (shard_pos, shard_pos ^ 1)]
        table = jnp.take(where, jnp.concatenate(lists), axis=0)
        mine, theirs = pick(after(table, *mlp_outs), jnp.concatenate(column + [empty]), 2)
        mine = mine + across(theirs, 1)
        w_qkv_new, w_out_new = attn_finish(mine, swap(mine, "tensor"), (w_qkv.shape, w_out.shape))
        w_up_new, w_down_new = from_slots(
            partial(mlp_return_body, rows, hidden_cols // BS),
            mlp_slots,
            place,
            mlp_all,
            (w_up.shape, w_down.shape),
        )
    else:
        attn_all = lax.all_gather(attn_dense, ("shard", "tensor"), axis=0, tiled=True)
        attn_new = unpack(jnp.take(attn_all, attn_slots, axis=0))
        qkv_count = 3 * rows * (group_cols // BS)
        new_qkv = join_blocks(attn_new[:qkv_count], (3,), features, group_cols)
        new_out = join_blocks(attn_new[qkv_count:], (), group_cols, features)
        w_qkv_new = lax.dynamic_slice_in_dim(new_qkv, shard_pos * own, own, 1)
        w_out_new = lax.dynamic_slice_in_dim(new_out, shard_pos * own, own, 1)
        mlp_new = unpack(jnp.take(mlp_all, mlp_slots, axis=0))
        up_count = rows * (hidden_cols // BS)
        new_up = join_blocks(mlp_new[:up_count], (), features, hidden_cols)
        new_down = join_blocks(mlp_new[up_count:], (), hidden_cols, features)
        w_up_new = lax.dynamic_slice_in_dim(new_up, shard_pos * own, own, 0)
        w_down_new = lax.dynamic_slice_in_dim(new_down, shard_pos * own, own, 1)

    return (
        out.reshape(per_out, slot_count, features),
        tokens_grad.reshape(per_out, slot_count, features),
        *small_sums,
        attn_sum[None],
        attn_first_new[None],
        attn_second_new[None],
        attn_master_new[None],
        *(jnp.transpose(array, (2, 0, 1))[None] for array in mlp_outs),
        w_qkv_new,
        w_out_new,
        w_up_new,
        w_down_new,
    )


def solution(mesh):
    placed = (
        P("shard", None, None),
        P("shard"),
        P(("shard", "head"), None, None),
        P(None, "shard", "head"),
        P("head", "shard"),
        P("shard", "tensor"),
        P("tensor", "shard"),
        P(),
        P(),
        P(),
        P(),
        P(),
        P(),
        P(),
        P("head", None, None),
        P("tensor", None, None),
        P("head", ("shard", "tensor"), None, None),
        P("head", ("shard", "tensor"), None, None),
        P("head", ("shard", "tensor"), None, None),
        P("head", ("shard", "tensor"), None, None),
        P("head", ("shard", "tensor"), None, None),
        P("tensor", ("shard", "head"), None, None),
        P("tensor", ("shard", "head"), None, None),
        P("tensor", ("shard", "head"), None, None),
        P("tensor", ("shard", "head"), None, None),
        P("tensor", ("shard", "head"), None, None),
    )
    return jax.shard_map(
        per_device,
        mesh=mesh,
        in_specs=placed,
        out_specs=(
            P(("shard", "head", "tensor"), None, None),
            P(("shard", "head", "tensor"), None, None),
            P(),
            P(),
            P(),
            P(),
            P(),
            P(),
            P(),
            P("head", ("shard", "tensor"), None, None),
            P("head", ("shard", "tensor"), None, None),
            P("head", ("shard", "tensor"), None, None),
            P("head", ("shard", "tensor"), None, None),
            P("tensor", ("shard", "head"), None, None),
            P("tensor", ("shard", "head"), None, None),
            P("tensor", ("shard", "head"), None, None),
            P("tensor", ("shard", "head"), None, None),
            P(None, "shard", "head"),
            P("head", "shard"),
            P("shard", "tensor"),
            P("tensor", "shard"),
        ),
        check_vma=False,
    )
```

time: 1540 us -> 563 us (0.37)
  waiting for transfers between devices: 732 us -> 198 us
  local copies, waits for them, and re-layouts: 381 us -> 55.3 us
  other arithmetic: 182 us -> 46.1 us
  Pallas kernels: 0 us -> 105 us
  matrix products: 175 us -> 109 us
  blocking collectives: 41.5 us -> 0 us
  starting transfers between devices: 0.57 us -> 25.8 us
    reduce_scatter x6 -> x1, waiting for transfers between devices: 460 us -> 0.01 us  [per_device(): lax.psum_scatter(mlp_parts, ('shard', 'head'), scatter_dimension=0, tiled...]
    all_gather x8 -> x3, waiting for transfers between devices: 270 us -> 101 us  [the longest x1 65.2 us: per_device(): attn_full = lax.all_gather(attn_mine, 'shard', axis=0, tiled=True)]
    gather x4 -> x1, local copies, waits for them, and re-layouts: 125 us -> 1.27 us  [per_device(): table = jnp.take(where, jnp.concatenate(lists), axis=0)]
    reshape x11 -> x0, local copies, waits for them, and re-layouts: 120 us -> none  [the longest x6 83 us: split_blocks(): matrix.reshape(leading + (row_count // block_size, block_size, col_count...]
    pallas_call x0 -> x9, Pallas kernels: none -> 105 us  [the longest x2 32.7 us: feed(): pl.pallas_call(feed_body, out_shape=(whole, whole, jax.ShapeDtypeStruct((...]
    ppermute x0 -> x24, waiting for transfers between devices: none -> 96.9 us  [the longest x10 51.4 us: swap(): return lax.ppermute(value, axis, [(0, 1), (1, 0)])]
    dot_general x18 -> x16, matrix products: 149 us -> 89.1 us  [dot(): lax.dot_general(left, right, ((contract[:1], contract[1:]), ((), ())), pr...]
    transpose x4 -> x0, local copies, waits for them, and re-layouts: 54.9 us -> none  [join_blocks(): shaped.transpose(axes_order).reshape(leading + (row_count, col_count))]
  transfers between devices with their start and end apart: 14 -> 28, of which waited for: 13 -> 14; matrix products, arithmetic and copies ran while one was open for 28% -> 31% of each run, Pallas kernels for 0% -> 10%
where the time goes in v1:
time: 563 us; the launch traced here: 554 us
  waiting for transfers between devices  198 us (35%)
  matrix products  109 us (19%)
  Pallas kernels  105 us (19%)
  local copies, waits for them, and re-layouts  55.3 us (10%)
  other arithmetic  46.1 us (8%)
  starting transfers between devices  25.8 us (5%)
  between operations  14.9 us (3%)
    dot_general x16, matrix products, dot(): lax.dot_general(left, right, ((contract[:1], contract[1:]), ((), ())), pr...  89.1 us
    all_gather x1, waiting for transfers between devices, per_device(): attn_full = lax.all_gather(attn_mine, 'shard', axis=0, tiled=True)  65.2 us
    ppermute x10, waiting for transfers between devices, swap(): return lax.ppermute(value, axis, [(0, 1), (1, 0)])  51.4 us
    ppermute x9, waiting for transfers between devices, across(): return lax.ppermute(value, 'shard', [(i, i ^ bits) for i in range(shards)])  36.2 us
    all_gather x1, waiting for transfers between devices, per_device(): lax.all_gather(jnp.where(head_pos == 0, w_up, w_down.T), 'shard', axis=0,...  35.7 us
    pallas_call x2, Pallas kernels, feed(): pl.pallas_call(feed_body, out_shape=(whole, whole, jax.ShapeDtypeStruct((...  32.7 us
    unnamed x138, local copies, waits for them, and re-layouts  31.6 us
    pallas_call x1, Pallas kernels, attn_backward(): pl.pallas_call(attn_backward_body, out_shape=jax.ShapeDtypeStruct(rows.sh...  28.1 us
  transfers between devices with their start and end apart: 28, of which 14 were waited for; matrix products, arithmetic and copies ran while one was open for 31% of the time, Pallas kernels for 10%

profile of v1, /device:TPU:0, one launch (start us, length us, event | category | flops | bytes accessed | tf_op | source)
XLA Modules:
  0.0 554.2 jit_solution(999670095170845084)
XLA Ops:
  22.9 65.2 %all-gather.4.cloned.1.call-done = bf16[1024,2048]{0,1:T(8,128)(2,1)} async-done(((bf16[128,2048]{0,1:T(8,128)(2,1)}), bf16[1024,2048]{0,1:T(8,128)(2,1)}) %all-gather.4.cloned.1.call-update) | async-done | bytes 4194320 | tf_op jit(solution)/shard_map/all_gather | solution.py:460
  88.1 9.6 %convolution_convert_fusion.rows = bf16[1280,1536]{1,0:T(8,128)(2,1)} fusion(bf16[1024,2048]{0,1:T(8,128)(2,1)} %all-gather.4.cloned.1.call-done, f32[1280,1024]{1,0:T(8,128)} %fusion, f32[1024]{0:T(1024)S(1)} %copy-done.55, f32[1024]{0:T(1024)S(1)} %copy-done.48), kind=kOutput, calls=%fused_computation.1 | convolution fusion | flops 4032430080 | bytes 12328960 | tf_op jit(solution)/shard_map/dot_general | solution.py:37
  97.7 17.6 %attn_forward.1 = bf16[1280,512]{1,0:T(8,128)(2,1)} custom-call(s32[4]{0:T(128)} %get-tuple-element.220.kept, bf16[1280,1536]{1,0:T(8,128)(2,1)} %convolution_convert_fusion.rows), custom_call_target="tpu_custom_call" | custom-call | tf_op jit(solution)/shard_map/attn_forward/pallas_call | solution.py:82
  126.2 35.7 %all-gather.6.cloned.1.call-done = bf16[1024,2048]{1,0:T(8,128)(2,1)} async-done(((bf16[128,2048]{1,0:T(8,128)(2,1)}), bf16[1024,2048]{1,0:T(8,128)(2,1)}) %all-gather.6.cloned.1.call-update) | async-done | bytes 4194320 | tf_op jit(solution)/shard_map/all_gather | solution.py:464
  170.0 5.2 broadcast_select_fusion.1
  175.2 16.3 %feed.2 = (bf16[1280,2048]{1,0:T(8,128)(2,1)}, bf16[1280,2048]{1,0:T(8,128)(2,1)}, f32[1,2048]{1,0:T(1,128)}) custom-call(bf16[640,1024]{1,0:T(8,128)(2,1)} %collective-permute-done.1.rows, bf16[1280,1024]{1,0:T(8,128)(2,1)} %bitcast_select_fusion.cot, bf16[1024,2048]{1,0:T(8,128)(2,1)} %get-tuple-element.185.up, ...), custom_call_target="tpu_custom_call" | custom-call | tf_op jit(solution)/shard_map/feed/pallas_call | solution.py:192
  191.5 6.9 %fusion.34 = bf16[640,1024]{1,0:T(8,128)(2,1)} fusion(bf16[1024,2048]{1,0:T(8,128)(2,1)} %get-tuple-element.185.up, bf16[1280,2048]{1,0:T(8,128)(2,1)} %get-tuple-element.46.refs_1_), kind=kOutput, calls=%fused_computation.69 | convolution fusion | flops 2685009920 | bytes 8126464 | tf_op jit(solution)/shard_map/dot_general | solution.py:37
  198.4 16.4 %feed.3 = (bf16[1280,2048]{1,0:T(8,128)(2,1)}, bf16[1280,2048]{1,0:T(8,128)(2,1)}, f32[1,2048]{1,0:T(1,128)}) custom-call(bf16[640,1024]{1,0:T(8,128)(2,1)} %copy-done.18, bf16[1280,1024]{1,0:T(8,128)(2,1)} %bitcast_select_fusion.cot, bf16[1024,2048]{1,0:T(8,128)(2,1)} %get-tuple-element.185.up, ...), custom_call_target="tpu_custom_call", output_to_operand_aliasing={{0}: (5, {}), {1}: (6, {})} | custom-call | tf_op jit(solution)/shard_map/feed/pallas_call | solution.py:192
  214.8 10.3 %convolution_convert_fusion.1.refs_1_ = bf16[2048,1024]{1,0:T(8,128)(2,1)} fusion(bf16[1280,2048]{1,0:T(8,128)(2,1)} %get-tuple-element.47, bf16[1280,1024]{1,0:T(8,128)(2,1)} %bitcast_select_fusion.cot), kind=kOutput, calls=%fused_computation.10 | convolution fusion | flops 5370806272 | bytes 12058624 | tf_op jit(solution)/shard_map/dot_general | solution.py:37
  225.2 8.7 %convolution_convert_fusion.2.refs_0_ = bf16[1024,2048]{1,0:T(8,128)(2,1)} fusion(bf16[1280,2048]{1,0:T(8,128)(2,1)S(1)} %copy-done.17, bf16[640,1024]{1,0:T(8,128)(2,1)} %collective-permute-done.1.rows, bf16[640,1024]{1,0:T(8,128)(2,1)S(1)} %copy-done.19), kind=kOutput, calls=%fused_computation.11 | convolution fusion | flops 5376049152 | bytes 12058624 | tf_op jit(solution)/shard_map/dot_general | solution.py:37
  233.9 10.3 %to_parcel.2 = bf16[1040,32,128]{2,1,0:T(8,128)(2,1)} custom-call(s32[1024]{0:T(1024)} %convert_add_fusion.5.slots, bf16[1024,2048]{1,0:T(8,128)(2,1)} %convolution_convert_fusion.2.refs_0_, bf16[2048,1024]{1,0:T(8,128)(2,1)} %convolution_convert_fusion.1.refs_1_), custom_call_target="tpu_custom_call" | custom-call | tf_op jit(solution)/shard_map/to_parcel/pallas_call | solution.py:249
  246.1 29.6 %collective-permute-done.4 = bf16[640,1024]{1,0:T(8,128)(2,1)S(1)} collective-permute-done((bf16[640,1024]{1,0:T(8,128)(2,1)}, bf16[640,1024]{1,0:T(8,128)(2,1)S(1)}, u32[]{:S(2)}, u32[]{:S(2)}) %collective-permute-start.4) | collective-permute-done | bytes 1310752 | tf_op jit(solution)/shard_map/ppermute | solution.py:22
  275.7 6.2 %multiply_reduce_fusion.1 = (f32[1024]{0:T(1024)S(1)}, f32[640]{0:T(1024)S(1)}, f32[640]{0:T(1024)S(1)}, f32[1024]{0:T(1024)S(1)}, f32[640,1024]{1,0:T(8,128)S(1)}) fusion(f32[640,1024]{1,0:T(8,128)} %copy-done.3, f32[640]{0:T(1024)S(1)} %add_rsqrt_fusion.1, f32[640]{0:T(1024)S(1)} %broadcast_multiply_fusion.5, f32[1024]{0:T(1024)S(1)} %copy-done.44, ...), kind=kOutput, calls=%fused_computation.29 | convolution fusion | flops 2691560448 | bytes 13391872 | tf_op jit(solution)/shard_map/dot_general | solution.py:37
  287.6 4.3 convolution_convert_fusion.4.grads
  291.9 28.1 %attn_backward.1 = bf16[1280,1536]{1,0:T(8,128)(2,1)} custom-call(s32[4]{0:T(128)} %get-tuple-element.220.kept, bf16[1280,1536]{1,0:T(8,128)(2,1)} %convolution_convert_fusion.rows, bf16[1280,512]{1,0:T(8,128)(2,1)} %convolution_convert_fusion.4.grads), custom_call_target="tpu_custom_call" | custom-call | tf_op jit(solution)/shard_map/attn_backward/pallas_call | solution.py:121
  320.0 4.4 fusion.45.refs_1_
  324.5 8.3 %convolution_convert_fusion.3.refs_0_ = bf16[1024,1536]{1,0:T(8,128)(2,1)} fusion(bf16[1280,1536]{1,0:T(8,128)(2,1)S(1)} %copy-done.31, f32[1280,1024]{1,0:T(8,128)} %fusion, f32[1024]{0:T(1024)S(1)} %copy-done.55, f32[1024]{0:T(1024)S(1)} %copy-done.48), kind=kOutput, calls=%fused_computation.12 | convolution fusion | flops 4032036864 | bytes 12328960 | tf_op jit(solution)/shard_map/dot_general | solution.py:37
  332.8 7.0 %to_parcel.3 = bf16[528,32,128]{2,1,0:T(8,128)(2,1)} custom-call(s32[512]{0:T(512)} %get-tuple-element.216.slots, bf16[1024,1536]{1,0:T(8,128)(2,1)} %convolution_convert_fusion.3.refs_0_, bf16[512,1024]{1,0:T(8,128)(2,1)} %fusion.45.refs_1_), custom_call_target="tpu_custom_call" | custom-call | tf_op jit(solution)/shard_map/to_parcel/pallas_call | solution.py:249
  353.1 3.9 copy.140
  357.0 3.9 copy.135
  360.9 3.9 copy.141
  385.9 4.9 fusion.125
  392.9 5.8 %fusion.40 = bf16[640,1024]{1,0:T(8,128)(2,1)} fusion(bf16[1024,2048]{0,1:T(8,128)(2,1)} %all-gather.4.cloned.1.call-done, bf16[1280,1536]{1,0:T(8,128)(2,1)} %attn_backward.1), kind=kOutput, calls=%fused_computation.72 | convolution fusion | flops 2013921280 | bytes 6422528 | tf_op jit(solution)/shard_map/dot_general | solution.py:37
  401.0 7.2 %fusion.37 = bf16[640,1024]{1,0:T(8,128)(2,1)} fusion(bf16[1024,2048]{1,0:T(8,128)(2,1)} %get-tuple-element.186.down_t, bf16[1280,2048]{1,0:T(8,128)(2,1)} %get-tuple-element.47), kind=kOutput, calls=%fused_computation.70 | convolution fusion | flops 2685009920 | bytes 8126464 | tf_op jit(solution)/shard_map/dot_general | solution.py:37
  410.2 5.5 multiply_reduce_fusion.2
  425.5 14.6 %collective-permute-done.3 = bf16[640,1024]{1,0:T(8,128)(2,1)} collective-permute-done((bf16[640,1024]{1,0:T(8,128)(2,1)}, bf16[640,1024]{1,0:T(8,128)(2,1)}, u32[]{:S(2)}, u32[]{:S(2)}) %collective-permute-start.3) | collective-permute-done | bytes 1310752 | tf_op jit(solution)/shard_map/ppermute | solution.py:22
  440.1 6.3 %multiply_convert_fusion = bf16[640,1024]{1,0:T(8,128)(2,1)} fusion(f32[640,1024]{1,0:T(8,128)S(1)} %copy-done.5, bf16[640,1024]{1,0:T(8,128)(2,1)} %collective-permute-done.3, f32[1024]{0:T(1024)S(1)} %copy-done.56, f32[640]{0:T(1024)S(1)} %reshape.521, bf16[1024,2048]{1,0:T(8,128)(2,1)S(1)} %copy-done.1, bf16[1280,2048]{1,0:T(8,128)(2,1)} %get-tuple-element.47), kind=kOutput, calls=%fused_computation.38 | convolution fusion | flops 2688286720 | bytes 12065280 | tf_op jit(solution)/shard_map/dot_general | solution.py:37
  447.7 27.0 %collective-permute-done.17 = bf16[33,32,128]{2,1,0:T(8,128)(2,1)S(1)} collective-permute-done((bf16[33,32,128]{2,1,0:T(8,128)(2,1)S(1)}, bf16[33,32,128]{2,1,0:T(8,128)(2,1)S(1)}, u32[]{:S(2)}, u32[]{:S(2)}) %collective-permute-start.17) | collective-permute-done | bytes 270368 | tf_op jit(solution)/shard_map/ppermute | solution.py:593
  489.5 9.0 %collective-permute-done.10 = f32[80,128]{1,0:T(8,128)S(1)} collective-permute-done((f32[80,128]{1,0:T(8,128)S(1)}, f32[80,128]{1,0:T(8,128)S(1)}, u32[]{:S(2)}, u32[]{:S(2)}) %collective-permute-start.10) | collective-permute-done | bytes 40992 | tf_op jit(solution)/shard_map/ppermute | solution.py:30
  499.3 5.2 collective-permute-done.20
  515.6 5.5 multiply_add_fusion.1
  542.8 4.7 from_slots.1
  (293 shorter events, 141.7 us)
Async XLA Ops:
  7.2 470.7 %copy-start = (f32[1,33,64,64]{3,2,1,0:T(8,128)S(1)}, f32[1,33,64,64]{3,2,1,0:T(8,128)}, u32[]{:S(2)}) copy-start(f32[1,33,64,64]{3,2,1,0:T(8,128)} %param.43) | copy-start | bytes 1622020
  7.2 80.9 %all-gather.4.cloned.1.call-start = ((), (), s32[]{:S(2)}) async-start(), calls=%async_computation.1 | async-start | bytes 4718592 | tf_op jit(solution)/shard_map/all_gather | solution.py:460
  10.6 151.2 %all-gather.6.cloned.1.call-start = ((), (), s32[]{:S(2)}) async-start(), calls=%async_computation.2 | async-start | bytes 4718592 | tf_op jit(solution)/shard_map/all_gather | solution.py:464
  11.8 363.8 %reduce-scatter.2.cloned.1.call-start = ((), (), s32[]{:S(2)}) async-start(), calls=%async_computation.3 | async-start | bytes 9052160 | tf_op jit(solution)/shard_map/reduce_scatter | solution.py:522
  20.0 68.1 %copy-start.48 = (f32[1024]{0:T(1024)S(1)}, f32[1024]{0:T(1024)}, u32[]{:S(2)}) copy-start(f32[1024]{0:T(1024)} %param.33) | copy-start | bytes 12292
  20.0 68.1 %copy-start.55 = (f32[1024]{0:T(1024)S(1)}, f32[1024]{0:T(1024)}, u32[]{:S(2)}) copy-start(f32[1024]{0:T(1024)} %param.34) | copy-start | bytes 12292
  117.7 3.1 collective-permute-start
  123.6 39.0 %copy-start.49 = (s32[1,1024,1]{1,2,0:T(1,128)S(1)}, s32[1,1024,1]{1,2,0:T(1,128)}, u32[]{:S(2)}) copy-start(s32[1,1024,1]{1,2,0:T(1,128)} %param.41) | copy-start | bytes 12292
  124.6 37.2 %collective-permute-start.1 = (bf16[640,1024]{1,0:T(8,128)(2,1)S(1)}, bf16[640,1024]{1,0:T(8,128)(2,1)}, u32[]{:S(2)}, u32[]{:S(2)}) collective-permute-start(bf16[640,1024]{1,0:T(8,128)(2,1)S(1)} %add_convert_fusion.1.rows), channel_id=1, source_target_pairs={{0,1},{1,0},{2,3},{3,2},{4,5},{5,4},{6,7},{7,6},{8,9},{9,8},{10,11... | collective-permute-start | bytes 3932168 | tf_op jit(solution)/shard_map/ppermute | solution.py:22
  161.8 7.5 %collective-permute-start.2 = (bf16[1024,2048]{1,0:T(8,128)(2,1)}, bf16[1024,2048]{1,0:T(8,128)(2,1)}, u32[]{:S(2)}, u32[]{:S(2)}) collective-permute-start(bf16[1024,2048]{1,0:T(8,128)(2,1)} %all-gather.6.cloned.1.call-done), channel_id=1, source_target_pairs={{0,2},{2,0},{1,3},{3,1},{4,6},{6,4},{5,7},{7,5},{8,10},{10,8},{9,1... | collective-permute-start | bytes 12582920 | tf_op jit(solution)/shard_map/ppermute | solution.py:22
  244.2 298.6 %all-gather.8.cloned.1.call-start = ((), (), s32[]{:S(2)}) async-start(), calls=%async_computation.4 | async-start | bytes 9052160 | tf_op jit(solution)/shard_map/all_gather | solution.py:633
  244.2 31.5 %collective-permute-start.4 = (bf16[640,1024]{1,0:T(8,128)(2,1)}, bf16[640,1024]{1,0:T(8,128)(2,1)S(1)}, u32[]{:S(2)}, u32[]{:S(2)}) collective-permute-start(bf16[640,1024]{1,0:T(8,128)(2,1)} %fusion.34), channel_id=1, source_target_pairs={{0,1},{1,0},{2,3},{3,2},{4,5},{5,4},{6,7},{7,6},{8,9},{9,8},{10,11... | collective-permute-start | bytes 3932168 | tf_op jit(solution)/shard_map/ppermute | solution.py:22
  284.5 3.2 collective-permute-start.5
  342.2 25.4 %collective-permute-start.14 = (bf16[128,32,128]{2,1,0:T(8,128)(2,1)}, bf16[128,32,128]{2,1,0:T(8,128)(2,1)}, u32[]{:S(2)}, u32[]{:S(2)}) collective-permute-start(bf16[128,32,128]{2,1,0:T(8,128)(2,1)} %slice.246), channel_id=1, source_target_pairs={{0,4},{4,0},{8,12},{12,8},{16,20},{20,16},{24,28},{28,24},{1,5},{5... | collective-permute-start | bytes 3145736 | tf_op jit(solution)/shard_map/ppermute | solution.py:593
  345.6 27.0 %collective-permute-start.12 = (bf16[136,32,128]{2,1,0:T(8,128)(2,1)}, bf16[136,32,128]{2,1,0:T(8,128)(2,1)}, u32[]{:S(2)}, u32[]{:S(2)}) collective-permute-start(bf16[136,32,128]{2,1,0:T(8,128)(2,1)} %slice.241), channel_id=1, source_target_pairs={{0,1},{1,0},{2,3},{3,2},{4,5},{5,4},{6,7},{7,6},{8,9},{9,8},{10,11... | collective-permute-start | bytes 3342344 | tf_op jit(solution)/shard_map/ppermute | solution.py:22
  369.8 22.8 %collective-permute-start.15 = (bf16[64,32,128]{2,1,0:T(8,128)(2,1)}, bf16[64,32,128]{2,1,0:T(8,128)(2,1)}, u32[]{:S(2)}, u32[]{:S(2)}) collective-permute-start(bf16[64,32,128]{2,1,0:T(8,128)(2,1)} %add_convert_fusion.3), channel_id=1, source_target_pairs={{0,1},{1,0},{2,3},{3,2},{4,5},{5,4},{6,7},{7,6},{8,9},{9,8},{10,11... | collective-permute-start | bytes 1572872 | tf_op jit(solution)/shard_map/ppermute | solution.py:22
  374.8 17.8 %collective-permute-start.13 = (bf16[68,32,128]{2,1,0:T(8,128)(2,1)}, bf16[68,32,128]{2,1,0:T(8,128)(2,1)}, u32[]{:S(2)}, u32[]{:S(2)}) collective-permute-start(bf16[68,32,128]{2,1,0:T(8,128)(2,1)} %add_convert_fusion.2), channel_id=1, source_target_pairs={{0,4},{4,0},{8,12},{12,8},{16,20},{20,16},{24,28},{28,24},{1,5},{5... | collective-permute-start | bytes 1671176 | tf_op jit(solution)/shard_map/ppermute | solution.py:593
  398.7 11.4 %collective-permute-start.6 = (bf16[640,1024]{1,0:T(8,128)(2,1)}, bf16[640,1024]{1,0:T(8,128)(2,1)}, u32[]{:S(2)}, u32[]{:S(2)}) collective-permute-start(bf16[640,1024]{1,0:T(8,128)(2,1)} %fusion.40), channel_id=1, source_target_pairs={{0,2},{2,0},{1,3},{3,1},{4,6},{6,4},{5,7},{7,5},{8,10},{10,8},{9,1... | collective-permute-start | bytes 3932168 | tf_op jit(solution)/shard_map/ppermute | solution.py:22
  408.2 31.9 %collective-permute-start.3 = (bf16[640,1024]{1,0:T(8,128)(2,1)}, bf16[640,1024]{1,0:T(8,128)(2,1)}, u32[]{:S(2)}, u32[]{:S(2)}) collective-permute-start(bf16[640,1024]{1,0:T(8,128)(2,1)} %fusion.37), channel_id=1, source_target_pairs={{0,1},{1,0},{2,3},{3,2},{4,5},{5,4},{6,7},{7,6},{8,9},{9,8},{10,11... | collective-permute-start | bytes 3932168 | tf_op jit(solution)/shard_map/ppermute | solution.py:22
  415.7 1.3 collective-permute-start.7
  417.0 29.4 %collective-permute-start.8 = (f32[80,128]{1,0:T(8,128)S(1)}, f32[80,128]{1,0:T(8,128)S(1)}, u32[]{:S(2)}, u32[]{:S(2)}) collective-permute-start(f32[80,128]{1,0:T(8,128)S(1)} %bitcast_add_fusion.1), channel_id=1, source_target_pairs={{0,1},{1,0},{2,3},{3,2},{4,5},{5,4},{6,7},{7,6},{8,9},{9,8},{10,11... | collective-permute-start | bytes 122888 | tf_op jit(solution)/shard_map/ppermute | solution.py:30
  421.0 26.7 %collective-permute-start.18 = (bf16[33,32,128]{2,1,0:T(8,128)(2,1)S(1)}, bf16[33,32,128]{2,1,0:T(8,128)(2,1)S(1)}, u32[]{:S(2)}, u32[]{:S(2)}) collective-permute-start(bf16[33,32,128]{2,1,0:T(8,128)(2,1)S(1)} %get-tuple-element.196), channel_id=1, source_target_pairs={{0,24},{4,28},{8,16},{12,20},{16,8},{20,12},{24,0},{28,4},{1,25},{... | collective-permute-start | bytes 811016 | tf_op jit(solution)/shard_map/ppermute | solution.py:593
  424.4 50.3 %collective-permute-start.17 = (bf16[33,32,128]{2,1,0:T(8,128)(2,1)S(1)}, bf16[33,32,128]{2,1,0:T(8,128)(2,1)S(1)}, u32[]{:S(2)}, u32[]{:S(2)}) collective-permute-start(bf16[33,32,128]{2,1,0:T(8,128)(2,1)S(1)} %get-tuple-element.197), channel_id=1, source_target_pairs={{0,16},{4,20},{8,24},{12,28},{16,0},{20,4},{24,8},{28,12},{1,17},{... | collective-permute-start | bytes 811016 | tf_op jit(solution)/shard_map/ppermute | solution.py:593
  424.4 50.3 %collective-permute-start.16 = (bf16[33,32,128]{2,1,0:T(8,128)(2,1)S(1)}, bf16[33,32,128]{2,1,0:T(8,128)(2,1)S(1)}, u32[]{:S(2)}, u32[]{:S(2)}) collective-permute-start(bf16[33,32,128]{2,1,0:T(8,128)(2,1)S(1)} %get-tuple-element.195), channel_id=1, source_target_pairs={{0,8},{4,12},{8,0},{12,4},{16,24},{20,28},{24,16},{28,20},{1,9},{5... | collective-permute-start | bytes 811016 | tf_op jit(solution)/shard_map/ppermute | solution.py:593
  446.4 38.6 %collective-permute-start.9 = (f32[80,128]{1,0:T(8,128)S(1)}, f32[80,128]{1,0:T(8,128)S(1)}, u32[]{:S(2)}, u32[]{:S(2)}) collective-permute-start(f32[80,128]{1,0:T(8,128)S(1)} %fusion.144), channel_id=1, source_target_pairs={{0,4},{4,0},{8,12},{12,8},{16,20},{20,16},{24,28},{28,24},{1,5},{5... | collective-permute-start | bytes 122888 | tf_op jit(solution)/shard_map/ppermute | solution.py:30
  485.0 13.6 %collective-permute-start.19 = (bf16[33,32,128]{2,1,0:T(8,128)(2,1)S(1)}, bf16[33,32,128]{2,1,0:T(8,128)(2,1)S(1)}, u32[]{:S(2)}, u32[]{:S(2)}) collective-permute-start(bf16[33,32,128]{2,1,0:T(8,128)(2,1)S(1)} %get-tuple-element.179), channel_id=1, source_target_pairs={{0,8},{4,12},{8,0},{12,4},{16,24},{20,28},{24,16},{28,20},{1,9},{5... | collective-permute-start | bytes 811016 | tf_op jit(solution)/shard_map/ppermute | solution.py:593
  485.0 13.6 %collective-permute-start.10 = (f32[80,128]{1,0:T(8,128)S(1)}, f32[80,128]{1,0:T(8,128)S(1)}, u32[]{:S(2)}, u32[]{:S(2)}) collective-permute-start(f32[80,128]{1,0:T(8,128)S(1)} %add.504), channel_id=1, source_target_pairs={{0,8},{4,12},{8,0},{12,4},{16,24},{20,28},{24,16},{28,20},{1,9},{5... | collective-permute-start | bytes 122888 | tf_op jit(solution)/shard_map/ppermute | solution.py:30
  487.1 17.4 %collective-permute-start.20 = (bf16[33,32,128]{2,1,0:T(8,128)(2,1)S(1)}, bf16[33,32,128]{2,1,0:T(8,128)(2,1)S(1)}, u32[]{:S(2)}, u32[]{:S(2)}) collective-permute-start(bf16[33,32,128]{2,1,0:T(8,128)(2,1)S(1)} %get-tuple-element.179), channel_id=1, source_target_pairs={{0,16},{4,20},{8,24},{12,28},{16,0},{20,4},{24,8},{28,12},{1,17},{... | collective-permute-start | bytes 811016 | tf_op jit(solution)/shard_map/ppermute | solution.py:593
  487.1 18.1 %collective-permute-start.21 = (bf16[33,32,128]{2,1,0:T(8,128)(2,1)S(1)}, bf16[33,32,128]{2,1,0:T(8,128)(2,1)S(1)}, u32[]{:S(2)}, u32[]{:S(2)}) collective-permute-start(bf16[33,32,128]{2,1,0:T(8,128)(2,1)S(1)} %get-tuple-element.179), channel_id=1, source_target_pairs={{0,24},{4,28},{8,16},{12,20},{16,8},{20,12},{24,0},{28,4},{1,25},{... | collective-permute-start | bytes 811016 | tf_op jit(solution)/shard_map/ppermute | solution.py:593
  498.5 22.6 %collective-permute-start.11 = (f32[80,128]{1,0:T(8,128)S(1)}, f32[80,128]{1,0:T(8,128)S(1)}, u32[]{:S(2)}, u32[]{:S(2)}) collective-permute-start(f32[80,128]{1,0:T(8,128)S(1)} %add.505), channel_id=1, source_target_pairs={{0,16},{4,20},{8,24},{12,28},{16,0},{20,4},{24,8},{28,12},{1,17},{... | collective-permute-start | bytes 122888 | tf_op jit(solution)/shard_map/ppermute | solution.py:30
  511.9 11.1 %collective-permute-start.22 = (bf16[64,32,128]{2,1,0:T(8,128)(2,1)}, bf16[64,32,128]{2,1,0:T(8,128)(2,1)S(1)}, u32[]{:S(2)}, u32[]{:S(2)}) collective-permute-start(bf16[64,32,128]{2,1,0:T(8,128)(2,1)} %get-tuple-element.59), channel_id=1, source_target_pairs={{0,4},{4,0},{8,12},{12,8},{16,20},{20,16},{24,28},{28,24},{1,5},{5... | collective-permute-start | bytes 1572872 | tf_op jit(solution)/shard_map/ppermute | solution.py:593
  523.9 16.7 %collective-permute-start.23 = (bf16[64,32,128]{2,1,0:T(8,128)(2,1)}, bf16[64,32,128]{2,1,0:T(8,128)(2,1)}, u32[]{:S(2)}, u32[]{:S(2)}) collective-permute-start(bf16[64,32,128]{2,1,0:T(8,128)(2,1)} %add.570.held), channel_id=1, source_target_pairs={{0,1},{1,0},{2,3},{3,2},{4,5},{5,4},{6,7},{7,6},{8,9},{9,8},{10,11... | collective-permute-start | bytes 1572872 | tf_op jit(solution)/shard_map/ppermute | solution.py:22
  (55 other events, 513.3 us)
Sparse Core Ops, SparseCore 0:
  10.7 77.3 all-gather.3
  90.8 70.9 all-gather.5
  244.3 103.8 reduce-scatter.1
  392.7 91.0 all-gather.7

commit v2 on v1

--- a/solution.py
+++ b/solution.py
@@ -7,11 +7,13 @@
 from jax.experimental.pallas import tpu as pltpu
 from jax.sharding import PartitionSpec as P
 
+
 HD = 64
 FF = 4096
 BUF = 64
 BS = 64
 LANES = 128
+SHARD, HEAD, TENSOR = "shard", "head", "tensor"
 F32 = jnp.float32
 BF16 = jnp.bfloat16
 
@@ -22,15 +24,21 @@
     return lax.ppermute(value, axis, [(0, 1), (1, 0)])
 
 
-def total_over_mesh(value):
-    for axis in ("head", "tensor", "shard"):
-        size = lax.axis_size(axis)
-        bit = 1
-        while bit < size:
-            partner = lax.ppermute(value, axis, [(i, i ^ bit) for i in range(size)])
-            value = value + partner
-            bit *= 2
-    return value
+def across(value, bits):
+    size = lax.axis_size(SHARD)
+    return lax.ppermute(value, SHARD, [(i, i ^ bits) for i in range(size)])
+
+
+def settle(*arrays):
+    anywhere = pl.BlockSpec(memory_space=pl.ANY)
+    return pl.pallas_call(
+        lambda *refs: None,
+        out_shape=tuple(jax.ShapeDtypeStruct(a.shape, a.dtype) for a in arrays),
+        in_specs=[anywhere] * len(arrays),
+        out_specs=(anywhere,) * len(arrays),
+        input_output_aliases={i: i for i in range(len(arrays))},
+        name="settle",
+    )(*arrays)
 
 
 def dot(left, right, contract):
@@ -51,29 +59,41 @@
     return (grad_in, jnp.sum(grad_out * normed, axis=0), jnp.sum(grad_out, axis=0))
 
 
-def masked_scores(rows, head, kept_valid, groups):
-    q = rows[:, head * HD : (head + 1) * HD]
-    k = rows[:, (groups + head) * HD : (groups + head + 1) * HD]
-    scores = dot(q, k, (1, 1)) * 0.125
-    return jnp.where(kept_valid, scores, -1000000000.0)
-
-
-def soft(scores):
-    shifted = jnp.exp(scores - jnp.max(scores, axis=-1, keepdims=True))
-    return shifted * (1.0 / jnp.sum(shifted, axis=-1, keepdims=True))
+def head_pair(rows, pair, which):
+    groups = rows.shape[1] // (3 * HD)
+    first = which * groups * HD + pair * LANES
+    return rows[:, first : first + LANES]
+
+
+def one_head_each(both):
+    first = lax.broadcasted_iota(jnp.int32, both.shape, 0) < HD
+    nothing = jnp.zeros_like(both)
+    return (jnp.where(first, both, nothing), jnp.where(first, nothing, both))
+
+
+def weights_of(keys, queries, valid):
+    scores = jnp.where(valid, dot(keys, queries, (1, 0)), -1000000000.0)
+    raised = jnp.exp(scores - jnp.max(scores, axis=0, keepdims=True))
+    return (raised, 1.0 / jnp.sum(raised, axis=0, keepdims=True))
+
+
+def key_mask(rows, count):
+    slots = rows.shape[0]
+    return lax.broadcasted_iota(jnp.int32, (slots, slots), 0) < BUF + count
 
 
 def attn_forward_body(kept, rows, out):
-    groups = rows.shape[1] // (3 * HD)
-    slots = rows.shape[0]
-    valid = lax.broadcasted_iota(jnp.int32, (slots, slots), 1) < BUF + kept[pl.program_id(0)]
-    for pair in range(groups // 2):
+    valid = key_mask(rows, kept[pl.program_id(0)])
+    for pair in range(rows.shape[1] // (6 * HD)):
+        queries = (head_pair(rows, pair, 0) * jnp.asarray(0.125, BF16)).T
+        keys = head_pair(rows, pair, 1)
+        values = head_pair(rows, pair, 2).T
         halves = []
-        for head in (2 * pair, 2 * pair + 1):
-            probs = soft(masked_scores(rows, head, valid, groups)).astype(BF16)
-            v = rows[:, (2 * groups + head) * HD : (2 * groups + head + 1) * HD]
-            halves.append(dot(probs, v, (1, 0)).astype(BF16))
-        out[:, pair * LANES : (pair + 1) * LANES] = jnp.concatenate(halves, axis=1)
+        for number, query in enumerate(one_head_each(queries)):
+            raised, scale = weights_of(keys, query, valid)
+            value = values[number * HD : (number + 1) * HD]
+            halves.append(dot(value, raised.astype(BF16), (1, 0)) * scale)
+        out[:, pair * LANES : (pair + 1) * LANES] = jnp.concatenate(halves).T.astype(BF16)
 
 
 def attn_forward(kept, rows, slots):
@@ -93,26 +113,30 @@
 
 
 def attn_backward_body(kept, rows, grads, out):
-    groups = rows.shape[1] // (3 * HD)
-    slots = rows.shape[0]
-    valid = lax.broadcasted_iota(jnp.int32, (slots, slots), 1) < BUF + kept[pl.program_id(0)]
-    for pair in range(groups // 2):
-        parts = ([], [], [])
-        for head in (2 * pair, 2 * pair + 1):
-            probs = soft(masked_scores(rows, head, valid, groups))
-            q = rows[:, head * HD : (head + 1) * HD]
-            k = rows[:, (groups + head) * HD : (groups + head + 1) * HD]
-            v = rows[:, (2 * groups + head) * HD : (2 * groups + head + 1) * HD]
-            g = grads[:, head * HD : (head + 1) * HD]
-            grad_probs = dot(g, v, (1, 1))
-            inner = jnp.sum(probs * grad_probs, axis=-1, keepdims=True)
+    valid = key_mask(rows, kept[pl.program_id(0)])
+    width = rows.shape[1] // 3
+    first = lax.broadcasted_iota(jnp.int32, (rows.shape[0], LANES), 1) < HD
+    for pair in range(width // LANES):
+        window = slice(pair * LANES, (pair + 1) * LANES)
+        queries = head_pair(rows, pair, 0) * jnp.asarray(0.125, BF16)
+        keys = head_pair(rows, pair, 1)
+        keys_t = keys.T
+        values = head_pair(rows, pair, 2)
+        grad = grads[:, window]
+        halves = ([], [], [])
+        for number, (query, grad_t) in enumerate(zip(one_head_each(queries.T), one_head_each(grad.T))):
+            raised, scale = weights_of(keys, query, valid)
+            probs = raised * scale
+            grad_probs = dot(values, grad_t, (1, 0))
+            inner = jnp.sum(probs * grad_probs, axis=0, keepdims=True)
             grad_scores = (probs * (grad_probs - inner)).astype(BF16)
-            parts[0].append((dot(grad_scores, k, (1, 0)) * 0.125).astype(BF16))
-            parts[1].append((dot(grad_scores, q, (0, 0)) * 0.125).astype(BF16))
-            parts[2].append(dot(probs.astype(BF16), g, (0, 0)).astype(BF16))
-        for which in range(3):
-            start = which * groups * HD + pair * LANES
-            out[:, start : start + LANES] = jnp.concatenate(parts[which], axis=1)
+            halves[0].append(dot(keys_t[number * HD : (number + 1) * HD], grad_scores, (1, 0)))
+            halves[1].append(dot(grad_scores, queries, (1, 0)))
+            halves[2].append(dot(probs.astype(BF16), grad, (1, 0)))
+        out[:, window] = (jnp.concatenate(halves[0]).T * 0.125).astype(BF16)
+        for which in (1, 2):
+            start = which * width + pair * LANES
+            out[:, start : start + LANES] = jnp.where(first, *halves[which]).astype(BF16)
 
 
 def attn_backward(kept, rows, grads, slots):
@@ -164,47 +188,81 @@
     return value * top / bottom
 
 
-def feed_body(rows, cot, up, down_t, bias, *refs):
-    hidden, grad_pre, bias_sum = refs[-3:]
-    pre = dot(rows[...], up[...], (1, 0)) + bias[...]
-    grad_hidden = dot(cot[...], down_t[...], (1, 0))
-    cdf = 0.5 + 0.5 * erf(pre * 0.7071067811865476)
-    density = 0.3989422804014327 * jnp.exp(-0.5 * pre * pre)
-    hidden[...] = (pre * cdf).astype(BF16)
-    grad = (grad_hidden * (cdf + pre * density)).astype(BF16)
-    grad_pre[...] = grad
-
-    @pl.when(pl.program_id(1) == 0)
+COL_CHUNK = 256
+
+
+def feed_body(flag, rows, cot, mine, other, bias, *refs):
+    hidden, grad_pre, bias_sum, grad_rows, up, down_t, total = refs[-7:]
+    step = pl.program_id(0)
+    for swapped in (False, True):
+
+        @pl.when((flag[0] != 0) == swapped)
+        def _():
+            up[...] = other[...] if swapped else mine[...]
+            down_t[...] = mine[...] if swapped else other[...]
+
+    part = None
+    for start in range(0, up.shape[1], COL_CHUNK):
+        window = slice(start, start + COL_CHUNK)
+        pre = dot(rows[...], up[:, window], (1, 0)) + bias[:, window]
+        grad_hidden = dot(cot[...], down_t[:, window], (1, 0))
+        cdf = 0.5 + 0.5 * erf(pre * 0.7071067811865476)
+        density = 0.3989422804014327 * jnp.exp(-0.5 * pre * pre)
+        hidden[:, window] = (pre * cdf).astype(BF16)
+        grad = (grad_hidden * (cdf + pre * density)).astype(BF16)
+        grad_pre[:, window] = grad
+        bias_sum[:, window] = jnp.sum(grad.astype(F32), axis=0, keepdims=True)
+        back = dot(grad, up[:, window], (1, 1))
+        part = back if part is None else part + back
+
+    @pl.when(step == 0)
     def _():
-        bias_sum[...] = jnp.zeros(bias_sum.shape, F32)
-
-    bias_sum[...] += jnp.sum(grad.astype(F32), axis=0, keepdims=True)
-
-
-def feed(rows, cot, up, down_t, bias, half, held, row_block, col_block):
+        total[...] = part
+
+    @pl.when(step > 0)
+    def _():
+        total[...] += part
+
+    @pl.when(step == pl.num_programs(0) - 1)
+    def _():
+        grad_rows[...] = total[...].astype(grad_rows.dtype)
+
+
+def feed(flag, rows, cot, mine, other, bias, half, held, col_block, grad_type):
     count, features = rows.shape
-    width = up.shape[1]
-    steps = count // row_block
-    first = half * steps
+    width = mine.shape[1]
     whole = jax.ShapeDtypeStruct((2 * count, width), BF16)
-    big = pl.BlockSpec((row_block, col_block), lambda j, i: (first + i, j))
+    big = pl.BlockSpec((count, col_block), lambda j: (half, j))
+    weight = pl.BlockSpec((features, col_block), lambda j: (0, j))
+    line = pl.BlockSpec((1, col_block), lambda j: (0, j))
     passed = [pl.BlockSpec(memory_space=pl.ANY) for _ in held]
     return pl.pallas_call(
         feed_body,
-        out_shape=(whole, whole, jax.ShapeDtypeStruct((1, width), F32)),
-        grid=(width // col_block, steps),
+        out_shape=(
+            whole,
+            whole,
+            jax.ShapeDtypeStruct((1, width), F32),
+            jax.ShapeDtypeStruct((count, features), grad_type),
+        ),
+        grid=(width // col_block,),
         in_specs=[
-            pl.BlockSpec((row_block, features), lambda j, i: (i, 0)),
-            pl.BlockSpec((row_block, features), lambda j, i: (first + i, 0)),
-            pl.BlockSpec((features, col_block), lambda j, i: (0, j)),
-            pl.BlockSpec((features, col_block), lambda j, i: (0, j)),
-            pl.BlockSpec((1, col_block), lambda j, i: (0, j)),
+            pl.BlockSpec(memory_space=pltpu.SMEM),
+            pl.BlockSpec((count, features), lambda j: (0, 0)),
+            pl.BlockSpec((count, features), lambda j: (half, 0)),
+            weight,
+            weight,
+            line,
             *passed,
         ],
-        out_specs=(big, big, pl.BlockSpec((1, col_block), lambda j, i: (0, j))),
-        input_output_aliases={5: 0, 6: 1} if held else {},
+        out_specs=(big, big, line, pl.BlockSpec((count, features), lambda j: (0, 0))),
+        scratch_shapes=[
+            pltpu.VMEM((features, col_block), BF16),
+            pltpu.VMEM((features, col_block), BF16),
+            pltpu.VMEM((count, features), F32),
+        ],
+        input_output_aliases={6: 0, 7: 1} if held else {},
         name="feed",
-    )(rows, cot, up, down_t, bias, *held)
+    )(flag, rows, cot, mine, other, bias, *held)
 
 
 def slot_numbers(owner_list, capacity, owners):
@@ -393,6 +451,26 @@
         out_specs=tuple(whole for _ in shapes),
         name="from_slots",
     )(slots, place, held)
+
+
+def add_up_body(*refs):
+    *inputs, out = refs
+    total = inputs[0][...].astype(F32)
+    for source in inputs[1:]:
+        total += source[...].astype(F32)
+    out[:, : BS // 2, :] = total[:, :, :BS]
+    out[:, BS // 2 :, :] = total[:, :, BS:]
+
+
+def add_up(first, others):
+    whole = pl.BlockSpec(memory_space=pltpu.VMEM)
+    return pl.pallas_call(
+        add_up_body,
+        out_shape=jax.ShapeDtypeStruct((first.shape[0], BS, BS), F32),
+        in_specs=[whole] * (1 + len(others)),
+        out_specs=whole,
+        name="add_up",
+    )(first, *others)
 
 
 def unpack(dense):
@@ -449,22 +527,38 @@
     mlp_second,
     mlp_master,
 ):
-    head_pos = lax.axis_index("head")
-    tensor_pos = lax.axis_index("tensor")
-    shard_pos = lax.axis_index("shard")
+    head_pos = lax.axis_index(HEAD)
+    tensor_pos = lax.axis_index(TENSOR)
+    shard_pos = lax.axis_index(SHARD)
     local_images, slot_count, features = tokens.shape
     per_out = local_images // 4
     own_rows = per_out * slot_count
 
+    group_cols = w_qkv.shape[2]
     attn_mine = jnp.concatenate([w_qkv[0], w_qkv[1], w_qkv[2], w_out.T], axis=1)
-    attn_full = lax.all_gather(attn_mine, "shard", axis=0, tiled=True)
-    group_cols = w_qkv.shape[2]
-    qkv_full = attn_full[:, : 3 * group_cols]
-    out_full_t = attn_full[:, 3 * group_cols :]
+    if lax.axis_size(TENSOR) == 2 and attn_mine.shape[0] % 32 == 0:
+        half_rows = attn_mine.shape[0] // 2
+        attn_half = lax.dynamic_slice_in_dim(attn_mine, tensor_pos * half_rows, half_rows, 0)
+        attn_half = lax.all_gather(attn_half, SHARD, axis=0)
+        first = tensor_pos == 0
+
+        def both_halves(held):
+            other = swap(held, TENSOR)
+            parts = [jnp.where(first, held, other), jnp.where(first, other, held)]
+            return jnp.stack(parts, axis=1).reshape(features, held.shape[2])
+
+        qkv_full = both_halves(attn_half[:, :, : 3 * group_cols])
+        out_full_t = both_halves(after(attn_half[:, :, 3 * group_cols :], qkv_full))
+    else:
+        attn_full = lax.all_gather(attn_mine, SHARD, axis=0, tiled=True)
+        qkv_full = attn_full[:, : 3 * group_cols]
+        out_full_t = attn_full[:, 3 * group_cols :]
     mlp_mine = lax.all_gather(
-        jnp.where(head_pos == 0, w_up, w_down.T), "shard", axis=0, tiled=True
+        after(jnp.where(head_pos == 0, w_up, w_down.T), attn_mine), SHARD, axis=0, tiled=True
     )
     hidden_cols = mlp_mine.shape[1]
+    mlp_state = settle(mlp_left[0], mlp_right[0], mlp_first[0], mlp_second[0], mlp_master[0])
+    qkv_full = after(qkv_full, *mlp_state)
 
     def images_of(array, start):
         return lax.dynamic_slice_in_dim(array, start * per_out, per_out, 0)
@@ -489,42 +583,33 @@
     projected = dot(low_one, qkv_full, (1, 0)).astype(BF16)
     heads_out = attn_forward(attn_kept, projected, slot_count)
     pair_branch = dot(heads_out[own_rows:], out_full_t, (1, 1)).astype(BF16)
-    branch_in = swap(pair_branch, "head")
+    branch_in = swap(pair_branch, HEAD)
     own_branch = dot(heads_out[:own_rows], out_full_t, (1, 1))
     residual = attn_tokens[:own_rows].astype(F32) + (own_branch + branch_in.astype(F32)) + out_bias
     normed_two, inv_two = norm_parts(residual)
     low_two = (normed_two * ln2_gain + ln2_bias).astype(BF16)
 
-    low_in = swap(low_two, "tensor")
-    mlp_mine = after(mlp_mine, low_in)
-    mlp_other = swap(mlp_mine, "head")
-    up_full = jnp.where(head_pos == 0, mlp_mine, mlp_other)
-    down_full_t = jnp.where(head_pos == 0, mlp_other, mlp_mine)
+    low_in = swap(low_two, TENSOR)
+    mlp_mine = after(mlp_mine, low_two)
+    mlp_other = swap(mlp_mine, HEAD)
+    flag = head_pos.reshape(1).astype(jnp.int32)
     up_local = lax.dynamic_slice_in_dim(up_bias, tensor_pos * hidden_cols, hidden_cols, 0)[None]
-    hidden_half, pre_half, pair_sum = feed(
-        low_in, mlp_cot, up_full, down_full_t, up_local, 1, (), slot_count, 512
-    )
-    pair_normed = dot(pre_half[own_rows:], up_full, (1, 1)).astype(BF16)
-    normed_in = swap(pair_normed, "tensor")
-    hidden, grad_pre, own_sum = feed(
-        low_two, mlp_cot, up_full, down_full_t, up_local, 0,
-        (hidden_half, after(pre_half, pair_normed)), slot_count, 512,
-    )
+    hidden, grad_pre, own_sum, own_grad_normed = feed(
+        flag, low_two, mlp_cot, mlp_mine, mlp_other, up_local, 0, (), 512, F32
+    )
+    hidden, grad_pre, pair_sum, pair_normed = feed(
+        flag, low_in, mlp_cot, mlp_mine, mlp_other, up_local, 1, (hidden, grad_pre), 512, BF16
+    )
+    normed_in = swap(pair_normed, TENSOR)
     up_bias_part = pair_sum + own_sum
-    own_grad_normed = dot(grad_pre[:own_rows], up_full, (1, 1))
     normed_rows = jnp.concatenate([low_two, low_in])
     up_grad = dot(normed_rows, grad_pre, (0, 0)).astype(BF16)
     down_grad = dot(hidden, mlp_cot, (0, 0)).astype(BF16)
-    mlp_owners = lax.axis_size(("shard", "head"))
+    mlp_owners = lax.axis_size((SHARD, HEAD))
     mlp_cap = mlp_master.shape[1]
     mlp_slots = slot_numbers(mlp_owner[0, :, 0], mlp_cap, mlp_owners)
     mlp_parts = mlp_parcel(mlp_slots, mlp_owners * mlp_cap, up_grad, down_grad)
-    mlp_sum = lax.psum_scatter(mlp_parts, ("shard", "head"), scatter_dimension=0, tiled=True)
-    pair_mlp = dot(hidden[own_rows:], down_full_t, (1, 1)).astype(BF16)
-    mlp_in = swap(pair_mlp, "tensor")
-    own_mlp = dot(hidden[:own_rows], down_full_t, (1, 1))
-    mlp_out = own_mlp + mlp_in.astype(F32) + down_bias
-    out = (own_valid * (residual + mlp_out)).astype(BF16)
+    mlp_sum = lax.psum_scatter(mlp_parts, (SHARD, HEAD), scatter_dimension=0, tiled=True)
     resid_from, ln2_gain_part, ln2_bias_part = norm_back(
         own_grad_normed + normed_in.astype(F32), normed_two, inv_two, ln2_gain
     )
@@ -533,14 +618,14 @@
     grad_branch = grad_resid.astype(BF16)
     out_bias_part = jnp.sum(grad_branch.astype(F32), axis=0)
 
-    branch_rows = jnp.concatenate([grad_branch, after(swap(grad_branch, "head"), mlp_parts)])
+    branch_rows = jnp.concatenate([grad_branch, after(swap(grad_branch, HEAD), mlp_parts)])
     grad_heads = dot(branch_rows, out_full_t, (1, 0)).astype(BF16)
     grad_proj = attn_backward(attn_kept, projected, grad_heads, slot_count)
     out_grad = dot(heads_out, branch_rows, (0, 0)).astype(BF16)
     qkv_grad = dot(low_one, grad_proj, (0, 0)).astype(BF16)
     pair_input = dot(grad_proj[own_rows:], qkv_full, (1, 1)).astype(BF16)
-    input_in = swap(pair_input, "head")
-    own_input = dot(grad_proj[:own_rows], qkv_full, (1, 1))
+    input_in = swap(pair_input, HEAD)
+    own_input = lax.optimization_barrier(dot(grad_proj[:own_rows], qkv_full, (1, 1)))
     tokens_from, ln1_gain_part, ln1_bias_part = norm_back(
         own_input + input_in.astype(F32), normed_one[:own_rows], inv_one[:own_rows], ln1_gain
     )
@@ -560,14 +645,23 @@
             up_whole,
         ]
     ).reshape(-1, LANES)
-    small = total_over_mesh(small).reshape(-1)
-    small_sums = [small[i * features : (i + 1) * features] for i in range(6)] + [small[6 * features :]]
+
+    def mlp_output(pair_mlp):
+        mlp_in = swap(pair_mlp, TENSOR)
+        own_mlp = dot(hidden[:own_rows], down_full_t, (1, 1))
+        mlp_out = own_mlp + mlp_in.astype(F32) + down_bias
+        return (own_valid * (residual + mlp_out)).astype(BF16)
+
+    hidden, down_full_t = lax.optimization_barrier(
+        (hidden, jnp.where(head_pos == 0, mlp_other, mlp_mine), grad_proj)
+    )[:2]
+    pair_mlp = dot(hidden[own_rows:], down_full_t, (1, 1)).astype(BF16)
 
     place = shard_pos.reshape(1).astype(jnp.int32)
     rows = features // BS
 
-    shards = lax.axis_size("shard")
-    tensors = lax.axis_size("tensor")
+    shards = lax.axis_size(SHARD)
+    tensors = lax.axis_size(TENSOR)
     attn_owners = shards * tensors
     attn_cap = attn_master.shape[1]
     attn_total = attn_owners * attn_cap
@@ -589,67 +683,79 @@
         )
         parts = attn_parcel(spot, attn_total, qkv_grad, out_grad)
 
-        def across(value, bits):
-            return lax.ppermute(value, "shard", [(i, i ^ bits) for i in range(shards)])
-
-        def so_far(which, first, count, arrived):
-            size = columns * sizes[which]
-            begin = which * start
-            total = parts[begin + first * size : begin + first * size + count].astype(F32)
+        def so_far(which, begin, count, arrived):
+            total = parts[which * start + begin : which * start + begin + count].astype(F32)
             for array in arrived:
-                total = total + array[first * size : first * size + count].astype(F32)
+                total = total + array[begin : begin + count].astype(F32)
             return total
 
         spans = [columns * size for size in sizes]
-        first_a = swap(parts[2 * spans[0] : 4 * spans[0]], "tensor")
+        first_a = swap(parts[2 * spans[0] : 4 * spans[0]], TENSOR)
         first_b = across(parts[start + 2 * spans[1] : start + 4 * spans[1]], 1)
-        next_a = so_far(0, 1, spans[0], (first_a,)).astype(BF16)
-        next_b = so_far(1, 1, spans[1], (first_b,)).astype(BF16)
-        mlp_sum = after(mlp_sum, next_a, next_b)
+        next_a = so_far(0, spans[0], spans[0], (first_a,)).astype(BF16)
+        next_b = so_far(1, spans[1], spans[1], (first_b,)).astype(BF16)
         second_a = across(next_a, 1)
-        second_b = swap(next_b, "tensor")
-        sums = jnp.concatenate(
-            [
-                so_far(0, 0, spans[0], (first_a, second_a)).reshape(columns, sizes[0], BS // 2, LANES),
-                so_far(1, 0, spans[1], (first_b, second_b)).reshape(columns, sizes[1], BS // 2, LANES),
-            ],
-            axis=1,
-        )
-        attn_sum = sums[0]
+        second_b = swap(next_b, TENSOR)
+        second_a = after(second_a, tokens_grad)
+        sums = [
+            jnp.concatenate(
+                [
+                    so_far(0, step * sizes[0], sizes[0], (first_a, second_a)),
+                    so_far(1, step * sizes[1], sizes[1], (first_b, second_b)),
+                ]
+            )
+            for step in range(columns)
+        ]
+        arrived = []
         for step in range(1, columns):
-            attn_sum = attn_sum + across(sums[step].astype(BF16), 2 * step).astype(F32)
+            arrived.append(across(sums[step].astype(BF16), 2 * step))
+        pair_mlp = after(pair_mlp, *sums)
+        mlp_sum = after(mlp_sum, *sums)
     else:
         parts = attn_parcel(attn_slots, attn_total, qkv_grad, out_grad)
-        attn_sum = lax.psum_scatter(parts, ("shard", "tensor"), scatter_dimension=0, tiled=True)
-    attn_sum = unpack(attn_sum).astype(F32)
+        attn_sum = lax.psum_scatter(parts, (SHARD, TENSOR), scatter_dimension=0, tiled=True)
+        attn_sum = unpack(attn_sum).astype(F32)
+
     mlp_sum = unpack(mlp_sum).astype(F32)
-
-    mlp_first_new, mlp_second_new, mlp_master_new = soap_update(
-        mlp_sum, mlp_left[0], mlp_right[0], mlp_first[0], mlp_second[0], mlp_master[0]
-    )
+    mlp_first_new, mlp_second_new, mlp_master_new = soap_update(mlp_sum, *mlp_state)
     mlp_dense = pack(mlp_master_new.astype(BF16))
+    mlp_all = lax.all_gather(mlp_dense, (SHARD, HEAD), axis=0, tiled=True)
+
     if direct:
-        mlp_dense = after(mlp_dense, second_a, second_b)
-    mlp_all = lax.all_gather(mlp_dense, ("shard", "head"), axis=0, tiled=True)
-    mlp_outs = lax.optimization_barrier(
-        tuple(jnp.transpose(a, (1, 2, 0)) for a in (mlp_sum, mlp_first_new, mlp_second_new, mlp_master_new))
-    )
+        arrived = lax.optimization_barrier((*arrived, mlp_dense))[:-1]
+        attn_sum = add_up(sums[0], arrived)
+    out = mlp_output(pair_mlp)
     attn_first_new, attn_second_new, attn_master_new = soap_update(
         attn_sum, attn_left[0], attn_right[0], attn_first[0], attn_second[0], attn_master[0]
     )
     attn_dense = pack(attn_master_new.astype(BF16))
+    mlp_news = settle(mlp_sum, mlp_first_new, mlp_second_new, mlp_master_new)
+    mlp_news = lax.optimization_barrier((*mlp_news, attn_dense))[:-1]
+    mlp_outs = settle(*(jnp.transpose(a, (1, 2, 0)) for a in mlp_news))
+    small = after(small, attn_dense)
+    small = small + swap(small, HEAD)
+    small = small + swap(small, TENSOR)
 
     own = w_qkv.shape[1]
     if direct:
-        column = [attn_dense] + [across(attn_dense, 2 * step) for step in range(1, columns)]
+        column = [attn_dense]
+        for step in range(1, columns):
+            column.append(across(attn_dense, 2 * step))
         empty = jnp.zeros((1,) + attn_dense.shape[1:], BF16)
         here = (off_tensor == 0) & (bit == 0)
         where = jnp.where(here, high * attn_cap + inner, columns * attn_cap)
         lists = [local_blocks(p, rows, group_cols // BS, own // BS) for p in (shard_pos, shard_pos ^ 1)]
         table = jnp.take(where, jnp.concatenate(lists), axis=0)
-        mine, theirs = pick(after(table, *mlp_outs), jnp.concatenate(column + [empty]), 2)
-        mine = mine + across(theirs, 1)
-        w_qkv_new, w_out_new = attn_finish(mine, swap(mine, "tensor"), (w_qkv.shape, w_out.shape))
+        table = after(table, *mlp_outs, small, out, tokens_grad)
+        mine, theirs = pick(table, jnp.concatenate(column + [empty]), 2)
+        small = after(small, theirs)
+        small = small + across(small, 2)
+        small = small + across(small, 4)
+        mine = after(mine + across(theirs, 1), small)
+        small = small + across(small, 1)
+        w_qkv_new, w_out_new = attn_finish(
+            after(mine, small), swap(mine, TENSOR), (w_qkv.shape, w_out.shape)
+        )
         w_up_new, w_down_new = from_slots(
             partial(mlp_return_body, rows, hidden_cols // BS),
             mlp_slots,
@@ -658,7 +764,11 @@
             (w_up.shape, w_down.shape),
         )
     else:
-        attn_all = lax.all_gather(attn_dense, ("shard", "tensor"), axis=0, tiled=True)
+        bit = 1
+        while bit < shards:
+            small = small + across(small, bit)
+            bit *= 2
+        attn_all = lax.all_gather(attn_dense, (SHARD, TENSOR), axis=0, tiled=True)
         attn_new = unpack(jnp.take(attn_all, attn_slots, axis=0))
         qkv_count = 3 * rows * (group_cols // BS)
         new_qkv = join_blocks(attn_new[:qkv_count], (3,), features, group_cols)
@@ -671,6 +781,9 @@
         new_down = join_blocks(mlp_new[up_count:], (), hidden_cols, features)
         w_up_new = lax.dynamic_slice_in_dim(new_up, shard_pos * own, own, 0)
         w_down_new = lax.dynamic_slice_in_dim(new_down, shard_pos * own, own, 1)
+
+    small = small.reshape(-1)
+    small_sums = [small[i * features : (i + 1) * features] for i in range(6)] + [small[6 * features :]]
 
     return (
         out.reshape(per_out, slot_count, features),
@@ -690,13 +803,13 @@
 
 def solution(mesh):
     placed = (
-        P("shard", None, None),
-        P("shard"),
-        P(("shard", "head"), None, None),
-        P(None, "shard", "head"),
-        P("head", "shard"),
-        P("shard", "tensor"),
-        P("tensor", "shard"),
+        P(SHARD, None, None),
+        P(SHARD),
+        P((SHARD, HEAD), None, None),
+        P(None, SHARD, HEAD),
+        P(HEAD, SHARD),
+        P(SHARD, TENSOR),
+        P(TENSOR, SHARD),
         P(),
         P(),
         P(),
@@ -704,26 +817,26 @@
         P(),
         P(),
         P(),
-        P("head", None, None),
-        P("tensor", None, None),
-        P("head", ("shard", "tensor"), None, None),
-        P("head", ("shard", "tensor"), None, None),
-        P("head", ("shard", "tensor"), None, None),
-        P("head", ("shard", "tensor"), None, None),
-        P("head", ("shard", "tensor"), None, None),
-        P("tensor", ("shard", "head"), None, None),
-        P("tensor", ("shard", "head"), None, None),
-        P("tensor", ("shard", "head"), None, None),
-        P("tensor", ("shard", "head"), None, None),
-        P("tensor", ("shard", "head"), None, None),
+        P(HEAD, None, None),
+        P(TENSOR, None, None),
+        P(HEAD, (SHARD, TENSOR), None, None),
+        P(HEAD, (SHARD, TENSOR), None, None),
+        P(HEAD, (SHARD, TENSOR), None, None),
+        P(HEAD, (SHARD, TENSOR), None, None),
+        P(HEAD, (SHARD, TENSOR), None, None),
+        P(TENSOR, (SHARD, HEAD), None, None),
+        P(TENSOR, (SHARD, HEAD), None, None),
+        P(TENSOR, (SHARD, HEAD), None, None),
+        P(TENSOR, (SHARD, HEAD), None, None),
+        P(TENSOR, (SHARD, HEAD), None, None),
     )
     return jax.shard_map(
         per_device,
         mesh=mesh,
         in_specs=placed,
         out_specs=(
-            P(("shard", "head", "tensor"), None, None),
-            P(("shard", "head", "tensor"), None, None),
+            P((SHARD, HEAD, TENSOR), None, None),
+            P((SHARD, HEAD, TENSOR), None, None),
             P(),
             P(),
             P(),
@@ -731,18 +844,18 @@
             P(),
             P(),
             P(),
-            P("head", ("shard", "tensor"), None, None),
-            P("head", ("shard", "tensor"), None, None),
-            P("head", ("shard", "tensor"), None, None),
-            P("head", ("shard", "tensor"), None, None),
-            P("tensor", ("shard", "head"), None, None),
-            P("tensor", ("shard", "head"), None, None),
-            P("tensor", ("shard", "head"), None, None),
-            P("tensor", ("shard", "head"), None, None),
-            P(None, "shard", "head"),
-            P("head", "shard"),
-            P("shard", "tensor"),
-            P("tensor", "shard"),
+            P(HEAD, (SHARD, TENSOR), None, None),
+            P(HEAD, (SHARD, TENSOR), None, None),
+            P(HEAD, (SHARD, TENSOR), None, None),
+            P(HEAD, (SHARD, TENSOR), None, None),
+            P(TENSOR, (SHARD, HEAD), None, None),
+            P(TENSOR, (SHARD, HEAD), None, None),
+            P(TENSOR, (SHARD, HEAD), None, None),
+            P(TENSOR, (SHARD, HEAD), None, None),
+            P(None, SHARD, HEAD),
+            P(HEAD, SHARD),
+            P(SHARD, TENSOR),
+            P(TENSOR, SHARD),
         ),
         check_vma=False,
     )

time: 563 us -> 543 us (0.964)
  the two profiles are of different devices: /device:TPU:0 before, /device:TPU:8 now
where the time goes in v2:
time: 543 us; the launch traced here: 533 us
  waiting for transfers between devices  181 us (33%)
  Pallas kernels  107 us (20%)
  matrix products  88.2 us (16%)
  local copies, waits for them, and re-layouts  69.5 us (13%)
  other arithmetic  46.1 us (8%)
  starting transfers between devices  25.6 us (5%)
  between operations  14.9 us (3%)
    ppermute x12, waiting for transfers between devices, across(): return lax.ppermute(value, SHARD, [(i, i ^ bits) for i in range(size)])  78.9 us
    dot_general x14, matrix products, dot(): lax.dot_general(left, right, ((contract[:1], contract[1:]), ((), ())), pr...  64.2 us
    ppermute x14, waiting for transfers between devices, swap(): return lax.ppermute(value, axis, [(0, 1), (1, 0)])  53.9 us
    all_gather x1, waiting for transfers between devices, per_device(): attn_half = lax.all_gather(attn_half, SHARD, axis=0)  46.1 us
    pallas_call x2, Pallas kernels, feed(): pl.pallas_call(feed_body, out_shape=(whole, whole, jax.ShapeDtypeStruct((...  42 us
    unnamed x144, local copies, waits for them, and re-layouts  35.5 us
    pallas_call x1, Pallas kernels, attn_backward(): pl.pallas_call(attn_backward_body, out_shape=jax.ShapeDtypeStruct(rows.sh...  22.4 us
    pallas_call x2, Pallas kernels, to_parcel(): pl.pallas_call(partial(to_parcel_body, indices_of), out_shape=jax.ShapeDt...  17.2 us
  transfers between devices with their start and end apart: 30, of which 18 were waited for; matrix products, arithmetic and copies ran while one was open for 29% of the time, Pallas kernels for 13%

profile of v2, /device:TPU:8, one launch (start us, length us, event | category | flops | bytes accessed | tf_op | source)
XLA Modules:
  0.0 532.9 jit_solution(6076494874700731297)
XLA Ops:
  15.0 46.1 %all-gather.9.cloned.1.call-done = bf16[512,2048]{1,0:T(8,128)(2,1)} async-done(((bf16[64,2048]{1,0:T(8,128)(2,1)}), bf16[512,2048]{1,0:T(8,128)(2,1)}) %all-gather.9.cloned.1.call-update) | async-done | bytes 2097168 | tf_op jit(solution)/shard_map/all_gather | solution.py:542
  70.2 4.0 copy.109
  82.0 4.0 copy.112
  90.6 8.6 %collective-permute-done = bf16[8,64,1536]{2,1,0:T(8,128)(2,1)} collective-permute-done((bf16[8,64,1536]{2,1,0:T(8,128)(2,1)}, bf16[8,64,1536]{2,1,0:T(8,128)(2,1)}, u32[]{:S(2)}, u32[]{:S(2)}) %collective-permute-start) | collective-permute-done | bytes 1572896 | tf_op jit(solution)/shard_map/ppermute | solution.py:24
  103.0 5.7 %convolution_convert_fusion.rows = bf16[1280,1536]{1,0:T(8,128)(2,1)} fusion(bf16[1024,1536]{1,0:T(8,128)(2,1)S(1)} %bitcast.155, f32[1280,1024]{1,0:T(8,128)S(1)} %fusion, f32[1024]{0:T(1024)S(1)} %copy-done.58, f32[1024]{0:T(1024)S(1)} %copy-done.49), kind=kOutput, calls=%fused_computation.1 | convolution fusion | flops 4032430080 | bytes 12328960 | tf_op jit(solution)/shard_map/dot_general | solution.py:45
  108.7 14.3 %attn_forward.1 = bf16[1280,512]{1,0:T(8,128)(2,1)} custom-call(s32[4]{0:T(128)} %get-tuple-element.178.kept, bf16[1280,1536]{1,0:T(8,128)(2,1)} %convolution_convert_fusion.rows), custom_call_target="tpu_custom_call" | custom-call | tf_op jit(solution)/shard_map/attn_forward/pallas_call | solution.py:102
  143.2 21.1 %feed.2 = (bf16[1280,2048]{1,0:T(8,128)(2,1)}, bf16[1280,2048]{1,0:T(8,128)(2,1)}, f32[1,2048]{1,0:T(1,128)}, f32[640,1024]{1,0:T(8,128)}) custom-call(s32[1]{0:T(128)} %bitcast.18.flag, bf16[640,1024]{1,0:T(8,128)(2,1)} %add_convert_fusion.1.rows, bf16[1280,1024]{1,0:T(8,128)(2,1)} %bitcast_select_fusion.cot, ...), custom_call_target="tpu_custom_call" | custom-call | tf_op jit(solution)/shard_map/feed/pallas_call | solution.py:239
  166.3 20.9 %feed.3 = (bf16[1280,2048]{1,0:T(8,128)(2,1)}, bf16[1280,2048]{1,0:T(8,128)(2,1)}, f32[1,2048]{1,0:T(1,128)}, bf16[640,1024]{1,0:T(8,128)(2,1)}) custom-call(s32[1]{0:T(128)} %bitcast.18.flag, bf16[640,1024]{1,0:T(8,128)(2,1)} %collective-permute-done.3.rows, ...), custom_call_target="tpu_custom_call", output_to_operand_aliasing={{0}: (6, {}), {1}: (7, {})} | custom-call | tf_op jit(solution)/shard_map/feed/pallas_call | solution.py:239
  187.2 10.3 %convolution_convert_fusion.1.refs_1_ = bf16[2048,1024]{1,0:T(8,128)(2,1)} fusion(bf16[1280,2048]{1,0:T(8,128)(2,1)} %get-tuple-element.86, bf16[1280,1024]{1,0:T(8,128)(2,1)} %bitcast_select_fusion.cot), kind=kOutput, calls=%fused_computation.9 | convolution fusion | flops 5370806272 | bytes 12058624 | tf_op jit(solution)/shard_map/dot_general | solution.py:45
  197.5 9.1 %convolution_convert_fusion.2.refs_0_ = bf16[1024,2048]{1,0:T(8,128)(2,1)} fusion(bf16[1280,2048]{1,0:T(8,128)(2,1)S(1)} %copy-done.19, bf16[640,1024]{1,0:T(8,128)(2,1)} %collective-permute-done.3.rows, bf16[640,1024]{1,0:T(8,128)(2,1)} %add_convert_fusion.1.rows), kind=kOutput, calls=%fused_computation.10 | convolution fusion | flops 5376049152 | bytes 12058624 | tf_op jit(solution)/shard_map/dot_general | solution.py:45
  206.6 10.3 %to_parcel.2 = bf16[1040,32,128]{2,1,0:T(8,128)(2,1)} custom-call(s32[1024]{0:T(1024)} %convert_add_fusion.11.slots, bf16[1024,2048]{1,0:T(8,128)(2,1)} %convolution_convert_fusion.2.refs_0_, bf16[2048,1024]{1,0:T(8,128)(2,1)} %convolution_convert_fusion.1.refs_1_), custom_call_target="tpu_custom_call" | custom-call | tf_op jit(solution)/shard_map/to_parcel/pallas_call | solution.py:307
  219.2 28.7 %collective-permute-done.5 = bf16[640,1024]{1,0:T(8,128)(2,1)S(1)} collective-permute-done((bf16[640,1024]{1,0:T(8,128)(2,1)}, bf16[640,1024]{1,0:T(8,128)(2,1)S(1)}, u32[]{:S(2)}, u32[]{:S(2)}) %collective-permute-start.5) | collective-permute-done | bytes 1310752 | tf_op jit(solution)/shard_map/ppermute | solution.py:24
  258.6 22.4 %attn_backward.1 = bf16[1280,1536]{1,0:T(8,128)(2,1)} custom-call(s32[4]{0:T(128)} %get-tuple-element.178.kept, bf16[1280,1536]{1,0:T(8,128)(2,1)} %convolution_convert_fusion.rows, bf16[1280,512]{1,0:T(8,128)(2,1)} %convolution_convert_fusion.4.grads), custom_call_target="tpu_custom_call" | custom-call | tf_op jit(solution)/shard_map/attn_backward/pallas_call | solution.py:145
  281.0 4.5 fusion.26.refs_1_
  285.4 8.4 %convolution_convert_fusion.3.refs_0_ = bf16[1024,1536]{1,0:T(8,128)(2,1)} fusion(bf16[1280,1536]{1,0:T(8,128)(2,1)S(1)} %copy-done.28, f32[1280,1024]{1,0:T(8,128)} %copy-done.5, f32[1024]{0:T(1024)S(1)} %copy-done.58, f32[1024]{0:T(1024)S(1)} %copy-done.49), kind=kOutput, calls=%fused_computation.11 | convolution fusion | flops 4032036864 | bytes 12328960 | tf_op jit(solution)/shard_map/dot_general | solution.py:45
  293.8 6.9 %to_parcel.3 = bf16[528,32,128]{2,1,0:T(8,128)(2,1)} custom-call(s32[512]{0:T(512)} %get-tuple-element.174.slots, bf16[1024,1536]{1,0:T(8,128)(2,1)} %convolution_convert_fusion.3.refs_0_, bf16[512,1024]{1,0:T(8,128)(2,1)} %fusion.26.refs_1_), custom_call_target="tpu_custom_call" | custom-call | tf_op jit(solution)/shard_map/to_parcel/pallas_call | solution.py:307
  307.9 5.2 fusion.23
  313.2 4.8 fusion.17
  317.9 14.4 %collective-permute-done.10 = bf16[128,32,128]{2,1,0:T(8,128)(2,1)} collective-permute-done((bf16[128,32,128]{2,1,0:T(8,128)(2,1)}, bf16[128,32,128]{2,1,0:T(8,128)(2,1)}, u32[]{:S(2)}, u32[]{:S(2)}) %collective-permute-start.10) | collective-permute-done | bytes 1048608 | tf_op jit(solution)/shard_map/ppermute | solution.py:29
  339.6 4.0 multiply_add_fusion.1
  358.5 4.7 fusion.10
  366.4 4.8 fusion.93
  380.0 4.0 fusion.20
  389.0 27.9 %collective-permute-done.15.refs_3_ = bf16[33,32,128]{2,1,0:T(8,128)(2,1)S(1)} collective-permute-done((bf16[33,32,128]{2,1,0:T(8,128)(2,1)S(1)}, bf16[33,32,128]{2,1,0:T(8,128)(2,1)S(1)}, u32[]{:S(2)}, u32[]{:S(2)}) %collective-permute-start.15) | collective-permute-done | bytes 270368 | tf_op jit(solution)/shard_map/ppermute | solution.py:29
  416.9 4.1 collective-permute-done.14.refs_2_
  439.3 5.7 %multiply_convert_fusion = bf16[640,1024]{1,0:T(8,128)(2,1)} fusion(f32[640,1024]{1,0:T(8,128)S(1)} %copy-done.3, bf16[640,1024]{1,0:T(8,128)(2,1)} %collective-permute-done.12, f32[1024]{0:T(1024)S(1)} %copy-done.59, f32[640]{0:T(1024)S(1)} %reshape.518, bf16[1024,2048]{1,0:T(8,128)(2,1)S(1)} %copy-done.27, bf16[1280,2048]{1,0:T(8,128)(2,1)S(1)} %bitcast.153), kind=kOutput, calls=%fused_computation.31 | convolution fusion | flops 2688286720 | bytes 12066816 | tf_op jit(solution)/shard_map/dot_general | solution.py:45
  464.3 7.5 %collective-permute-done.19 = bf16[33,32,128]{2,1,0:T(8,128)(2,1)} collective-permute-done((bf16[33,32,128]{2,1,0:T(8,128)(2,1)}, bf16[33,32,128]{2,1,0:T(8,128)(2,1)}, u32[]{:S(2)}, u32[]{:S(2)}) %collective-permute-start.19) | collective-permute-done | bytes 270368 | tf_op jit(solution)/shard_map/ppermute | solution.py:29
  473.5 12.5 %collective-permute-done.20 = bf16[33,32,128]{2,1,0:T(8,128)(2,1)} collective-permute-done((bf16[33,32,128]{2,1,0:T(8,128)(2,1)}, bf16[33,32,128]{2,1,0:T(8,128)(2,1)}, u32[]{:S(2)}, u32[]{:S(2)}) %collective-permute-start.20) | collective-permute-done | bytes 270368 | tf_op jit(solution)/shard_map/ppermute | solution.py:29
  491.5 4.0 collective-permute-done.21
  495.5 4.9 collective-permute-done.22
  512.2 6.3 %collective-permute-done.25.arrived = bf16[64,32,128]{2,1,0:T(8,128)(2,1)S(1)} collective-permute-done((bf16[64,32,128]{2,1,0:T(8,128)(2,1)S(1)}, bf16[64,32,128]{2,1,0:T(8,128)(2,1)S(1)}, u32[]{:S(2)}, u32[]{:S(2)}) %collective-permute-start.25) | collective-permute-done | bytes 524320 | tf_op jit(solution)/shard_map/ppermute | solution.py:24
  521.5 4.7 from_slots.1
  (319 shorter events, 173.5 us)
Async XLA Ops:
  7.2 421.3 %copy-start = (f32[1,33,64,64]{3,2,1,0:T(8,128)S(1)}, f32[1,33,64,64]{3,2,1,0:T(8,128)}, u32[]{:S(2)}) copy-start(f32[1,33,64,64]{3,2,1,0:T(8,128)} %param.43) | copy-start | bytes 1622020
  7.2 53.8 %all-gather.9.cloned.1.call-start = ((), (), s32[]{:S(2)}) async-start(), calls=%async_computation.4 | async-start | bytes 2359296 | tf_op jit(solution)/shard_map/all_gather | solution.py:542
  10.3 124.5 %all-gather.5.cloned.1.call-start = ((), (), s32[]{:S(2)}) async-start(), calls=%async_computation.1 | async-start | bytes 4718592 | tf_op jit(solution)/shard_map/all_gather | solution.py:556
  11.5 342.4 %reduce-scatter.2.cloned.1.call-start = ((), (), s32[]{:S(2)}) async-start(), calls=%async_computation.2 | async-start | bytes 9052160 | tf_op jit(solution)/shard_map/reduce_scatter | solution.py:612
  63.8 35.4 %collective-permute-start = (bf16[8,64,1536]{2,1,0:T(8,128)(2,1)}, bf16[8,64,1536]{2,1,0:T(8,128)(2,1)}, u32[]{:S(2)}, u32[]{:S(2)}) collective-permute-start(bf16[8,64,1536]{2,1,0:T(8,128)(2,1)} %slice.267), channel_id=1, source_target_pairs={{0,1},{1,0},{2,3},{3,2},{4,5},{5,4},{6,7},{7,6},{8,9},{9,8},{10,11... | collective-permute-start | bytes 4718600 | tf_op jit(solution)/shard_map/ppermute | solution.py:24
  101.4 21.5 %collective-permute-start.1 = (bf16[8,64,512]{2,1,0:T(8,128)(2,1)S(1)}, bf16[8,64,512]{2,1,0:T(8,128)(2,1)S(1)}, u32[]{:S(2)}, u32[]{:S(2)}) collective-permute-start(bf16[8,64,512]{2,1,0:T(8,128)(2,1)S(1)} %slice.269), channel_id=1, source_target_pairs={{0,1},{1,0},{2,3},{3,2},{4,5},{5,4},{6,7},{7,6},{8,9},{9,8},{10,11... | collective-permute-start | bytes 1572872 | tf_op jit(solution)/shard_map/ppermute | solution.py:24
  125.3 3.1 collective-permute-start.2
  134.8 8.4 %collective-permute-start.4 = (bf16[1024,2048]{1,0:T(8,128)(2,1)}, bf16[1024,2048]{1,0:T(8,128)(2,1)}, u32[]{:S(2)}, u32[]{:S(2)}) collective-permute-start(bf16[1024,2048]{1,0:T(8,128)(2,1)} %all-gather.5.cloned.1.call-done.mine), channel_id=1, source_target_pairs={{0,2},{2,0},{1,3},{3,1},{4,6},{6,4},{5,7},{7,5},{8,10},{10,8},{9,1... | collective-permute-start | bytes 12582920 | tf_op jit(solution)/shard_map/ppermute | solution.py:24
  134.8 31.5 %collective-permute-start.3 = (bf16[640,1024]{1,0:T(8,128)(2,1)}, bf16[640,1024]{1,0:T(8,128)(2,1)}, u32[]{:S(2)}, u32[]{:S(2)}) collective-permute-start(bf16[640,1024]{1,0:T(8,128)(2,1)} %add_convert_fusion.1.rows), channel_id=1, source_target_pairs={{0,1},{1,0},{2,3},{3,2},{4,5},{5,4},{6,7},{7,6},{8,9},{9,8},{10,11... | collective-permute-start | bytes 3932168 | tf_op jit(solution)/shard_map/ppermute | solution.py:24
  216.9 304.6 %all-gather.7.cloned.1.call-start = ((), (), s32[]{:S(2)}) async-start(), calls=%async_computation.3 | async-start | bytes 9052160 | tf_op jit(solution)/shard_map/all_gather | solution.py:722
  217.3 30.6 %collective-permute-start.5 = (bf16[640,1024]{1,0:T(8,128)(2,1)}, bf16[640,1024]{1,0:T(8,128)(2,1)S(1)}, u32[]{:S(2)}, u32[]{:S(2)}) collective-permute-start(bf16[640,1024]{1,0:T(8,128)(2,1)} %get-tuple-element.83), channel_id=1, source_target_pairs={{0,1},{1,0},{2,3},{3,2},{4,5},{5,4},{6,7},{7,6},{8,9},{9,8},{10,11... | collective-permute-start | bytes 3932168 | tf_op jit(solution)/shard_map/ppermute | solution.py:24
  251.5 3.2 collective-permute-start.6
  305.6 28.7 %collective-permute-start.7 = (bf16[136,32,128]{2,1,0:T(8,128)(2,1)}, bf16[136,32,128]{2,1,0:T(8,128)(2,1)S(1)}, u32[]{:S(2)}, u32[]{:S(2)}) collective-permute-start(bf16[136,32,128]{2,1,0:T(8,128)(2,1)} %slice.275), channel_id=1, source_target_pairs={{0,1},{1,0},{2,3},{3,2},{4,5},{5,4},{6,7},{7,6},{8,9},{9,8},{10,11... | collective-permute-start | bytes 3342344 | tf_op jit(solution)/shard_map/ppermute | solution.py:24
  307.0 25.3 %collective-permute-start.10 = (bf16[128,32,128]{2,1,0:T(8,128)(2,1)}, bf16[128,32,128]{2,1,0:T(8,128)(2,1)}, u32[]{:S(2)}, u32[]{:S(2)}) collective-permute-start(bf16[128,32,128]{2,1,0:T(8,128)(2,1)} %slice.284), channel_id=1, source_target_pairs={{0,4},{4,0},{8,12},{12,8},{16,20},{20,16},{24,28},{28,24},{1,5},{5... | collective-permute-start | bytes 3145736 | tf_op jit(solution)/shard_map/ppermute | solution.py:29
  313.1 23.6 %collective-permute-start.9 = (bf16[640,1024]{1,0:T(8,128)(2,1)}, bf16[640,1024]{1,0:T(8,128)(2,1)S(1)}, u32[]{:S(2)}, u32[]{:S(2)}) collective-permute-start(bf16[640,1024]{1,0:T(8,128)(2,1)} %fusion.23), channel_id=1, source_target_pairs={{0,2},{2,0},{1,3},{3,1},{4,6},{6,4},{5,7},{7,5},{8,10},{10,8},{9,1... | collective-permute-start | bytes 3932168 | tf_op jit(solution)/shard_map/ppermute | solution.py:24
  333.7 13.0 %collective-permute-start.11 = (bf16[64,32,128]{2,1,0:T(8,128)(2,1)S(1)}, bf16[64,32,128]{2,1,0:T(8,128)(2,1)S(1)}, u32[]{:S(2)}, u32[]{:S(2)}) collective-permute-start(bf16[64,32,128]{2,1,0:T(8,128)(2,1)S(1)} %add_convert_fusion.3), channel_id=1, source_target_pairs={{0,1},{1,0},{2,3},{3,2},{4,5},{5,4},{6,7},{7,6},{8,9},{9,8},{10,11... | collective-permute-start | bytes 1572872 | tf_op jit(solution)/shard_map/ppermute | solution.py:24
  335.9 13.4 %collective-permute-start.8 = (bf16[68,32,128]{2,1,0:T(8,128)(2,1)S(1)}, bf16[68,32,128]{2,1,0:T(8,128)(2,1)S(1)}, u32[]{:S(2)}, u32[]{:S(2)}) collective-permute-start(bf16[68,32,128]{2,1,0:T(8,128)(2,1)S(1)} %add_convert_fusion.2), channel_id=1, source_target_pairs={{0,4},{4,0},{8,12},{12,8},{16,20},{20,16},{24,28},{28,24},{1,5},{5... | collective-permute-start | bytes 1671176 | tf_op jit(solution)/shard_map/ppermute | solution.py:29
  384.0 32.9 %collective-permute-start.15 = (bf16[33,32,128]{2,1,0:T(8,128)(2,1)S(1)}, bf16[33,32,128]{2,1,0:T(8,128)(2,1)S(1)}, u32[]{:S(2)}, u32[]{:S(2)}) collective-permute-start(bf16[33,32,128]{2,1,0:T(8,128)(2,1)S(1)} %copy-done.46), channel_id=1, source_target_pairs={{0,24},{4,28},{8,16},{12,20},{16,8},{20,12},{24,0},{28,4},{1,25},{... | collective-permute-start | bytes 811016 | tf_op jit(solution)/shard_map/ppermute | solution.py:29
  385.1 35.9 %collective-permute-start.14 = (bf16[33,32,128]{2,1,0:T(8,128)(2,1)S(1)}, bf16[33,32,128]{2,1,0:T(8,128)(2,1)S(1)}, u32[]{:S(2)}, u32[]{:S(2)}) collective-permute-start(bf16[33,32,128]{2,1,0:T(8,128)(2,1)S(1)} %fusion.82), channel_id=1, source_target_pairs={{0,16},{4,20},{8,24},{12,28},{16,0},{20,4},{24,8},{28,12},{1,17},{... | collective-permute-start | bytes 811016 | tf_op jit(solution)/shard_map/ppermute | solution.py:29
  387.2 33.8 %collective-permute-start.13 = (bf16[33,32,128]{2,1,0:T(8,128)(2,1)S(1)}, bf16[33,32,128]{2,1,0:T(8,128)(2,1)S(1)}, u32[]{:S(2)}, u32[]{:S(2)}) collective-permute-start(bf16[33,32,128]{2,1,0:T(8,128)(2,1)S(1)} %copy-done.47), channel_id=1, source_target_pairs={{0,8},{4,12},{8,0},{12,4},{16,24},{20,28},{24,16},{28,20},{1,9},{5... | collective-permute-start | bytes 811016 | tf_op jit(solution)/shard_map/ppermute | solution.py:29
  387.6 51.7 %collective-permute-start.12 = (bf16[640,1024]{1,0:T(8,128)(2,1)}, bf16[640,1024]{1,0:T(8,128)(2,1)}, u32[]{:S(2)}, u32[]{:S(2)}) collective-permute-start(bf16[640,1024]{1,0:T(8,128)(2,1)} %fusion.20), channel_id=1, source_target_pairs={{0,1},{1,0},{2,3},{3,2},{4,5},{5,4},{6,7},{7,6},{8,9},{9,8},{10,11... | collective-permute-start | bytes 3932168 | tf_op jit(solution)/shard_map/ppermute | solution.py:24
  435.7 27.8 %collective-permute-start.18 = (bf16[33,32,128]{2,1,0:T(8,128)(2,1)}, bf16[33,32,128]{2,1,0:T(8,128)(2,1)S(1)}, u32[]{:S(2)}, u32[]{:S(2)}) collective-permute-start(bf16[33,32,128]{2,1,0:T(8,128)(2,1)} %get-tuple-element.128), channel_id=1, source_target_pairs={{0,8},{4,12},{8,0},{12,4},{16,24},{20,28},{24,16},{28,20},{1,9},{5... | collective-permute-start | bytes 811016 | tf_op jit(solution)/shard_map/ppermute | solution.py:29
  439.2 7.3 %collective-permute-start.16 = (f32[80,128]{1,0:T(8,128)S(1)}, f32[80,128]{1,0:T(8,128)S(1)}, u32[]{:S(2)}, u32[]{:S(2)}) collective-permute-start(f32[80,128]{1,0:T(8,128)S(1)} %bitcast.166), channel_id=1, source_target_pairs={{0,2},{2,0},{1,3},{3,1},{4,6},{6,4},{5,7},{7,5},{8,10},{10,8},{9,1... | collective-permute-start | bytes 122888 | tf_op jit(solution)/shard_map/ppermute | solution.py:24
  445.0 26.8 %collective-permute-start.19 = (bf16[33,32,128]{2,1,0:T(8,128)(2,1)}, bf16[33,32,128]{2,1,0:T(8,128)(2,1)}, u32[]{:S(2)}, u32[]{:S(2)}) collective-permute-start(bf16[33,32,128]{2,1,0:T(8,128)(2,1)} %get-tuple-element.128), channel_id=1, source_target_pairs={{0,16},{4,20},{8,24},{12,28},{16,0},{20,4},{24,8},{28,12},{1,17},{... | collective-permute-start | bytes 811016 | tf_op jit(solution)/shard_map/ppermute | solution.py:29
  445.0 41.0 %collective-permute-start.20 = (bf16[33,32,128]{2,1,0:T(8,128)(2,1)}, bf16[33,32,128]{2,1,0:T(8,128)(2,1)}, u32[]{:S(2)}, u32[]{:S(2)}) collective-permute-start(bf16[33,32,128]{2,1,0:T(8,128)(2,1)} %get-tuple-element.128), channel_id=1, source_target_pairs={{0,24},{4,28},{8,16},{12,20},{16,8},{20,12},{24,0},{28,4},{1,25},{... | collective-permute-start | bytes 811016 | tf_op jit(solution)/shard_map/ppermute | solution.py:29
  446.6 16.2 %collective-permute-start.17 = (f32[80,128]{1,0:T(8,128)S(1)}, f32[80,128]{1,0:T(8,128)}, u32[]{:S(2)}, u32[]{:S(2)}) collective-permute-start(f32[80,128]{1,0:T(8,128)S(1)} %add.569), channel_id=1, source_target_pairs={{0,1},{1,0},{2,3},{3,2},{4,5},{5,4},{6,7},{7,6},{8,9},{9,8},{10,11... | collective-permute-start | bytes 122888 | tf_op jit(solution)/shard_map/ppermute | solution.py:24
  464.3 43.3 %copy-start.25 = (f32[33,64,64]{2,1,0:T(8,128)S(1)}, f32[33,64,64]{2,1,0:T(8,128)}, u32[]{:S(2)}) copy-start(f32[33,64,64]{2,1,0:T(8,128)} %copy-done.24) | copy-start | bytes 1622020
  490.5 14.4 %collective-permute-start.24 = (bf16[64,32,128]{2,1,0:T(8,128)(2,1)}, bf16[64,32,128]{2,1,0:T(8,128)(2,1)S(1)}, u32[]{:S(2)}, u32[]{:S(2)}) collective-permute-start(bf16[64,32,128]{2,1,0:T(8,128)(2,1)} %get-tuple-element.110), channel_id=1, source_target_pairs={{0,4},{4,0},{8,12},{12,8},{16,20},{20,16},{24,28},{28,24},{1,5},{5... | collective-permute-start | bytes 1572872 | tf_op jit(solution)/shard_map/ppermute | solution.py:29
  491.5 4.0 collective-permute-start.21
  495.5 4.9 collective-permute-start.22
  500.4 10.6 %collective-permute-start.23 = (f32[80,128]{1,0:T(8,128)S(1)}, f32[80,128]{1,0:T(8,128)S(1)}, u32[]{:S(2)}, u32[]{:S(2)}) collective-permute-start(f32[80,128]{1,0:T(8,128)S(1)} %add.608), channel_id=1, source_target_pairs={{0,4},{4,0},{8,12},{12,8},{16,20},{20,16},{24,28},{28,24},{1,5},{5... | collective-permute-start | bytes 122888 | tf_op jit(solution)/shard_map/ppermute | solution.py:29
  506.1 12.5 %collective-permute-start.25 = (bf16[64,32,128]{2,1,0:T(8,128)(2,1)S(1)}, bf16[64,32,128]{2,1,0:T(8,128)(2,1)S(1)}, u32[]{:S(2)}, u32[]{:S(2)}) collective-permute-start(bf16[64,32,128]{2,1,0:T(8,128)(2,1)S(1)} %add.610.held), channel_id=1, source_target_pairs={{0,1},{1,0},{2,3},{3,2},{4,5},{5,4},{6,7},{7,6},{8,9},{9,8},{10,11... | collective-permute-start | bytes 1572872 | tf_op jit(solution)/shard_map/ppermute | solution.py:24
  (62 other events, 372.3 us)
Sparse Core Ops, SparseCore 0:
  10.7 50.2 all-gather.8
  63.7 70.9 all-gather.4
  217.0 104.1 reduce-scatter.1
  372.7 107.8 all-gather.6

commit v3 on v2

--- a/solution.py
+++ b/solution.py
@@ -17,7 +17,7 @@
 F32 = jnp.float32
 BF16 = jnp.bfloat16
 
-precise = lax.Precision.HIGHEST
+precise = lax.Precision.HIGH
 
 
 def swap(value, axis):
@@ -71,8 +71,12 @@
     return (jnp.where(first, both, nothing), jnp.where(first, nothing, both))
 
 
-def weights_of(keys, queries, valid):
-    scores = jnp.where(valid, dot(keys, queries, (1, 0)), -1000000000.0)
+def scaled(rows, pair):
+    return head_pair(rows, pair, 0) * jnp.asarray(0.125, BF16)
+
+
+def weights_of(scores, valid):
+    scores = jnp.where(valid, scores, -1000000000.0)
     raised = jnp.exp(scores - jnp.max(scores, axis=0, keepdims=True))
     return (raised, 1.0 / jnp.sum(raised, axis=0, keepdims=True))
 
@@ -82,15 +86,26 @@
     return lax.broadcasted_iota(jnp.int32, (slots, slots), 0) < BUF + count
 
 
+def products(left, right):
+    return [dot(left, one, (1, 0)) for one in one_head_each(right.T)]
+
+
 def attn_forward_body(kept, rows, out):
     valid = key_mask(rows, kept[pl.program_id(0)])
-    for pair in range(rows.shape[1] // (6 * HD)):
-        queries = (head_pair(rows, pair, 0) * jnp.asarray(0.125, BF16)).T
-        keys = head_pair(rows, pair, 1)
+    pairs = rows.shape[1] // (6 * HD)
+
+    def scores_of(pair):
+        return products(head_pair(rows, pair, 1), scaled(rows, pair))
+
+    ahead = scores_of(0)
+    for pair in range(pairs):
+        scores = ahead
+        if pair + 1 < pairs:
+            ahead = scores_of(pair + 1)
         values = head_pair(rows, pair, 2).T
         halves = []
-        for number, query in enumerate(one_head_each(queries)):
-            raised, scale = weights_of(keys, query, valid)
+        for number in range(2):
+            raised, scale = weights_of(scores[number], valid)
             value = values[number * HD : (number + 1) * HD]
             halves.append(dot(value, raised.astype(BF16), (1, 0)) * scale)
         out[:, pair * LANES : (pair + 1) * LANES] = jnp.concatenate(halves).T.astype(BF16)
@@ -115,28 +130,35 @@
 def attn_backward_body(kept, rows, grads, out):
     valid = key_mask(rows, kept[pl.program_id(0)])
     width = rows.shape[1] // 3
+    pairs = width // LANES
     first = lax.broadcasted_iota(jnp.int32, (rows.shape[0], LANES), 1) < HD
-    for pair in range(width // LANES):
+
+    def ahead_of(pair):
+        grad = grads[:, pair * LANES : (pair + 1) * LANES]
+        scores = products(head_pair(rows, pair, 1), scaled(rows, pair))
+        return (scores, products(head_pair(rows, pair, 2), grad))
+
+    ahead = ahead_of(0)
+    for pair in range(pairs):
+        scores, grad_probs = ahead
+        if pair + 1 < pairs:
+            ahead = ahead_of(pair + 1)
         window = slice(pair * LANES, (pair + 1) * LANES)
-        queries = head_pair(rows, pair, 0) * jnp.asarray(0.125, BF16)
-        keys = head_pair(rows, pair, 1)
-        keys_t = keys.T
-        values = head_pair(rows, pair, 2)
-        grad = grads[:, window]
-        halves = ([], [], [])
-        for number, (query, grad_t) in enumerate(zip(one_head_each(queries.T), one_head_each(grad.T))):
-            raised, scale = weights_of(keys, query, valid)
-            probs = raised * scale
-            grad_probs = dot(values, grad_t, (1, 0))
-            inner = jnp.sum(probs * grad_probs, axis=0, keepdims=True)
-            grad_scores = (probs * (grad_probs - inner)).astype(BF16)
-            halves[0].append(dot(keys_t[number * HD : (number + 1) * HD], grad_scores, (1, 0)))
-            halves[1].append(dot(grad_scores, queries, (1, 0)))
-            halves[2].append(dot(probs.astype(BF16), grad, (1, 0)))
-        out[:, window] = (jnp.concatenate(halves[0]).T * 0.125).astype(BF16)
-        for which in (1, 2):
+        probs = []
+        grad_scores = []
+        for number in range(2):
+            raised, scale = weights_of(scores[number], valid)
+            inner = jnp.sum(raised * grad_probs[number], axis=0, keepdims=True) * scale
+            weights = raised * scale
+            probs.append(weights.astype(BF16))
+            grad_scores.append((weights * (grad_probs[number] - inner)).astype(BF16))
+        keys_t = head_pair(rows, pair, 1).T
+        parts = [dot(keys_t[n * HD : (n + 1) * HD], grad_scores[n], (1, 0)) for n in range(2)]
+        out[:, window] = (jnp.concatenate(parts).T * 0.125).astype(BF16)
+        for which, lefts, right in ((1, grad_scores, scaled(rows, pair)), (2, probs, grads[:, window])):
             start = which * width + pair * LANES
-            out[:, start : start + LANES] = jnp.where(first, *halves[which]).astype(BF16)
+            parts = [dot(left, right, (1, 0)) for left in lefts]
+            out[:, start : start + LANES] = jnp.where(first, *parts).astype(BF16)
 
 
 def attn_backward(kept, rows, grads, slots):
@@ -201,19 +223,19 @@
             up[...] = other[...] if swapped else mine[...]
             down_t[...] = mine[...] if swapped else other[...]
 
-    part = None
-    for start in range(0, up.shape[1], COL_CHUNK):
-        window = slice(start, start + COL_CHUNK)
+    windows = [slice(start, start + COL_CHUNK) for start in range(0, up.shape[1], COL_CHUNK)]
+    pairs = []
+    for window in windows:
         pre = dot(rows[...], up[:, window], (1, 0)) + bias[:, window]
-        grad_hidden = dot(cot[...], down_t[:, window], (1, 0))
+        pairs.append((pre, dot(cot[...], down_t[:, window], (1, 0))))
+    for window, (pre, grad_hidden) in zip(windows, pairs):
         cdf = 0.5 + 0.5 * erf(pre * 0.7071067811865476)
         density = 0.3989422804014327 * jnp.exp(-0.5 * pre * pre)
         hidden[:, window] = (pre * cdf).astype(BF16)
         grad = (grad_hidden * (cdf + pre * density)).astype(BF16)
         grad_pre[:, window] = grad
         bias_sum[:, window] = jnp.sum(grad.astype(F32), axis=0, keepdims=True)
-        back = dot(grad, up[:, window], (1, 1))
-        part = back if part is None else part + back
+    part = dot(grad_pre[...], up[...], (1, 1))
 
     @pl.when(step == 0)
     def _():
@@ -734,7 +756,6 @@
     mlp_outs = settle(*(jnp.transpose(a, (1, 2, 0)) for a in mlp_news))
     small = after(small, attn_dense)
     small = small + swap(small, HEAD)
-    small = small + swap(small, TENSOR)
 
     own = w_qkv.shape[1]
     if direct:
@@ -746,7 +767,8 @@
         where = jnp.where(here, high * attn_cap + inner, columns * attn_cap)
         lists = [local_blocks(p, rows, group_cols // BS, own // BS) for p in (shard_pos, shard_pos ^ 1)]
         table = jnp.take(where, jnp.concatenate(lists), axis=0)
-        table = after(table, *mlp_outs, small, out, tokens_grad)
+        small = small + swap(small, TENSOR)
+        table = after(table, *mlp_outs, small, out)
         mine, theirs = pick(table, jnp.concatenate(column + [empty]), 2)
         small = after(small, theirs)
         small = small + across(small, 2)
@@ -764,6 +786,7 @@
             (w_up.shape, w_down.shape),
         )
     else:
+        small = small + swap(small, TENSOR)
         bit = 1
         while bit < shards:
             small = small + across(small, bit)

time: 543 us -> 539 us (level)
  the two profiles are of different devices: /device:TPU:8 before, /device:TPU:10 now
where the time goes in v3:
time: 539 us; the launch traced here: 530 us
  waiting for transfers between devices  190 us (35%)
  Pallas kernels  98.7 us (18%)
  matrix products  80.9 us (15%)
  local copies, waits for them, and re-layouts  72 us (13%)
  other arithmetic  46 us (9%)
  starting transfers between devices  27.1 us (5%)
  between operations  14.9 us (3%)
    ppermute x12, waiting for transfers between devices, across(): return lax.ppermute(value, SHARD, [(i, i ^ bits) for i in range(size)])  85.2 us
    dot_general x14, matrix products, dot(): lax.dot_general(left, right, ((contract[:1], contract[1:]), ((), ())), pr...  64 us
    ppermute x14, waiting for transfers between devices, swap(): return lax.ppermute(value, axis, [(0, 1), (1, 0)])  53.5 us
    all_gather x1, waiting for transfers between devices, per_device(): attn_half = lax.all_gather(attn_half, SHARD, axis=0)  45.1 us
    pallas_call x2, Pallas kernels, feed(): pl.pallas_call(feed_body, out_shape=(whole, whole, jax.ShapeDtypeStruct((...  41.3 us
    unnamed x144, local copies, waits for them, and re-layouts  38.2 us
    pallas_call x1, Pallas kernels, attn_backward(): pl.pallas_call(attn_backward_body, out_shape=jax.ShapeDtypeStruct(rows.sh...  18.6 us
    pallas_call x2, Pallas kernels, to_parcel(): pl.pallas_call(partial(to_parcel_body, indices_of), out_shape=jax.ShapeDt...  17.3 us
  transfers between devices with their start and end apart: 30, of which 18 were waited for; matrix products, arithmetic and copies ran while one was open for 28% of the time, Pallas kernels for 12%

profile of v3, /device:TPU:10, one launch (start us, length us, event | category | flops | bytes accessed | tf_op | source)
XLA Modules:
  0.0 530.1 jit_solution(3934041133735434350)
XLA Ops:
  15.0 45.1 %all-gather.9.cloned.1.call-done = bf16[512,2048]{1,0:T(8,128)(2,1)} async-done(((bf16[64,2048]{1,0:T(8,128)(2,1)}), bf16[512,2048]{1,0:T(8,128)(2,1)}) %all-gather.9.cloned.1.call-update) | async-done | bytes 2097168 | tf_op jit(solution)/shard_map/all_gather | solution.py:564
  69.3 4.0 copy.109
  77.2 3.9 copy.111
  81.1 4.0 copy.112
  89.7 8.5 %collective-permute-done = bf16[8,64,1536]{2,1,0:T(8,128)(2,1)} collective-permute-done((bf16[8,64,1536]{2,1,0:T(8,128)(2,1)}, bf16[8,64,1536]{2,1,0:T(8,128)(2,1)}, u32[]{:S(2)}, u32[]{:S(2)}) %collective-permute-start) | collective-permute-done | bytes 1572896 | tf_op jit(solution)/shard_map/ppermute | solution.py:24
  102.0 5.7 %convolution_convert_fusion.rows = bf16[1280,1536]{1,0:T(8,128)(2,1)} fusion(bf16[1024,1536]{1,0:T(8,128)(2,1)S(1)} %bitcast.155, f32[1280,1024]{1,0:T(8,128)S(1)} %fusion, f32[1024]{0:T(1024)S(1)} %copy-done.58, f32[1024]{0:T(1024)S(1)} %copy-done.49), kind=kOutput, calls=%fused_computation.1 | convolution fusion | flops 4032430080 | bytes 12328960 | tf_op jit(solution)/shard_map/dot_general | solution.py:45
  107.8 10.0 %attn_forward.1 = bf16[1280,512]{1,0:T(8,128)(2,1)} custom-call(s32[4]{0:T(128)} %get-tuple-element.178.kept, bf16[1280,1536]{1,0:T(8,128)(2,1)} %convolution_convert_fusion.rows), custom_call_target="tpu_custom_call" | custom-call | tf_op jit(solution)/shard_map/attn_forward/pallas_call | solution.py:117
  127.3 6.5 %all-gather.5.cloned.1.call-done.mine = bf16[1024,2048]{1,0:T(8,128)(2,1)} async-done(((bf16[128,2048]{1,0:T(8,128)(2,1)}), bf16[1024,2048]{1,0:T(8,128)(2,1)}) %all-gather.5.cloned.1.call-update) | async-done | bytes 4194320 | tf_op jit(solution)/shard_map/all_gather | solution.py:578
  142.2 20.6 %feed.2 = (bf16[1280,2048]{1,0:T(8,128)(2,1)}, bf16[1280,2048]{1,0:T(8,128)(2,1)}, f32[1,2048]{1,0:T(1,128)}, f32[640,1024]{1,0:T(8,128)}) custom-call(s32[1]{0:T(128)} %bitcast.18.flag, bf16[640,1024]{1,0:T(8,128)(2,1)} %add_convert_fusion.1.rows, bf16[1280,1024]{1,0:T(8,128)(2,1)} %bitcast_select_fusion.cot, ...), custom_call_target="tpu_custom_call" | custom-call | tf_op jit(solution)/shard_map/feed/pallas_call | solution.py:261
  165.4 20.7 %feed.3 = (bf16[1280,2048]{1,0:T(8,128)(2,1)}, bf16[1280,2048]{1,0:T(8,128)(2,1)}, f32[1,2048]{1,0:T(1,128)}, bf16[640,1024]{1,0:T(8,128)(2,1)}) custom-call(s32[1]{0:T(128)} %bitcast.18.flag, bf16[640,1024]{1,0:T(8,128)(2,1)} %collective-permute-done.3.rows, ...), custom_call_target="tpu_custom_call", output_to_operand_aliasing={{0}: (6, {}), {1}: (7, {})} | custom-call | tf_op jit(solution)/shard_map/feed/pallas_call | solution.py:261
  186.1 10.3 %convolution_convert_fusion.1.refs_1_ = bf16[2048,1024]{1,0:T(8,128)(2,1)} fusion(bf16[1280,2048]{1,0:T(8,128)(2,1)} %get-tuple-element.86, bf16[1280,1024]{1,0:T(8,128)(2,1)} %bitcast_select_fusion.cot), kind=kOutput, calls=%fused_computation.9 | convolution fusion | flops 5370806272 | bytes 12058624 | tf_op jit(solution)/shard_map/dot_general | solution.py:45
  196.4 9.1 %convolution_convert_fusion.2.refs_0_ = bf16[1024,2048]{1,0:T(8,128)(2,1)} fusion(bf16[1280,2048]{1,0:T(8,128)(2,1)S(1)} %copy-done.19, bf16[640,1024]{1,0:T(8,128)(2,1)} %collective-permute-done.3.rows, bf16[640,1024]{1,0:T(8,128)(2,1)} %add_convert_fusion.1.rows), kind=kOutput, calls=%fused_computation.10 | convolution fusion | flops 5376049152 | bytes 12058624 | tf_op jit(solution)/shard_map/dot_general | solution.py:45
  205.5 10.3 %to_parcel.2 = bf16[1040,32,128]{2,1,0:T(8,128)(2,1)} custom-call(s32[1024]{0:T(1024)} %convert_add_fusion.11.slots, bf16[1024,2048]{1,0:T(8,128)(2,1)} %convolution_convert_fusion.2.refs_0_, bf16[2048,1024]{1,0:T(8,128)(2,1)} %convolution_convert_fusion.1.refs_1_), custom_call_target="tpu_custom_call" | custom-call | tf_op jit(solution)/shard_map/to_parcel/pallas_call | solution.py:329
  217.9 28.7 %collective-permute-done.5 = bf16[640,1024]{1,0:T(8,128)(2,1)S(1)} collective-permute-done((bf16[640,1024]{1,0:T(8,128)(2,1)}, bf16[640,1024]{1,0:T(8,128)(2,1)S(1)}, u32[]{:S(2)}, u32[]{:S(2)}) %collective-permute-start.5) | collective-permute-done | bytes 1310752 | tf_op jit(solution)/shard_map/ppermute | solution.py:24
  257.2 18.6 %attn_backward.1 = bf16[1280,1536]{1,0:T(8,128)(2,1)} custom-call(s32[4]{0:T(128)} %get-tuple-element.178.kept, bf16[1280,1536]{1,0:T(8,128)(2,1)} %convolution_convert_fusion.rows, bf16[1280,512]{1,0:T(8,128)(2,1)} %convolution_convert_fusion.4.grads), custom_call_target="tpu_custom_call" | custom-call | tf_op jit(solution)/shard_map/attn_backward/pallas_call | solution.py:167
  275.8 4.5 fusion.26.refs_1_
  280.3 8.5 %convolution_convert_fusion.3.refs_0_ = bf16[1024,1536]{1,0:T(8,128)(2,1)} fusion(bf16[1280,1536]{1,0:T(8,128)(2,1)S(1)} %copy-done.28, f32[1280,1024]{1,0:T(8,128)} %copy-done.5, f32[1024]{0:T(1024)S(1)} %copy-done.58, f32[1024]{0:T(1024)S(1)} %copy-done.49), kind=kOutput, calls=%fused_computation.11 | convolution fusion | flops 4032036864 | bytes 12328960 | tf_op jit(solution)/shard_map/dot_general | solution.py:45
  288.8 7.0 %to_parcel.3 = bf16[528,32,128]{2,1,0:T(8,128)(2,1)} custom-call(s32[512]{0:T(512)} %get-tuple-element.174.slots, bf16[1024,1536]{1,0:T(8,128)(2,1)} %convolution_convert_fusion.3.refs_0_, bf16[512,1024]{1,0:T(8,128)(2,1)} %fusion.26.refs_1_), custom_call_target="tpu_custom_call" | custom-call | tf_op jit(solution)/shard_map/to_parcel/pallas_call | solution.py:329
  303.6 5.2 fusion.23
  308.8 4.8 fusion.17
  313.6 15.8 %collective-permute-done.10 = bf16[128,32,128]{2,1,0:T(8,128)(2,1)} collective-permute-done((bf16[128,32,128]{2,1,0:T(8,128)(2,1)}, bf16[128,32,128]{2,1,0:T(8,128)(2,1)}, u32[]{:S(2)}, u32[]{:S(2)}) %collective-permute-start.10) | collective-permute-done | bytes 1048608 | tf_op jit(solution)/shard_map/ppermute | solution.py:29
  338.3 4.0 multiply_add_fusion.1
  375.8 4.0 fusion.20
  384.3 28.6 %collective-permute-done.15.refs_3_ = bf16[33,32,128]{2,1,0:T(8,128)(2,1)S(1)} collective-permute-done((bf16[33,32,128]{2,1,0:T(8,128)(2,1)S(1)}, bf16[33,32,128]{2,1,0:T(8,128)(2,1)S(1)}, u32[]{:S(2)}, u32[]{:S(2)}) %collective-permute-start.15) | collective-permute-done | bytes 270368 | tf_op jit(solution)/shard_map/ppermute | solution.py:29
  412.9 5.4 %collective-permute-done.14.refs_2_ = bf16[33,32,128]{2,1,0:T(8,128)(2,1)S(1)} collective-permute-done((bf16[33,32,128]{2,1,0:T(8,128)(2,1)S(1)}, bf16[33,32,128]{2,1,0:T(8,128)(2,1)S(1)}, u32[]{:S(2)}, u32[]{:S(2)}) %collective-permute-start.14) | collective-permute-done | bytes 270368 | tf_op jit(solution)/shard_map/ppermute | solution.py:29
  434.6 5.3 %multiply_convert_fusion = bf16[640,1024]{1,0:T(8,128)(2,1)} fusion(f32[640,1024]{1,0:T(8,128)S(1)} %copy-done.3, bf16[640,1024]{1,0:T(8,128)(2,1)} %collective-permute-done.12, f32[1024]{0:T(1024)S(1)} %copy-done.59, f32[640]{0:T(1024)S(1)} %reshape.518, bf16[1024,2048]{1,0:T(8,128)(2,1)S(1)} %copy-done.27, bf16[1280,2048]{1,0:T(8,128)(2,1)S(1)} %bitcast.153), kind=kOutput, calls=%fused_computation.31 | convolution fusion | flops 2688286720 | bytes 12066816 | tf_op jit(solution)/shard_map/dot_general | solution.py:45
  459.6 7.8 %collective-permute-done.19 = bf16[33,32,128]{2,1,0:T(8,128)(2,1)} collective-permute-done((bf16[33,32,128]{2,1,0:T(8,128)(2,1)}, bf16[33,32,128]{2,1,0:T(8,128)(2,1)}, u32[]{:S(2)}, u32[]{:S(2)}) %collective-permute-start.19) | collective-permute-done | bytes 270368 | tf_op jit(solution)/shard_map/ppermute | solution.py:29
  469.1 14.0 %collective-permute-done.20 = bf16[33,32,128]{2,1,0:T(8,128)(2,1)} collective-permute-done((bf16[33,32,128]{2,1,0:T(8,128)(2,1)}, bf16[33,32,128]{2,1,0:T(8,128)(2,1)}, u32[]{:S(2)}, u32[]{:S(2)}) %collective-permute-start.20) | collective-permute-done | bytes 270368 | tf_op jit(solution)/shard_map/ppermute | solution.py:29
  488.2 4.1 collective-permute-done.21
  492.3 4.9 collective-permute-done.22
  509.2 6.5 %collective-permute-done.25.arrived = bf16[64,32,128]{2,1,0:T(8,128)(2,1)S(1)} collective-permute-done((bf16[64,32,128]{2,1,0:T(8,128)(2,1)S(1)}, bf16[64,32,128]{2,1,0:T(8,128)(2,1)S(1)}, u32[]{:S(2)}, u32[]{:S(2)}) %collective-permute-start.25) | collective-permute-done | bytes 524320 | tf_op jit(solution)/shard_map/ppermute | solution.py:24
  518.7 4.7 from_slots.1
  (319 shorter events, 174.2 us)
Async XLA Ops:
  7.2 417.8 %copy-start = (f32[1,33,64,64]{3,2,1,0:T(8,128)S(1)}, f32[1,33,64,64]{3,2,1,0:T(8,128)}, u32[]{:S(2)}) copy-start(f32[1,33,64,64]{3,2,1,0:T(8,128)} %param.43) | copy-start | bytes 1622020
  7.2 52.9 %all-gather.9.cloned.1.call-start = ((), (), s32[]{:S(2)}) async-start(), calls=%async_computation.4 | async-start | bytes 2359296 | tf_op jit(solution)/shard_map/all_gather | solution.py:564
  10.3 123.5 %all-gather.5.cloned.1.call-start = ((), (), s32[]{:S(2)}) async-start(), calls=%async_computation.1 | async-start | bytes 4718592 | tf_op jit(solution)/shard_map/all_gather | solution.py:578
  11.5 341.1 %reduce-scatter.2.cloned.1.call-start = ((), (), s32[]{:S(2)}) async-start(), calls=%async_computation.2 | async-start | bytes 9052160 | tf_op jit(solution)/shard_map/reduce_scatter | solution.py:634
  62.9 35.4 %collective-permute-start = (bf16[8,64,1536]{2,1,0:T(8,128)(2,1)}, bf16[8,64,1536]{2,1,0:T(8,128)(2,1)}, u32[]{:S(2)}, u32[]{:S(2)}) collective-permute-start(bf16[8,64,1536]{2,1,0:T(8,128)(2,1)} %slice.267), channel_id=1, source_target_pairs={{0,1},{1,0},{2,3},{3,2},{4,5},{5,4},{6,7},{7,6},{8,9},{9,8},{10,11... | collective-permute-start | bytes 4718600 | tf_op jit(solution)/shard_map/ppermute | solution.py:24
  100.5 17.2 %collective-permute-start.1 = (bf16[8,64,512]{2,1,0:T(8,128)(2,1)S(1)}, bf16[8,64,512]{2,1,0:T(8,128)(2,1)S(1)}, u32[]{:S(2)}, u32[]{:S(2)}) collective-permute-start(bf16[8,64,512]{2,1,0:T(8,128)(2,1)S(1)} %slice.269), channel_id=1, source_target_pairs={{0,1},{1,0},{2,3},{3,2},{4,5},{5,4},{6,7},{7,6},{8,9},{9,8},{10,11... | collective-permute-start | bytes 1572872 | tf_op jit(solution)/shard_map/ppermute | solution.py:24
  120.0 3.1 collective-permute-start.2
  133.8 8.4 %collective-permute-start.4 = (bf16[1024,2048]{1,0:T(8,128)(2,1)}, bf16[1024,2048]{1,0:T(8,128)(2,1)}, u32[]{:S(2)}, u32[]{:S(2)}) collective-permute-start(bf16[1024,2048]{1,0:T(8,128)(2,1)} %all-gather.5.cloned.1.call-done.mine), channel_id=1, source_target_pairs={{0,2},{2,0},{1,3},{3,1},{4,6},{6,4},{5,7},{7,5},{8,10},{10,8},{9,1... | collective-permute-start | bytes 12582920 | tf_op jit(solution)/shard_map/ppermute | solution.py:24
  133.9 31.5 %collective-permute-start.3 = (bf16[640,1024]{1,0:T(8,128)(2,1)}, bf16[640,1024]{1,0:T(8,128)(2,1)}, u32[]{:S(2)}, u32[]{:S(2)}) collective-permute-start(bf16[640,1024]{1,0:T(8,128)(2,1)} %add_convert_fusion.1.rows), channel_id=1, source_target_pairs={{0,1},{1,0},{2,3},{3,2},{4,5},{5,4},{6,7},{7,6},{8,9},{9,8},{10,11... | collective-permute-start | bytes 3932168 | tf_op jit(solution)/shard_map/ppermute | solution.py:24
  215.8 302.9 %all-gather.7.cloned.1.call-start = ((), (), s32[]{:S(2)}) async-start(), calls=%async_computation.3 | async-start | bytes 9052160 | tf_op jit(solution)/shard_map/all_gather | solution.py:744
  216.0 30.6 %collective-permute-start.5 = (bf16[640,1024]{1,0:T(8,128)(2,1)}, bf16[640,1024]{1,0:T(8,128)(2,1)S(1)}, u32[]{:S(2)}, u32[]{:S(2)}) collective-permute-start(bf16[640,1024]{1,0:T(8,128)(2,1)} %get-tuple-element.83), channel_id=1, source_target_pairs={{0,1},{1,0},{2,3},{3,2},{4,5},{5,4},{6,7},{7,6},{8,9},{9,8},{10,11... | collective-permute-start | bytes 3932168 | tf_op jit(solution)/shard_map/ppermute | solution.py:24
  250.1 3.2 collective-permute-start.6
  300.6 31.6 %collective-permute-start.7 = (bf16[136,32,128]{2,1,0:T(8,128)(2,1)}, bf16[136,32,128]{2,1,0:T(8,128)(2,1)S(1)}, u32[]{:S(2)}, u32[]{:S(2)}) collective-permute-start(bf16[136,32,128]{2,1,0:T(8,128)(2,1)} %slice.275), channel_id=1, source_target_pairs={{0,1},{1,0},{2,3},{3,2},{4,5},{5,4},{6,7},{7,6},{8,9},{9,8},{10,11... | collective-permute-start | bytes 3342344 | tf_op jit(solution)/shard_map/ppermute | solution.py:24
  302.1 27.3 %collective-permute-start.10 = (bf16[128,32,128]{2,1,0:T(8,128)(2,1)}, bf16[128,32,128]{2,1,0:T(8,128)(2,1)}, u32[]{:S(2)}, u32[]{:S(2)}) collective-permute-start(bf16[128,32,128]{2,1,0:T(8,128)(2,1)} %slice.284), channel_id=1, source_target_pairs={{0,4},{4,0},{8,12},{12,8},{16,20},{20,16},{24,28},{28,24},{1,5},{5... | collective-permute-start | bytes 3145736 | tf_op jit(solution)/shard_map/ppermute | solution.py:29
  308.7 26.7 %collective-permute-start.9 = (bf16[640,1024]{1,0:T(8,128)(2,1)}, bf16[640,1024]{1,0:T(8,128)(2,1)S(1)}, u32[]{:S(2)}, u32[]{:S(2)}) collective-permute-start(bf16[640,1024]{1,0:T(8,128)(2,1)} %fusion.23), channel_id=1, source_target_pairs={{0,2},{2,0},{1,3},{3,1},{4,6},{6,4},{5,7},{7,5},{8,10},{10,8},{9,1... | collective-permute-start | bytes 3932168 | tf_op jit(solution)/shard_map/ppermute | solution.py:24
  330.7 13.7 %collective-permute-start.11 = (bf16[64,32,128]{2,1,0:T(8,128)(2,1)S(1)}, bf16[64,32,128]{2,1,0:T(8,128)(2,1)S(1)}, u32[]{:S(2)}, u32[]{:S(2)}) collective-permute-start(bf16[64,32,128]{2,1,0:T(8,128)(2,1)S(1)} %add_convert_fusion.3), channel_id=1, source_target_pairs={{0,1},{1,0},{2,3},{3,2},{4,5},{5,4},{6,7},{7,6},{8,9},{9,8},{10,11... | collective-permute-start | bytes 1572872 | tf_op jit(solution)/shard_map/ppermute | solution.py:24
  333.9 14.1 %collective-permute-start.8 = (bf16[68,32,128]{2,1,0:T(8,128)(2,1)S(1)}, bf16[68,32,128]{2,1,0:T(8,128)(2,1)S(1)}, u32[]{:S(2)}, u32[]{:S(2)}) collective-permute-start(bf16[68,32,128]{2,1,0:T(8,128)(2,1)S(1)} %add_convert_fusion.2), channel_id=1, source_target_pairs={{0,4},{4,0},{8,12},{12,8},{16,20},{20,16},{24,28},{28,24},{1,5},{5... | collective-permute-start | bytes 1671176 | tf_op jit(solution)/shard_map/ppermute | solution.py:29
  379.8 33.1 %collective-permute-start.15 = (bf16[33,32,128]{2,1,0:T(8,128)(2,1)S(1)}, bf16[33,32,128]{2,1,0:T(8,128)(2,1)S(1)}, u32[]{:S(2)}, u32[]{:S(2)}) collective-permute-start(bf16[33,32,128]{2,1,0:T(8,128)(2,1)S(1)} %copy-done.46), channel_id=1, source_target_pairs={{0,24},{4,28},{8,16},{12,20},{16,8},{20,12},{24,0},{28,4},{1,25},{... | collective-permute-start | bytes 811016 | tf_op jit(solution)/shard_map/ppermute | solution.py:29
  381.5 36.9 %collective-permute-start.14 = (bf16[33,32,128]{2,1,0:T(8,128)(2,1)S(1)}, bf16[33,32,128]{2,1,0:T(8,128)(2,1)S(1)}, u32[]{:S(2)}, u32[]{:S(2)}) collective-permute-start(bf16[33,32,128]{2,1,0:T(8,128)(2,1)S(1)} %fusion.82), channel_id=1, source_target_pairs={{0,16},{4,20},{8,24},{12,28},{16,0},{20,4},{24,8},{28,12},{1,17},{... | collective-permute-start | bytes 811016 | tf_op jit(solution)/shard_map/ppermute | solution.py:29
  382.9 35.5 %collective-permute-start.13 = (bf16[33,32,128]{2,1,0:T(8,128)(2,1)S(1)}, bf16[33,32,128]{2,1,0:T(8,128)(2,1)S(1)}, u32[]{:S(2)}, u32[]{:S(2)}) collective-permute-start(bf16[33,32,128]{2,1,0:T(8,128)(2,1)S(1)} %copy-done.47), channel_id=1, source_target_pairs={{0,8},{4,12},{8,0},{12,4},{16,24},{20,28},{24,16},{28,20},{1,9},{5... | collective-permute-start | bytes 811016 | tf_op jit(solution)/shard_map/ppermute | solution.py:29
  383.8 50.8 %collective-permute-start.12 = (bf16[640,1024]{1,0:T(8,128)(2,1)}, bf16[640,1024]{1,0:T(8,128)(2,1)}, u32[]{:S(2)}, u32[]{:S(2)}) collective-permute-start(bf16[640,1024]{1,0:T(8,128)(2,1)} %fusion.20), channel_id=1, source_target_pairs={{0,1},{1,0},{2,3},{3,2},{4,5},{5,4},{6,7},{7,6},{8,9},{9,8},{10,11... | collective-permute-start | bytes 3932168 | tf_op jit(solution)/shard_map/ppermute | solution.py:24
  431.2 27.7 %collective-permute-start.18 = (bf16[33,32,128]{2,1,0:T(8,128)(2,1)}, bf16[33,32,128]{2,1,0:T(8,128)(2,1)S(1)}, u32[]{:S(2)}, u32[]{:S(2)}) collective-permute-start(bf16[33,32,128]{2,1,0:T(8,128)(2,1)} %get-tuple-element.128), channel_id=1, source_target_pairs={{0,8},{4,12},{8,0},{12,4},{16,24},{20,28},{24,16},{28,20},{1,9},{5... | collective-permute-start | bytes 811016 | tf_op jit(solution)/shard_map/ppermute | solution.py:29
  434.5 7.4 %collective-permute-start.16 = (f32[80,128]{1,0:T(8,128)S(1)}, f32[80,128]{1,0:T(8,128)S(1)}, u32[]{:S(2)}, u32[]{:S(2)}) collective-permute-start(f32[80,128]{1,0:T(8,128)S(1)} %bitcast.166), channel_id=1, source_target_pairs={{0,2},{2,0},{1,3},{3,1},{4,6},{6,4},{5,7},{7,5},{8,10},{10,8},{9,1... | collective-permute-start | bytes 122888 | tf_op jit(solution)/shard_map/ppermute | solution.py:24
  439.9 27.5 %collective-permute-start.19 = (bf16[33,32,128]{2,1,0:T(8,128)(2,1)}, bf16[33,32,128]{2,1,0:T(8,128)(2,1)}, u32[]{:S(2)}, u32[]{:S(2)}) collective-permute-start(bf16[33,32,128]{2,1,0:T(8,128)(2,1)} %get-tuple-element.128), channel_id=1, source_target_pairs={{0,16},{4,20},{8,24},{12,28},{16,0},{20,4},{24,8},{28,12},{1,17},{... | collective-permute-start | bytes 811016 | tf_op jit(solution)/shard_map/ppermute | solution.py:29
  440.2 43.0 %collective-permute-start.20 = (bf16[33,32,128]{2,1,0:T(8,128)(2,1)}, bf16[33,32,128]{2,1,0:T(8,128)(2,1)}, u32[]{:S(2)}, u32[]{:S(2)}) collective-permute-start(bf16[33,32,128]{2,1,0:T(8,128)(2,1)} %get-tuple-element.128), channel_id=1, source_target_pairs={{0,24},{4,28},{8,16},{12,20},{16,8},{20,12},{24,0},{28,4},{1,25},{... | collective-permute-start | bytes 811016 | tf_op jit(solution)/shard_map/ppermute | solution.py:29
  441.9 16.2 %collective-permute-start.17 = (f32[80,128]{1,0:T(8,128)S(1)}, f32[80,128]{1,0:T(8,128)}, u32[]{:S(2)}, u32[]{:S(2)}) collective-permute-start(f32[80,128]{1,0:T(8,128)S(1)} %add.569), channel_id=1, source_target_pairs={{0,1},{1,0},{2,3},{3,2},{4,5},{5,4},{6,7},{7,6},{8,9},{9,8},{10,11... | collective-permute-start | bytes 122888 | tf_op jit(solution)/shard_map/ppermute | solution.py:24
  459.6 45.0 %copy-start.25 = (f32[33,64,64]{2,1,0:T(8,128)S(1)}, f32[33,64,64]{2,1,0:T(8,128)}, u32[]{:S(2)}) copy-start(f32[33,64,64]{2,1,0:T(8,128)} %copy-done.24) | copy-start | bytes 1622020
  487.7 14.3 %collective-permute-start.24 = (bf16[64,32,128]{2,1,0:T(8,128)(2,1)}, bf16[64,32,128]{2,1,0:T(8,128)(2,1)S(1)}, u32[]{:S(2)}, u32[]{:S(2)}) collective-permute-start(bf16[64,32,128]{2,1,0:T(8,128)(2,1)} %get-tuple-element.110), channel_id=1, source_target_pairs={{0,4},{4,0},{8,12},{12,8},{16,20},{20,16},{24,28},{28,24},{1,5},{5... | collective-permute-start | bytes 1572872 | tf_op jit(solution)/shard_map/ppermute | solution.py:29
  488.2 4.1 collective-permute-start.21
  492.3 4.9 collective-permute-start.22
  497.2 10.8 %collective-permute-start.23 = (f32[80,128]{1,0:T(8,128)S(1)}, f32[80,128]{1,0:T(8,128)S(1)}, u32[]{:S(2)}, u32[]{:S(2)}) collective-permute-start(f32[80,128]{1,0:T(8,128)S(1)} %add.608), channel_id=1, source_target_pairs={{0,4},{4,0},{8,12},{12,8},{16,20},{20,16},{24,28},{28,24},{1,5},{5... | collective-permute-start | bytes 122888 | tf_op jit(solution)/shard_map/ppermute | solution.py:29
  503.3 12.4 %collective-permute-start.25 = (bf16[64,32,128]{2,1,0:T(8,128)(2,1)S(1)}, bf16[64,32,128]{2,1,0:T(8,128)(2,1)S(1)}, u32[]{:S(2)}, u32[]{:S(2)}) collective-permute-start(bf16[64,32,128]{2,1,0:T(8,128)(2,1)S(1)} %add.610.held), channel_id=1, source_target_pairs={{0,1},{1,0},{2,3},{3,2},{4,5},{5,4},{6,7},{7,6},{8,9},{9,8},{10,11... | collective-permute-start | bytes 1572872 | tf_op jit(solution)/shard_map/ppermute | solution.py:24
  (62 other events, 371.3 us)
Sparse Core Ops, SparseCore 0:
  10.7 49.3 all-gather.8
  62.8 70.9 all-gather.4
  215.9 105.1 reduce-scatter.1
  368.9 108.7 all-gather.6
